TPU v7x, 32 devices: a whole 2x2x4 slice. The times are simulated.
32 devices in a mesh: wide: 8 (over z, x), narrow: 4 (over y, core).
Axes of the slice: x: 2, y: 2, z: 4, core: 2. Of those that a mesh axis runs over, the one named last changes fastest.
Arguments:
- query_states: bfloat16 [2, 128, 32, 768], P(None, ('wide', 'narrow')), may hold values from -6 to 6
- passage_states: bfloat16 [2, 32, 512, 768], P(None, ('narrow', 'wide')), may hold values from -6 to 6
- lengths: int32 [2, 32], replicated, may hold values from 1 to 512, 8192 in all within a row
- positives: int32 [2, 128], replicated, may hold values from 0 to 31
- query_weight: bfloat16 [768, 768], replicated, may hold values from -0.21875 to 0.21875
- query_bias: bfloat16 [768], replicated, may hold values from -3 to 3
- key_weight: bfloat16 [768, 768], replicated, may hold values from -0.21875 to 0.21875
- value_weight: bfloat16 [768, 768], replicated, may hold values from -0.21875 to 0.21875
- value_bias: bfloat16 [768], replicated, may hold values from -3 to 3
- out_weight: bfloat16 [768, 768], replicated, may hold values from -0.875 to 0.875
- out_bias: bfloat16 [768], replicated, may hold values from -3 to 3
- first_gain: bfloat16 [768], replicated, may hold values from 0.099609375 to 1.8984375
- first_shift: bfloat16 [768], replicated, may hold values from -2 to 2
- inner_weight: bfloat16 [768, 3072], replicated, may hold values from -0.21875 to 0.21875
- inner_bias: bfloat16 [3072], replicated, may hold values from -3 to 3
- outer_weight: bfloat16 [3072, 768], replicated, may hold values from -0.109375 to 0.109375
- outer_bias: bfloat16 [768], replicated, may hold values from -3 to 3
- second_gain: bfloat16 [768], replicated, may hold values from 0.099609375 to 1.8984375
- second_shift: bfloat16 [768], replicated, may hold values from -2 to 2
- linear_weight: bfloat16 [768, 128], replicated, may hold values from -0.21875 to 0.21875
Outputs:
- scores: float32 [2, 128, 32], P(None, 'wide', 'narrow')
- losses: float32 [2, 128], P(None, 'wide')
- query_states_gradient: float32 [2, 128, 32, 768], P(None, ('wide', 'narrow'))
- passage_states_gradient: float32 [2, 32, 512, 768], P(None, ('narrow', 'wide'))
- query_weight_gradient: float32 [768, 768], P('wide')
- query_bias_gradient: float32 [768], P('wide')
- key_weight_gradient: float32 [768, 768], P('wide')
- value_weight_gradient: float32 [768, 768], P('wide')
- value_bias_gradient: float32 [768], P('wide')
- out_weight_gradient: float32 [768, 768], P('wide')
- out_bias_gradient: float32 [768], P('wide')
- first_gain_gradient: float32 [768], P('wide')
- first_shift_gradient: float32 [768], P('wide')
- inner_weight_gradient: float32 [768, 3072], P('wide')
- inner_bias_gradient: float32 [3072], P('wide')
- outer_weight_gradient: float32 [3072, 768], P('wide')
- outer_bias_gradient: float32 [768], P('wide')
- second_gain_gradient: float32 [768], P('wide')
- second_shift_gradient: float32 [768], P('wide')
- linear_weight_gradient: float32 [768, 128], P('wide')
Inputs may be any that keep to these rules, and one draw needn't show every extreme that they name: In each micro-batch the lengths sum to 8192, and the largest is 512.
All inputs are finite; a program needn't handle non-finite values.
Results may differ from a plain program's by a relative error of at most 0.02.
Values may be sent and summed in bfloat16 or wider, within the bound.
A program may use at most 320 MiB of HBM per device.

v0:
```python
import jax
import jax.numpy as jnp
from jax import lax
from jax.sharding import PartitionSpec as P

HEADS = 12


SHARP = 16.0
LAYER_EPS = 1e-12
NORM_EPS = 1e-06
MASKED = -1e30
SLOPE_CONST = 0.3989422804014327
ROOT_HALF = 0.7071067811865476


def product(left_side, right_side):
    return jnp.dot(left_side, right_side, preferred_element_type=jnp.float32)


def product_back(grad_low, weight_in):
    return jnp.einsum("ble,de->bld", grad_low, weight_in, preferred_element_type=jnp.float32)


def outer_sum(left_low, grad_low):
    return jnp.einsum("bld,ble->de", left_low, grad_low, preferred_element_type=jnp.float32)


def column_sum(grad_low):
    return jnp.sum(grad_low, axis=(0, 1), dtype=jnp.float32)


def norm_forward(field, norm_gain, norm_shift):
    center = field - jnp.mean(field, axis=-1, keepdims=True)
    inverse = lax.rsqrt(jnp.mean(center * center, axis=-1, keepdims=True) + LAYER_EPS)
    normed = center * inverse
    return (normed * norm_gain + norm_shift, normed, inverse)


def norm_backward(grad_out, normed, inverse, norm_gain):
    grad_normed = grad_out * norm_gain
    mean_grad = jnp.mean(grad_normed, axis=-1, keepdims=True)
    mean_cross = jnp.mean(grad_normed * normed, axis=-1, keepdims=True)
    return inverse * (grad_normed - mean_grad - normed * mean_cross)


def encode_forward(states, valid_keys, weights):
    (
        query_weight,
        query_bias,
        key_weight,
        value_weight,
        value_bias,
        out_weight,
        out_bias,
        first_gain,
        first_shift,
        inner_weight,
        inner_bias,
        outer_weight,
        outer_bias,
        second_gain,
        second_shift,
        linear_weight,
    ) = weights
    sequences, length, model_width = states.shape
    head_dim = model_width // HEADS
    score_scale = head_dim ** (-0.5)
    head_shape = (sequences, length, HEADS, head_dim)
    queries = (
        (product(states, query_weight) + query_bias.astype(jnp.float32))
        .astype(jnp.bfloat16)
        .reshape(head_shape)
    )
    key_rows = product(states, key_weight).astype(jnp.bfloat16).reshape(head_shape)
    value_rows = (
        (product(states, value_weight) + value_bias.astype(jnp.float32))
        .astype(jnp.bfloat16)
        .reshape(head_shape)
    )
    logits = (
        jnp.einsum("blhd,bmhd->bhlm", queries, key_rows, preferred_element_type=jnp.float32)
        * score_scale
    )
    logits = jnp.where(valid_keys[:, None, None, :], logits, MASKED)
    attention = jax.nn.softmax(logits, axis=-1)
    context = jnp.einsum(
        "bhlm,bmhd->blhd",
        attention.astype(jnp.bfloat16),
        value_rows,
        preferred_element_type=jnp.float32,
    )
    context = context.reshape(sequences, length, model_width).astype(jnp.bfloat16)
    attended = product(context, out_weight) + out_bias.astype(jnp.float32)
    first_norm, first_normed, first_inverse = norm_forward(
        states.astype(jnp.float32) + attended,
        first_gain.astype(jnp.float32),
        first_shift.astype(jnp.float32),
    )
    first_low = first_norm.astype(jnp.bfloat16)
    inner_pre = product(first_low, inner_weight) + inner_bias.astype(jnp.float32)
    activated = jax.nn.gelu(inner_pre, approximate=False).astype(jnp.bfloat16)
    outer_out = product(activated, outer_weight) + outer_bias.astype(jnp.float32)
    final_norm, final_normed, final_inverse = norm_forward(
        first_norm + outer_out, second_gain.astype(jnp.float32), second_shift.astype(jnp.float32)
    )
    final_low = final_norm.astype(jnp.bfloat16)
    projected = product(final_low, linear_weight)
    unit_inverse = lax.rsqrt(jnp.sum(projected * projected, axis=-1, keepdims=True) + NORM_EPS)
    unit_rows = projected * unit_inverse
    kept = (
        states,
        queries,
        key_rows,
        value_rows,
        attention,
        context,
        first_normed,
        first_inverse,
        first_low,
        inner_pre,
        activated,
        final_normed,
        final_inverse,
        final_low,
        unit_rows,
        unit_inverse,
    )
    return (unit_rows.astype(jnp.bfloat16), kept)


def encode_backward(kept, grad_embed, weights):
    (
        query_weight,
        query_bias,
        key_weight,
        value_weight,
        value_bias,
        out_weight,
        out_bias,
        first_gain,
        first_shift,
        inner_weight,
        inner_bias,
        outer_weight,
        outer_bias,
        second_gain,
        second_shift,
        linear_weight,
    ) = weights
    (
        states,
        queries,
        key_rows,
        value_rows,
        attention,
        context,
        first_normed,
        first_inverse,
        first_low,
        inner_pre,
        activated,
        final_normed,
        final_inverse,
        final_low,
        unit_rows,
        unit_inverse,
    ) = kept
    sequences, length, heads_count, head_dim = queries.shape
    model_width = heads_count * head_dim
    score_scale = head_dim ** (-0.5)
    grad_projected = unit_inverse * (
        grad_embed - unit_rows * jnp.sum(grad_embed * unit_rows, axis=-1, keepdims=True)
    )
    projected_low = grad_projected.astype(jnp.bfloat16)
    linear_grad = outer_sum(final_low, projected_low)
    grad_final = product_back(projected_low, linear_weight)
    second_gain_grad = jnp.sum(grad_final * final_normed, axis=(0, 1))
    second_shift_grad = jnp.sum(grad_final, axis=(0, 1))
    grad_second = norm_backward(
        grad_final, final_normed, final_inverse, second_gain.astype(jnp.float32)
    )
    outer_low = grad_second.astype(jnp.bfloat16)
    outer_weight_grad = outer_sum(activated, outer_low)
    outer_bias_grad = column_sum(outer_low)
    grad_activated = product_back(outer_low, outer_weight)
    slope = (
        0.5 * (1.0 + lax.erf(inner_pre * ROOT_HALF))
        + inner_pre * jnp.exp(-0.5 * inner_pre * inner_pre) * SLOPE_CONST
    )
    inner_low = (grad_activated * slope).astype(jnp.bfloat16)
    inner_weight_grad = outer_sum(first_low, inner_low)
    inner_bias_grad = column_sum(inner_low)
    grad_first = grad_second + product_back(inner_low, inner_weight)
    first_gain_grad = jnp.sum(grad_first * first_normed, axis=(0, 1))
    first_shift_grad = jnp.sum(grad_first, axis=(0, 1))
    grad_hidden = norm_backward(
        grad_first, first_normed, first_inverse, first_gain.astype(jnp.float32)
    )
    attended_low = grad_hidden.astype(jnp.bfloat16)
    out_weight_grad = outer_sum(context, attended_low)
    out_bias_grad = column_sum(attended_low)
    context_low = product_back(attended_low, out_weight).astype(jnp.bfloat16).reshape(queries.shape)
    grad_attention = jnp.einsum(
        "blhd,bmhd->bhlm", context_low, value_rows, preferred_element_type=jnp.float32
    )
    value_low = jnp.einsum(
        "bhlm,blhd->bmhd",
        attention.astype(jnp.bfloat16),
        context_low,
        preferred_element_type=jnp.float32,
    )
    value_low = value_low.astype(jnp.bfloat16).reshape(sequences, length, model_width)
    grad_logits = attention * (
        grad_attention - jnp.sum(grad_attention * attention, axis=-1, keepdims=True)
    )
    logits_low = grad_logits.astype(jnp.bfloat16)
    query_low = (
        jnp.einsum("bhlm,bmhd->blhd", logits_low, key_rows, preferred_element_type=jnp.float32)
        * score_scale
    )
    query_low = query_low.astype(jnp.bfloat16).reshape(sequences, length, model_width)
    key_low = (
        jnp.einsum("bhlm,blhd->bmhd", logits_low, queries, preferred_element_type=jnp.float32)
        * score_scale
    )
    key_low = key_low.astype(jnp.bfloat16).reshape(sequences, length, model_width)
    query_weight_grad = outer_sum(states, query_low)
    query_bias_grad = column_sum(query_low)
    key_weight_grad = outer_sum(states, key_low)
    value_weight_grad = outer_sum(states, value_low)
    value_bias_grad = column_sum(value_low)
    grad_states = (
        grad_hidden
        + product_back(query_low, query_weight)
        + product_back(key_low, key_weight)
        + product_back(value_low, value_weight)
    )
    grads = (
        query_weight_grad,
        query_bias_grad,
        key_weight_grad,
        value_weight_grad,
        value_bias_grad,
        out_weight_grad,
        out_bias_grad,
        first_gain_grad,
        first_shift_grad,
        inner_weight_grad,
        inner_bias_grad,
        outer_weight_grad,
        outer_bias_grad,
        second_gain_grad,
        second_shift_grad,
        linear_grad,
    )
    return (grad_states, grads)


def block_size(count, row_count):
    size_now = max(1, min(8, count, 4096 // row_count))
    while count % size_now:
        size_now = size_now - 1
    return size_now


def sharpened_sims(query_flat, block_embed, block_lengths):
    slot_positions = jnp.arange(block_embed.shape[1], dtype=jnp.int32)
    sims = (
        jnp.einsum("rk,pjk->rpj", query_flat, block_embed, preferred_element_type=jnp.float32)
        * SHARP
    )
    return jnp.where((slot_positions[None, :] < block_lengths[:, None])[None], sims, MASKED)


def token_scores(query_flat, embeds, column_lengths):
    count, slot_count, embed_width = embeds.shape
    row_count = query_flat.shape[0]
    size_now = block_size(count, row_count)

    def one_block(item):
        block_embed, block_lengths = item
        return jax.nn.logsumexp(sharpened_sims(query_flat, block_embed, block_lengths), axis=2)

    blocks = lax.map(
        one_block,
        (
            embeds.reshape(count // size_now, size_now, slot_count, embed_width),
            column_lengths.reshape(count // size_now, size_now),
        ),
    )
    return jnp.transpose(blocks, (1, 0, 2)).reshape(row_count, count)


def token_grads(query_flat, embeds, column_lengths, token_lse, row_grads):
    count, slot_count, embed_width = embeds.shape
    row_count = query_flat.shape[0]
    size_now = block_size(count, row_count)
    block_total = count // size_now

    def one_block(carry, item):
        block_embed, block_lengths, block_lse, block_grad = item
        sims = sharpened_sims(query_flat, block_embed, block_lengths)
        weighted = (jnp.exp(sims - block_lse[:, :, None]) * block_grad[:, :, None]).astype(
            jnp.bfloat16
        )
        carry = carry + jnp.einsum(
            "rpj,pjk->rk", weighted, block_embed, preferred_element_type=jnp.float32
        )
        return (
            carry,
            jnp.einsum("rpj,rk->pjk", weighted, query_flat, preferred_element_type=jnp.float32),
        )

    split_lse = jnp.transpose(token_lse.reshape(row_count, block_total, size_now), (1, 0, 2))
    split_grad = jnp.transpose(row_grads.reshape(row_count, block_total, size_now), (1, 0, 2))
    query_part, passage_part = lax.scan(
        one_block,
        jnp.zeros((row_count, embed_width), jnp.float32),
        (
            embeds.reshape(block_total, size_now, slot_count, embed_width),
            column_lengths.reshape(block_total, size_now),
            split_lse,
            split_grad,
        ),
    )
    return (query_part, passage_part.reshape(count, slot_count, embed_width))


def add_trees(left_tree, right_tree):
    return jax.tree.map(lambda left_part, right_part: left_part + right_part, left_tree, right_tree)


def score_backward_rows(block_scores, row_total, target_hit, query_len):
    row_count, column_count = block_scores.shape
    score_grads = jnp.exp(block_scores - row_total[:, None]) - target_hit.astype(jnp.float32)
    return jnp.broadcast_to(score_grads[:, None, :], (row_count, query_len, column_count)).reshape(
        -1, column_count
    )


def grid_line(
    query_embed,
    passage_embed,
    lengths_now,
    positives_now,
    wide_index,
    narrow_index,
    n_wide,
    n_narrow,
):
    query_dev, query_len, embed_width = query_embed.shape
    passage_dev = passage_embed.shape[0]
    column_count = passage_dev * n_wide
    row_count = query_dev * n_narrow
    column_lengths = lax.dynamic_slice_in_dim(
        lengths_now, narrow_index * column_count, column_count
    )
    row_positives = lax.dynamic_slice_in_dim(positives_now, wide_index * row_count, row_count)
    column_ids = jnp.arange(column_count, dtype=jnp.int32)
    query_rows = lax.all_gather(query_embed, "narrow", axis=0, tiled=True)
    query_flat = query_rows.reshape(-1, embed_width)
    passage_column = lax.all_gather(passage_embed, "wide", axis=0, tiled=True)
    token_lse = token_scores(query_flat, passage_column, column_lengths)
    block_scores = jnp.sum(token_lse.reshape(row_count, query_len, column_count), axis=1) / SHARP
    targets = row_positives - narrow_index * column_count
    target_hit = column_ids[None, :] == targets[:, None]
    full_scores = lax.all_gather(block_scores, "narrow", axis=1, tiled=True)
    row_total = jax.nn.logsumexp(full_scores, axis=1)
    all_ids = jnp.arange(full_scores.shape[1], dtype=jnp.int32)
    picked = jnp.sum(
        jnp.where(all_ids[None, :] == row_positives[:, None], full_scores, 0.0), axis=1
    )
    row_grads = score_backward_rows(block_scores, row_total, target_hit, query_len)
    query_part, passage_part = token_grads(
        query_flat, passage_column, column_lengths, token_lse, row_grads
    )
    query_embed_grad = lax.psum_scatter(
        query_part.astype(jnp.bfloat16), "narrow", scatter_dimension=0, tiled=True
    ).astype(jnp.float32)
    passage_embed_grad = lax.psum_scatter(passage_part, "wide", scatter_dimension=0, tiled=True)
    return (
        block_scores,
        row_total - picked,
        query_embed_grad.reshape(query_embed.shape),
        passage_embed_grad,
    )


def local(
    query_states,
    passage_states,
    lengths,
    positives,
    query_weight,
    query_bias,
    key_weight,
    value_weight,
    value_bias,
    out_weight,
    out_bias,
    first_gain,
    first_shift,
    inner_weight,
    inner_bias,
    outer_weight,
    outer_bias,
    second_gain,
    second_shift,
    linear_weight,
):
    weights = (
        query_weight,
        query_bias,
        key_weight,
        value_weight,
        value_bias,
        out_weight,
        out_bias,
        first_gain,
        first_shift,
        inner_weight,
        inner_bias,
        outer_weight,
        outer_bias,
        second_gain,
        second_shift,
        linear_weight,
    )
    wide_index = lax.axis_index("wide")
    narrow_index = lax.axis_index("narrow")
    n_wide = lax.axis_size("wide")
    n_narrow = lax.axis_size("narrow")
    own_passages = passage_states.shape[1]
    query_count = query_states.shape[1]
    query_len = query_states.shape[2]
    slot_count = passage_states.shape[2]
    slot_positions = jnp.arange(slot_count, dtype=jnp.int32)
    query_valid = jnp.broadcast_to(
        jnp.arange(query_len, dtype=jnp.int32)[None, :] >= 0, (query_count, query_len)
    )
    totals = None
    score_list = []
    loss_list = []
    query_grad_list = []
    passage_grad_list = []
    for micro_step in range(query_states.shape[0]):
        lengths_now = lengths[micro_step]
        positives_now = positives[micro_step]
        own_lengths = lax.dynamic_slice_in_dim(
            lengths_now, (narrow_index * n_wide + wide_index) * own_passages, own_passages
        )
        passage_valid = slot_positions[None, :] < own_lengths[:, None]
        query_embed, query_kept = encode_forward(query_states[micro_step], query_valid, weights)
        passage_embed, passage_kept = encode_forward(
            passage_states[micro_step], passage_valid, weights
        )
        scores_now, losses_now, query_embed_grad, passage_embed_grad = grid_line(
            query_embed,
            passage_embed,
            lengths_now,
            positives_now,
            wide_index,
            narrow_index,
            n_wide,
            n_narrow,
        )
        query_input_grad, query_weight_grads = encode_backward(
            query_kept, query_embed_grad, weights
        )
        passage_input_grad, passage_weight_grads = encode_backward(
            passage_kept, passage_embed_grad, weights
        )
        step_grads = add_trees(query_weight_grads, passage_weight_grads)
        totals = step_grads if totals is None else add_trees(totals, step_grads)
        score_list.append(scores_now)
        loss_list.append(losses_now)
        query_grad_list.append(query_input_grad)
        passage_grad_list.append(passage_input_grad)
    (
        grad_query_weight,
        grad_query_bias,
        grad_key_weight,
        grad_value_weight,
        grad_value_bias,
        grad_out_weight,
        grad_out_bias,
        grad_first_gain,
        grad_first_shift,
        grad_inner_weight,
        grad_inner_bias,
        grad_outer_weight,
        grad_outer_bias,
        grad_second_gain,
        grad_second_shift,
        grad_linear_weight,
    ) = totals
    (
        wide_query_weight,
        wide_query_bias,
        wide_key_weight,
        wide_value_weight,
        wide_value_bias,
        wide_out_weight,
        wide_out_bias,
        wide_first_gain,
        wide_first_shift,
        wide_inner_weight,
        wide_inner_bias,
        wide_outer_weight,
        wide_outer_bias,
        wide_second_gain,
        wide_second_shift,
        wide_linear_weight,
    ) = (
        lax.psum_scatter(grad_query_weight, "wide", scatter_dimension=0, tiled=True),
        lax.psum_scatter(grad_query_bias, "wide", scatter_dimension=0, tiled=True),
        lax.psum_scatter(grad_key_weight, "wide", scatter_dimension=0, tiled=True),
        lax.psum_scatter(grad_value_weight, "wide", scatter_dimension=0, tiled=True),
        lax.psum_scatter(grad_value_bias, "wide", scatter_dimension=0, tiled=True),
        lax.psum_scatter(grad_out_weight, "wide", scatter_dimension=0, tiled=True),
        lax.psum_scatter(grad_out_bias, "wide", scatter_dimension=0, tiled=True),
        lax.psum_scatter(grad_first_gain, "wide", scatter_dimension=0, tiled=True),
        lax.psum_scatter(grad_first_shift, "wide", scatter_dimension=0, tiled=True),
        lax.psum_scatter(grad_inner_weight, "wide", scatter_dimension=0, tiled=True),
        lax.psum_scatter(grad_inner_bias, "wide", scatter_dimension=0, tiled=True),
        lax.psum_scatter(grad_outer_weight, "wide", scatter_dimension=0, tiled=True),
        lax.psum_scatter(grad_outer_bias, "wide", scatter_dimension=0, tiled=True),
        lax.psum_scatter(grad_second_gain, "wide", scatter_dimension=0, tiled=True),
        lax.psum_scatter(grad_second_shift, "wide", scatter_dimension=0, tiled=True),
        lax.psum_scatter(grad_linear_weight, "wide", scatter_dimension=0, tiled=True),
    )
    reduced = (
        lax.psum(wide_query_weight.astype(jnp.bfloat16), "narrow").astype(jnp.float32),
        lax.psum(wide_query_bias.astype(jnp.bfloat16), "narrow").astype(jnp.float32),
        lax.psum(wide_key_weight.astype(jnp.bfloat16), "narrow").astype(jnp.float32),
        lax.psum(wide_value_weight.astype(jnp.bfloat16), "narrow").astype(jnp.float32),
        lax.psum(wide_value_bias.astype(jnp.bfloat16), "narrow").astype(jnp.float32),
        lax.psum(wide_out_weight.astype(jnp.bfloat16), "narrow").astype(jnp.float32),
        lax.psum(wide_out_bias.astype(jnp.bfloat16), "narrow").astype(jnp.float32),
        lax.psum(wide_first_gain.astype(jnp.bfloat16), "narrow").astype(jnp.float32),
        lax.psum(wide_first_shift.astype(jnp.bfloat16), "narrow").astype(jnp.float32),
        lax.psum(wide_inner_weight.astype(jnp.bfloat16), "narrow").astype(jnp.float32),
        lax.psum(wide_inner_bias.astype(jnp.bfloat16), "narrow").astype(jnp.float32),
        lax.psum(wide_outer_weight.astype(jnp.bfloat16), "narrow").astype(jnp.float32),
        lax.psum(wide_outer_bias.astype(jnp.bfloat16), "narrow").astype(jnp.float32),
        lax.psum(wide_second_gain.astype(jnp.bfloat16), "narrow").astype(jnp.float32),
        lax.psum(wide_second_shift.astype(jnp.bfloat16), "narrow").astype(jnp.float32),
        lax.psum(wide_linear_weight.astype(jnp.bfloat16), "narrow").astype(jnp.float32),
    )
    return (
        jnp.stack(score_list),
        jnp.stack(loss_list),
        jnp.stack(query_grad_list),
        jnp.stack(passage_grad_list),
        reduced[0],
        reduced[1],
        reduced[2],
        reduced[3],
        reduced[4],
        reduced[5],
        reduced[6],
        reduced[7],
        reduced[8],
        reduced[9],
        reduced[10],
        reduced[11],
        reduced[12],
        reduced[13],
        reduced[14],
        reduced[15],
    )


def solution(mesh):
    return jax.shard_map(
        local,
        mesh=mesh,
        in_specs=(
            P(None, ("wide", "narrow"), None, None),
            P(None, ("narrow", "wide"), None, None),
            P(),
            P(),
            P(),
            P(),
            P(),
            P(),
            P(),
            P(),
            P(),
            P(),
            P(),
            P(),
            P(),
            P(),
            P(),
            P(),
            P(),
            P(),
        ),
        out_specs=(
            P(None, "wide", "narrow"),
            P(None, "wide"),
            P(None, ("wide", "narrow"), None, None),
            P(None, ("narrow", "wide"), None, None),
            P("wide", None),
            P("wide"),
            P("wide", None),
            P("wide", None),
            P("wide"),
            P("wide", None),
            P("wide"),
            P("wide"),
            P("wide"),
            P("wide", None),
            P("wide"),
            P("wide", None),
            P("wide"),
            P("wide"),
            P("wide"),
            P("wide", None),
        ),
        check_vma=False,
    )
```

profile of v0, /device:TPU:0, one launch (start us, length us, event | category | flops | bytes accessed | tf_op | source)
XLA Modules:
  0.0 1233.4 jit_solution(5177678585884068793)
XLA Ops:
  8.0 3.3 add_convert_fusion.1
  28.0 10.9 fusion.496
  38.9 6.1 fusion.133
  55.3 10.9 fusion.494
  66.3 6.2 fusion.127
  78.2 31.8 %fusion.14 = (bf16[512,3072]{1,0:T(8,128)(2,1)S(1)}, bf16[512,3072]{1,0:T(8,128)(2,1)S(1)}, f32[512,3072]{1,0:T(8,128)}) fusion(f32[3072]{0:T(1024)S(1)} %convert_element_type.646, f32[512,3072]{1,0:T(8,128)S(1)} %fusion.471, bf16[768,3072]{1,0:T(8,128)(2,1)S(1)} %bitcast.548, f32[512,768]{1,0:T(8,128)S(1)} %get-tuple-element.287, ...), kind=kOutput, calls=%fused_computation.36 | convolution fusion | flops 2625503232 | bytes 25188352 | tf_op jit(solution)/shard_map/dot_general | solution.py:18
  143.8 3.9 fusion.255
  148.9 3.5 fusion.101
  152.5 3.6 fusion.506
  157.0 7.5 all_gather.18
  166.8 4.3 fusion.493
  172.5 6.0 all_gather.20
  185.5 5.7 fusion.10
  194.0 8.9 all-gather.7.cloned.1.call-done
  205.1 5.1 fusion.11
  212.8 4.5 exponential_reduce_fusion.1
  220.9 5.6 all_gather.22
  233.9 5.8 fusion.226
  239.8 4.5 exponential_reduce_fusion
  248.0 5.6 all_gather.23
  260.9 5.9 fusion.227
  266.9 6.0 fusion.435
  272.9 6.0 fusion.436
  285.7 3.2 convert_reduce_fusion.17
  292.1 5.3 convert_reduce_fusion.4
  297.4 5.0 convert_reduce_fusion.5
  305.1 3.1 convert_reduce_fusion.19
  311.4 3.2 convert_reduce_fusion.12
  315.6 3.0 convert_reduce_fusion.13
  343.0 15.2 %reduce-scatter.22.cloned.1.call-done = f32[1,512,128]{1,2,0:T(8,128)} async-done(((f32[8,512,128]{1,2,0:T(8,128)}), f32[1,512,128]{1,2,0:T(8,128)}) %reduce-scatter.22.cloned.1.call-update) | async-done | bytes 262160 | tf_op jit(solution)/shard_map/reduce_scatter | solution.py:381
  360.3 3.9 multiply_reduce_fusion.3
  364.3 64.9 %reduce-scatter.24.cloned.1.call-done = f32[1,512,128]{1,2,0:T(8,128)} async-done(((f32[8,512,128]{1,2,0:T(8,128)}), f32[1,512,128]{1,2,0:T(8,128)}) %reduce-scatter.24.cloned.1.call-update) | async-done | bytes 262160 | tf_op jit(solution)/shard_map/reduce_scatter | solution.py:381
  431.2 3.5 convert_reduce_fusion.3
  435.9 9.1 convert_reduce_fusion
  445.1 5.4 convert_reduce_fusion.1
  450.5 3.6 multiply_reduce_fusion.5
  454.2 5.4 convert_reduce_fusion.7
  465.0 7.6 convert_reduce_fusion.9
  477.7 8.4 convert_reduce_fusion.8
  491.7 3.9 fusion.94
  495.6 3.1 copy.225
  498.7 6.8 multiply_reduce_fusion.1
  505.5 7.0 multiply_convert_fusion.1
  518.3 12.1 multiply_reduce_fusion
  530.4 6.9 multiply_convert_fusion
  544.8 3.1 copy.223
  559.3 4.8 convert_reduce_fusion.11
  570.4 3.1 copy.221
  574.6 6.2 fusion.525
  583.6 5.1 fusion.407
  588.7 11.9 fusion.8
  604.5 5.6 fusion.473
  610.2 5.6 fusion.469
  615.8 12.5 %fusion.9 = f32[768,3072]{1,0:T(8,128)} fusion(f32[768,3072]{1,0:T(8,128)} %fusion.469, f32[768,3072]{1,0:T(8,128)} %fusion.473, f32[768,3072,1]{1,0,2:T(8,128)S(1)} %fusion.430, bf16[4,32,3072]{2,1,0:T(8,128)(2,1)S(1)} %copy-done.69, f32[4,32,768]{2,1,0:T(8,128)S(1)} %copy-done.17, f32[4,32]{1,0:T(4,128)S(1)} %copy-done.182, f32[4,32]{1,0:T(4,128)S(1)} %copy-done.166, ...), kind=kOutput, calls=%fused_computation.24 | convolution fusion | flops 611549184 | bytes 38935552 | tf_op jit(solution)/shard_map/bld,ble->de/dot_general | solution.py:26
  647.4 3.3 fusion.519
  666.2 36.9 %all-reduce.9 = (bf16[768]{0:T(1024)(128)(2,1)}, bf16[768]{0:T(1024)(128)(2,1)}, bf16[768]{0:T(1024)(128)(2,1)}, bf16[768]{0:T(1024)(128)(2,1)}, bf16[768]{0:T(1...) all-reduce(f32[768]{0:T(1024)} %add.838, ...), channel_id=9, replica_groups=mesh['wide'=8,'narrow'=4] {'wide'}, use_global_device_ids=true, to_apply=%region_74.75.clone | all-reduce | flops 9216 | bytes 55296
  712.3 3.3 fusion.521
  715.5 3.9 add_bitcast_fusion.1
  724.7 49.6 %reduce-scatter.34.cloned.1.call-done = f32[96,768]{1,0:T(8,128)} async-done(((f32[768,768]{1,0:T(8,128)}), f32[96,768]{1,0:T(8,128)}) %reduce-scatter.34.cloned.1.call-update) | async-done | bytes 294928
  776.0 163.1 %reduce-scatter.30.cloned.1.call-done = f32[384,768]{1,0:T(8,128)} async-done(((f32[3072,768]{1,0:T(8,128)}), f32[384,768]{1,0:T(8,128)}) %reduce-scatter.30.cloned.1.call-update) | async-done | bytes 1179664 | tf_op jit(solution)/shard_map/reduce_scatter | solution.py:527
  941.3 162.5 %reduce-scatter.28.cloned.1.call-done = f32[96,3072]{1,0:T(8,128)} async-done(((f32[768,3072]{1,0:T(8,128)}), f32[96,3072]{1,0:T(8,128)}) %reduce-scatter.28.cloned.1.call-update) | async-done | bytes 1179664 | tf_op jit(solution)/shard_map/reduce_scatter | solution.py:525
  1112.5 55.9 %reduce-scatter.32.cloned.1.call-done = f32[96,128]{1,0:T(8,128)} async-done(((f32[768,128]{1,0:T(8,128)}), f32[96,128]{1,0:T(8,128)}) %reduce-scatter.32.cloned.1.call-update) | async-done | bytes 49168 | tf_op jit(solution)/shard_map/reduce_scatter | solution.py:531
  1169.3 10.3 all-reduce.10
  1184.9 35.1 %all-reduce.14.cloned.1.call-done = (bf16[96,768]{0,1:T(8,128)(2,1)}, bf16[96,768]{0,1:T(8,128)(2,1)}, bf16[96,768]{0,1:T(8,128)(2,1)}, bf16[96,768]{1,0:T(8,128...) async-done(((bf16[96,768]{0,1:T(8,128)(2,1)}, bf16[96,768]{0,1:T(8,128)(2,1)}, bf16[96,768]{0,1:T(8,128)(2,1)}, bf16[96,768]{1,0:T(8,128)(2,1)}, ...) | async-done | bytes 1769488 | tf_op jit(solution)/shard_map/psum | solution.py:534
  (912 shorter events, 281.8 us)
Async XLA Ops:
  7.2 37.8 %copy-start = (bf16[768,768]{1,0:T(8,128)(2,1)S(1)}, bf16[768,768]{1,0:T(8,128)(2,1)}, u32[]{:S(2)}) copy-start(bf16[768,768]{1,0:T(8,128)(2,1)} %param.29) | copy-start | bytes 3538948
  7.2 176.0 %all-gather.5.cloned.1.call-start = ((), (), s32[]{:S(2)}) async-start(), calls=%async_computation.19 | async-start | bytes 1179648 | tf_op jit(solution)/shard_map/all_gather | solution.py:363
  28.0 44.4 %copy-start.193 = (f32[768]{0:T(1024)}, f32[768]{0:T(1024)S(1)}, u32[]{:S(2)}) copy-start(f32[768]{0:T(1024)S(1)} %convert_element_type.642) | copy-start | bytes 9220
  46.0 64.0 %copy-start.211 = (f32[512]{0:T(512)}, f32[512]{0:T(512)S(1)}, u32[]{:S(2)}) copy-start(f32[512]{0:T(512)S(1)} %broadcast_multiply_fusion.11) | copy-start | bytes 6148
  47.4 62.5 %copy-start.236 = (f32[512]{0:T(512)}, f32[512]{0:T(512)S(1)}, u32[]{:S(2)}) copy-start(f32[512]{0:T(512)S(1)} %add_rsqrt_fusion.2) | copy-start | bytes 6148
  47.5 104.9 %copy-start.186 = (f32[768]{0:T(1024)}, f32[768]{0:T(1024)S(1)}, u32[]{:S(2)}) copy-start(f32[768]{0:T(1024)S(1)} %convert_element_type.644) | copy-start | bytes 9220
  55.3 18.9 %slice-start.2 = ((s8[4718592]{0:T(1024)(128)(4,1)}), s8[524288]{0:T(1024)(128)(4,1)S(1)}, s32[]{:S(2)}) async-start(s8[4718592]{0:T(1024)(128)(4,1)} %bitcast.547), calls=%async_computation.27 | async-start | bytes 1048576
  73.4 39.7 %copy-start.89 = (f32[512,768]{1,0:T(8,128)}, f32[512,768]{1,0:T(8,128)S(1)}, u32[]{:S(2)}) copy-start(f32[512,768]{1,0:T(8,128)S(1)} %get-tuple-element.287) | copy-start | bytes 4718596
  73.5 39.6 %copy-start.239 = (f32[512]{0:T(512)}, f32[512]{0:T(512)S(1)}, u32[]{:S(2)}) copy-start(f32[512]{0:T(512)S(1)} %broadcast_multiply_fusion.13) | copy-start | bytes 6148
  74.1 39.0 %copy-start.252 = (f32[512]{0:T(512)}, f32[512]{0:T(512)S(1)}, u32[]{:S(2)}) copy-start(f32[512]{0:T(512)S(1)} %add_rsqrt_fusion.8) | copy-start | bytes 6148
  75.4 37.7 %copy-start.229 = (f32[768]{0:T(1024)}, f32[768]{0:T(1024)S(1)}, u32[]{:S(2)}) copy-start(f32[768]{0:T(1024)S(1)} %convert_element_type.648) | copy-start | bytes 9220
  75.4 34.5 %slice-start.13 = ((s8[4718592]{0:T(1024)(128)(4,1)}), s8[4194304]{0:T(1024)(128)(4,1)S(1)}, s32[]{:S(2)}) async-start(s8[4718592]{0:T(1024)(128)(4,1)} %bitcast.557), calls=%async_computation.38 | async-start | bytes 8388608
  78.1 31.8 %copy-start.272 = (f32[512,3072]{1,0:T(8,128)}, f32[512,3072]{1,0:T(8,128)S(1)}, u32[]{:S(2)}) copy-start(f32[512,3072]{1,0:T(8,128)S(1)} %fusion.471) | copy-start | bytes 18874372
  78.1 31.8 %slice-start.14 = ((s8[4718592]{0:T(1024)(128)(4,1)}), s8[524288]{0:T(1024)(128)(4,1)S(1)}, s32[]{:S(2)}) async-start(s8[4718592]{0:T(1024)(128)(4,1)} %bitcast.557), calls=%async_computation.39 | async-start | bytes 1048576
  116.7 318.1 %copy-start.137 = (f32[768]{0:T(1024)}, f32[768]{0:T(1024)S(1)}, u32[]{:S(2)}) copy-start(f32[768]{0:T(1024)S(1)} %convert_element_type.649) | copy-start | bytes 9220
  120.1 82.8 %all-gather.7.cloned.1.call-start = ((), (), s32[]{:S(2)}) async-start(), calls=%async_computation.20 | async-start | bytes 1179648 | tf_op jit(solution)/shard_map/all_gather | solution.py:363
  121.9 157.3 %reduce-scatter.18.cloned.1.call-start = ((), (), s32[]{:S(2)}) async-start(), calls=%async_computation.11 | async-start | bytes 163840 | tf_op jit(solution)/shard_map/reduce_scatter | solution.py:378
  135.6 169.3 %copy-start.19 = (f32[4,32,768]{2,1,0:T(8,128)}, f32[4,32,768]{2,1,0:T(8,128)S(1)}, u32[]{:S(2)}) copy-start(f32[4,32,768]{2,1,0:T(8,128)S(1)} %get-tuple-element.304) | copy-start | bytes 1179652
  135.7 169.3 %copy-start.153 = (f32[4,32]{1,0:T(4,128)}, f32[4,32]{1,0:T(4,128)S(1)}, u32[]{:S(2)}) copy-start(f32[4,32]{1,0:T(4,128)S(1)} %broadcast_multiply_fusion.25) | copy-start | bytes 1540
  143.4 164.8 %copy-start.16 = (f32[4,32,768]{2,1,0:T(8,128)}, f32[4,32,768]{2,1,0:T(8,128)S(1)}, u32[]{:S(2)}) copy-start(f32[4,32,768]{2,1,0:T(8,128)S(1)} %get-tuple-element.278) | copy-start | bytes 1179652
  143.4 23.4 %copy-start.164 = (f32[4,32]{1,0:T(4,128)}, f32[4,32]{1,0:T(4,128)S(1)}, u32[]{:S(2)}) copy-start(f32[4,32]{1,0:T(4,128)S(1)} %broadcast_multiply_fusion.23) | copy-start | bytes 1540
  143.8 23.0 %copy-start.180 = (f32[4,32]{1,0:T(4,128)}, f32[4,32]{1,0:T(4,128)S(1)}, u32[]{:S(2)}) copy-start(f32[4,32]{1,0:T(4,128)S(1)} %get-tuple-element.356) | copy-start | bytes 1540
  143.8 20.7 %slice-start.4 = ((s8[4718592]{0:T(1024)(128)(4,1)}), s8[4194304]{0:T(1024)(128)(4,1)S(1)}, s32[]{:S(2)}) async-start(s8[4718592]{0:T(1024)(128)(4,1)} %bitcast.549), calls=%async_computation.29 | async-start | bytes 8388608
  148.9 15.7 %slice-start.5 = ((s8[4718592]{0:T(1024)(128)(4,1)}), s8[524288]{0:T(1024)(128)(4,1)S(1)}, s32[]{:S(2)}) async-start(s8[4718592]{0:T(1024)(128)(4,1)} %bitcast.549), calls=%async_computation.30 | async-start | bytes 1048576
  152.5 14.3 %slice-start.15 = ((s8[4718592]{0:T(1024)(128)(4,1)}), s8[4194304]{0:T(1024)(128)(4,1)S(1)}, s32[]{:S(2)}) async-start(s8[4718592]{0:T(1024)(128)(4,1)} %bitcast.559), calls=%async_computation.40 | async-start | bytes 8388608
  156.1 146.4 %copy-start.27 = (f32[4,32,768]{2,1,0:T(8,128)}, f32[4,32,768]{2,1,0:T(8,128)S(1)}, u32[]{:S(2)}) copy-start(f32[4,32,768]{2,1,0:T(8,128)S(1)} %get-tuple-element.307) | copy-start | bytes 1179652
  156.1 146.3 %copy-start.156 = (f32[4,32]{1,0:T(4,128)}, f32[4,32]{1,0:T(4,128)S(1)}, u32[]{:S(2)}) copy-start(f32[4,32]{1,0:T(4,128)S(1)} %broadcast_multiply_fusion.24) | copy-start | bytes 1540
  171.2 133.8 %copy-start.26 = (f32[4,32,768]{2,1,0:T(8,128)}, f32[4,32,768]{2,1,0:T(8,128)S(1)}, u32[]{:S(2)}) copy-start(f32[4,32,768]{2,1,0:T(8,128)S(1)} %get-tuple-element.281) | copy-start | bytes 1179652
  239.8 45.9 %reduce-scatter.20.cloned.1.call-start = ((), (), s32[]{:S(2)}) async-start(), calls=%async_computation.12 | async-start | bytes 163840 | tf_op jit(solution)/shard_map/reduce_scatter | solution.py:378
  266.8 91.4 %reduce-scatter.22.cloned.1.call-start = ((), (), s32[]{:S(2)}) async-start(), calls=%async_computation.13 | async-start | bytes 2359296 | tf_op jit(solution)/shard_map/reduce_scatter | solution.py:381
  272.9 156.3 %reduce-scatter.24.cloned.1.call-start = ((), (), s32[]{:S(2)}) async-start(), calls=%async_computation.14 | async-start | bytes 2359296 | tf_op jit(solution)/shard_map/reduce_scatter | solution.py:381
  279.0 440.5 %reduce-scatter.26.cloned.1.call-start = ((), (), s32[]{:S(2)}) async-start(), calls=%async_computation.15 | async-start | bytes 2654208 | tf_op jit(solution)/shard_map/reduce_scatter | solution.py:521
  341.1 17.2 %copy-start.56 = (f32[512,128]{0,1:T(8,128)S(1)}, f32[512,128]{0,1:T(8,128)}, u32[]{:S(2)}) copy-start(f32[512,128]{0,1:T(8,128)} %copy-done.55) | copy-start | bytes 786436
  341.1 17.2 %copy-start.179 = (f32[512]{0:T(512)S(1)}, f32[512]{0:T(512)}, u32[]{:S(2)}) copy-start(f32[512]{0:T(512)} %copy-done.178) | copy-start | bytes 6148
  341.1 19.2 %copy-start.210 = (f32[512]{0:T(512)S(1)}, f32[512]{0:T(512)}, u32[]{:S(2)}) copy-start(f32[512]{0:T(512)} %copy-done.209) | copy-start | bytes 6148
  341.1 19.2 %copy-start.224 = (f32[512]{0:T(512)S(1)}, f32[512]{0:T(512)}, u32[]{:S(2)}) copy-start(f32[512]{0:T(512)} %copy-done.223) | copy-start | bytes 6148
  360.3 68.9 %copy-start.54 = (f32[512,128]{0,1:T(8,128)S(1)}, f32[512,128]{0,1:T(8,128)}, u32[]{:S(2)}) copy-start(f32[512,128]{0,1:T(8,128)} %copy-done.53) | copy-start | bytes 786436
  360.3 68.9 %copy-start.177 = (f32[512]{0:T(512)S(1)}, f32[512]{0:T(512)}, u32[]{:S(2)}) copy-start(f32[512]{0:T(512)} %copy-done.176) | copy-start | bytes 6148
  360.3 70.9 %copy-start.7 = (f32[512,768]{1,0:T(8,128)S(1)}, f32[512,768]{1,0:T(8,128)}, u32[]{:S(2)}) copy-start(f32[512,768]{1,0:T(8,128)} %copy-done.6) | copy-start | bytes 4718596
  360.3 70.9 %copy-start.185 = (f32[512]{0:T(512)S(1)}, f32[512]{0:T(512)}, u32[]{:S(2)}) copy-start(f32[512]{0:T(512)} %copy-done.184) | copy-start | bytes 6148
  360.3 70.9 %copy-start.208 = (f32[512]{0:T(512)S(1)}, f32[512]{0:T(512)}, u32[]{:S(2)}) copy-start(f32[512]{0:T(512)} %copy-done.207) | copy-start | bytes 6148
  434.7 15.7 %copy-start.48 = (f32[512,768]{1,0:T(8,128)}, f32[512,768]{1,0:T(8,128)S(1)}, u32[]{:S(2)}) copy-start(f32[512,768]{1,0:T(8,128)S(1)} %get-tuple-element.224) | copy-start | bytes 4718596
  435.9 18.3 %copy-start.41 = (f32[512,768]{1,0:T(8,128)}, f32[512,768]{1,0:T(8,128)S(1)}, u32[]{:S(2)}) copy-start(f32[512,768]{1,0:T(8,128)S(1)} %get-tuple-element.228) | copy-start | bytes 4718596
  435.9 14.6 %slice-start.8 = ((s8[4718592]{0:T(1024)(128)(4,1)}), s8[4194304]{0:T(1024)(128)(4,1)S(1)}, s32[]{:S(2)}) async-start(s8[4718592]{0:T(1024)(128)(4,1)} %bitcast.553), calls=%async_computation.33 | async-start | bytes 8388608
  472.6 15.8 %copy-start.72 = (bf16[12,64,512]{2,1,0:T(8,128)(2,1)}, bf16[12,64,512]{2,1,0:T(8,128)(2,1)S(1)}, u32[]{:S(2)}) copy-start(bf16[12,64,512]{2,1,0:T(8,128)(2,1)S(1)} %get-tuple-element.345) | copy-start | bytes 2359300
  473.7 12.4 %copy-start.22 = (f32[512,768]{1,0:T(8,128)}, f32[512,768]{1,0:T(8,128)S(1)}, u32[]{:S(2)}) copy-start(f32[512,768]{1,0:T(8,128)S(1)} %get-tuple-element.236) | copy-start | bytes 4718596
  488.4 232.7 %reduce-scatter.38.cloned.1.call-start = ((), (), s32[]{:S(2)}) async-start(), calls=%async_computation.23 | async-start | bytes 2654208
  517.2 205.7 %reduce-scatter.36.cloned.1.call-start = ((), (), s32[]{:S(2)}) async-start(), calls=%async_computation.22 | async-start | bytes 2654208
  517.5 12.9 %slice-start.10 = ((s8[12582912]{0:T(1024)(128)(4,1)}), s8[4194304]{0:T(1024)(128)(4,1)S(1)}, s32[]{:S(2)}) async-start(s8[12582912]{0:T(1024)(128)(4,1)} %bitcast.555), calls=%async_computation.35 | async-start | bytes 8388608
  518.3 12.1 slice-start.11
  518.3 12.1 slice-start.12
  518.3 12.1 copy-start.204
  547.9 226.3 %reduce-scatter.34.cloned.1.call-start = ((), (), s32[]{:S(2)}) async-start(), calls=%async_computation.21 | async-start | bytes 2654208
  573.5 365.6 %reduce-scatter.30.cloned.1.call-start = ((), (), s32[]{:S(2)}) async-start(), calls=%async_computation.17 | async-start | bytes 10616832 | tf_op jit(solution)/shard_map/reduce_scatter | solution.py:527
  600.7 503.1 %reduce-scatter.28.cloned.1.call-start = ((), (), s32[]{:S(2)}) async-start(), calls=%async_computation.16 | async-start | bytes 10616832 | tf_op jit(solution)/shard_map/reduce_scatter | solution.py:525
  628.5 540.0 %reduce-scatter.32.cloned.1.call-start = ((), (), s32[]{:S(2)}) async-start(), calls=%async_computation.18 | async-start | bytes 442368 | tf_op jit(solution)/shard_map/reduce_scatter | solution.py:531
  650.7 12.0 copy-start.225
  652.8 567.2 %all-reduce.14.cloned.1.call-start = ((), (), s32[]{:S(2)}) async-start(), calls=%async_computation.24 | async-start | bytes 3833856 | tf_op jit(solution)/shard_map/psum | solution.py:534
  941.3 164.7 %copy-start.15 = (bf16[768,768]{1,0:T(8,128)(2,1)S(1)}, bf16[768,768]{1,0:T(8,128)(2,1)}, u32[]{:S(2)}) copy-start(bf16[768,768]{1,0:T(8,128)(2,1)} %param.26) | copy-start | bytes 3538948
  1110.6 58.6 %copy-start.266 = (bf16[96]{0:T(256)(128)(2,1)S(1)}, bf16[96]{0:T(256)(128)(2,1)}, u32[]{:S(2)}) copy-start(bf16[96]{0:T(256)(128)(2,1)} %dynamic-slice.41) | copy-start | bytes 580
  1110.6 58.6 %copy-start.267 = (bf16[96]{0:T(256)(128)(2,1)S(1)}, bf16[96]{0:T(256)(128)(2,1)}, u32[]{:S(2)}) copy-start(bf16[96]{0:T(256)(128)(2,1)} %dynamic-slice.42) | copy-start | bytes 580
  1110.6 58.6 %copy-start.268 = (bf16[96]{0:T(256)(128)(2,1)S(1)}, bf16[96]{0:T(256)(128)(2,1)}, u32[]{:S(2)}) copy-start(bf16[96]{0:T(256)(128)(2,1)} %dynamic-slice.43) | copy-start | bytes 580
  1110.7 58.6 %copy-start.269 = (bf16[96]{0:T(256)(128)(2,1)S(1)}, bf16[96]{0:T(256)(128)(2,1)}, u32[]{:S(2)}) copy-start(bf16[96]{0:T(256)(128)(2,1)} %dynamic-slice.44) | copy-start | bytes 580
  1110.7 58.6 %copy-start.270 = (bf16[96]{0:T(256)(128)(2,1)S(1)}, bf16[96]{0:T(256)(128)(2,1)}, u32[]{:S(2)}) copy-start(bf16[96]{0:T(256)(128)(2,1)} %dynamic-slice.45) | copy-start | bytes 580
  (254 other events, 847.6 us)
Sparse Core Ops, SparseCore 0:
  120.2 42.1 all-gather.4
  164.4 38.4 all-gather.6
  239.9 18.7 reduce-scatter.17
  266.9 18.7 reduce-scatter.19
  289.7 68.4 reduce-scatter.21
  361.6 67.5 reduce-scatter.23
  488.5 68.5 reduce-scatter.25
  560.6 68.8 reduce-scatter.37
  633.0 69.0 reduce-scatter.35
  705.4 68.7 reduce-scatter.33
  777.8 161.2 reduce-scatter.29
  942.6 161.1 reduce-scatter.27
  1107.1 61.3 reduce-scatter.31
  1172.2 47.7 all-reduce.13
where the time goes:
time: 1250 us; the launch traced here: 1230 us
  waiting for transfers between devices  557 us (45%)
  matrix products  381 us (30%)
  local copies, waits for them, and re-layouts  106 us (8%)
  other arithmetic  97.7 us (8%)
  blocking collectives  72 us (6%)
  between operations  18.8 us (2%)
    reduce_scatter x1, waiting for transfers between devices, local(): lax.psum_scatter(grad_outer_weight, 'wide', scatter_dimension=0, tiled=True)  163 us
    reduce_scatter x1, waiting for transfers between devices, local(): lax.psum_scatter(grad_inner_weight, 'wide', scatter_dimension=0, tiled=True)  162 us
    dot_general x28, matrix products, outer_sum(): jnp.einsum('bld,ble->de', left_low, grad_low, preferred_element_type=jnp....  89.2 us
    reduce_scatter x2, waiting for transfers between devices, grid_line(): lax.psum_scatter(passage_part, 'wide', scatter_dimension=0, tiled=True)  80.1 us
    dot_general x28, matrix products, product(): return jnp.dot(left_side, right_side, preferred_element_type=jnp.float32)  78.1 us
    dot_general x28, matrix products, product_back(): jnp.einsum('ble,de->bld', grad_low, weight_in, preferred_element_type=jnp...  77.9 us
    reduce_scatter x1, waiting for transfers between devices, local(): lax.psum_scatter(grad_linear_weight, 'wide', scatter_dimension=0, tiled=T...  55.9 us
    unnamed x627, local copies, waits for them, and re-layouts  55.4 us
  transfers between devices with their start and end apart: 14, of which 9 were waited for; matrix products, arithmetic and copies ran while one was open for 29% of the time, Pallas kernels for 0%

commit v1 on v0

v1 whole, which is shorter than its diff:
```python
import functools

import jax
import jax.numpy as jnp
from jax import lax
from jax.experimental import pallas as pl
from jax.experimental.pallas import tpu as pltpu
from jax.sharding import PartitionSpec as P

HEADS = 12
HEAD_DIM = 64
SHARP = 16.0
LAYER_EPS = 1e-12
NORM_EPS = 1e-06
MASKED = -1e30
SLOPE_CONST = 0.3989422804014327
ROOT_HALF = 0.7071067811865476
BF16 = jnp.bfloat16
F32 = jnp.float32
VMEM_LIMIT = 62 * 1024 * 1024

NN = (((1,), (0,)), ((), ()))
NT = (((1,), (1,)), ((), ()))
TN = (((0,), (0,)), ((), ()))


def mm(left, right, dims=NN):
    return lax.dot_general(left, right, dims, preferred_element_type=F32)


ANY = pl.BlockSpec(memory_space=pl.ANY)

ROW_BQ, ROW_BV, ROW_BO, ROW_G1, ROW_S1, ROW_B2, ROW_G2, ROW_S2, ROW_BI = range(9)


def vec_row(vec_ref, row):
    return vec_ref[row : row + 1, :]


def mean_row(value):
    return jnp.sum(value, axis=-1, keepdims=True) * (1.0 / value.shape[-1])


class Loader:
    def __init__(self, sources, targets, sem):
        self.copies = [
            pltpu.make_async_copy(source, target, sem.at[index])
            for index, (source, target) in enumerate(zip(sources, targets))
        ]
        self.first = pl.program_id(0) == 0

    def start(self):
        @pl.when(self.first)
        def _():
            for copy in self.copies:
                copy.start()

    def need(self, *indices):
        @pl.when(self.first)
        def _():
            for index in indices:
                self.copies[index].wait()


def fwd_kernel(grouped, alias_count, *refs):
    lens_ref, x_ref, vec_ref = refs[:3]
    sources = refs[3:10]
    refs = refs[10 + alias_count :]
    (
        q_ref,
        k_ref,
        v_ref,
        att_ref,
        ctx_ref,
        n1_ref,
        r1_ref,
        first_ref,
        act_ref,
        slope_ref,
        n2_ref,
        r2_ref,
        final_ref,
        unit_ref,
        uinv_ref,
        embed_ref,
    ) = refs[:16]
    wq, wk, wv, wo, wi, w2, wl, sem, acc_ref = refs[16:]
    loader = Loader(sources, (wq, wk, wv, wo, wi, w2, wl), sem)
    loader.start()
    rows = x_ref.shape[0]
    x = x_ref[...]
    scale = HEAD_DIM ** (-0.5)
    loader.need(0)
    q_ref[...] = ((mm(x, wq[...]) + vec_row(vec_ref, ROW_BQ)).astype(BF16) * scale).astype(BF16)
    loader.need(1)
    k_ref[...] = mm(x, wk[...]).astype(BF16)
    loader.need(2)
    v_ref[...] = (mm(x, wv[...]) + vec_row(vec_ref, ROW_BV)).astype(BF16)
    if grouped:
        valid = (
            lax.broadcasted_iota(jnp.int32, (rows, rows), 0) // grouped
            == lax.broadcasted_iota(jnp.int32, (rows, rows), 1) // grouped
        )
    else:
        length = lens_ref[pl.program_id(0)]
        valid = lax.broadcasted_iota(jnp.int32, (1, rows), 1) < length
    bias = jnp.where(valid, 0.0, MASKED)
    low_half = lax.broadcasted_iota(jnp.int32, (rows, 128), 1) < HEAD_DIM

    def pair_body(pair, carry):
        cols = pl.ds(pl.multiple_of(pair * 128, 128), 128)
        q_pair, k_pair, v_pair = q_ref[:, cols], k_ref[:, cols], v_ref[:, cols]
        parts = []
        for half in range(2):
            mask = low_half if half == 0 else jnp.logical_not(low_half)
            logits = mm(jnp.where(mask, q_pair, jnp.zeros_like(q_pair)), k_pair, NT) + bias
            peak = jnp.max(logits, axis=-1, keepdims=True)
            e = jnp.exp(logits - peak)
            inv = 1.0 / jnp.sum(e, axis=-1, keepdims=True)
            low = (e * inv).astype(BF16)
            att_ref[0, 2 * pair + half] = low
            parts.append(mm(low, v_pair))
        ctx_ref[:, cols] = jnp.where(low_half, parts[0], parts[1]).astype(BF16)
        return carry

    lax.fori_loop(0, HEADS // 2, pair_body, 0)
    loader.need(3)
    field = x.astype(F32) + (mm(ctx_ref[...], wo[...]) + vec_row(vec_ref, ROW_BO))
    center = field - mean_row(field)
    inverse = lax.rsqrt(mean_row(center * center) + LAYER_EPS)
    normed = center * inverse
    n1_ref[...] = normed.astype(BF16)
    r1_ref[...] = jnp.broadcast_to(inverse, r1_ref.shape)
    first = normed * vec_row(vec_ref, ROW_G1) + vec_row(vec_ref, ROW_S1)
    first_ref[...] = first.astype(BF16)
    acc_ref[...] = first + vec_row(vec_ref, ROW_B2)
    loader.need(4, 5)
    width = x.shape[1]

    def chunk_body(chunk, carry):
        cols = pl.ds(pl.multiple_of(chunk * width, width), width)
        inner = mm(first_ref[...], wi[:, cols]) + vec_ref[pl.ds(ROW_BI + chunk, 1), :]
        phi = 0.5 * (1.0 + lax.erf(inner * ROOT_HALF))
        activated = (inner * phi).astype(BF16)
        act_ref[:, cols] = activated
        slope_ref[:, cols] = (phi + inner * jnp.exp(-0.5 * inner * inner) * SLOPE_CONST).astype(
            BF16
        )
        acc_ref[...] += mm(activated, w2[cols, :])
        return carry

    lax.fori_loop(0, wi.shape[1] // width, chunk_body, 0)
    field = acc_ref[...]
    center = field - mean_row(field)
    inverse = lax.rsqrt(mean_row(center * center) + LAYER_EPS)
    normed = center * inverse
    n2_ref[...] = normed.astype(BF16)
    r2_ref[...] = jnp.broadcast_to(inverse, r2_ref.shape)
    final = (normed * vec_row(vec_ref, ROW_G2) + vec_row(vec_ref, ROW_S2)).astype(BF16)
    final_ref[...] = final
    loader.need(6)
    projected = mm(final, wl[...])
    uinv = lax.rsqrt(jnp.sum(projected * projected, axis=-1, keepdims=True) + NORM_EPS)
    unit = projected * uinv
    unit_ref[...] = unit
    uinv_ref[...] = jnp.broadcast_to(uinv, uinv_ref.shape)
    embed_ref[...] = unit.astype(BF16)


def encode(x, lens, vec, weights, blocks, grouped, total, offset, earlier):
    rows = x.shape[0] // blocks
    width = x.shape[1]
    wide = weights[4].shape[1]
    embed_width = weights[6].shape[1]
    base = offset // rows

    def row_spec(columns):
        return pl.BlockSpec((rows, columns), lambda i, lens: (base + i, 0))

    def own_spec(columns):
        return pl.BlockSpec((rows, columns), lambda i, lens: (i, 0))

    def shape(count, columns, dtype):
        return jax.ShapeDtypeStruct((count, columns), dtype)

    own = x.shape[0]
    out_shapes = [
        shape(own, width, BF16),
        shape(own, width, BF16),
        shape(own, width, BF16),
        jax.ShapeDtypeStruct((blocks, HEADS, rows, rows), BF16),
        shape(total, width, BF16),
        shape(own, width, BF16),
        shape(own, embed_width, F32),
        shape(total, width, BF16),
        shape(total, wide, BF16),
        shape(own, wide, BF16),
        shape(own, width, BF16),
        shape(own, embed_width, F32),
        shape(total, width, BF16),
        shape(own, embed_width, F32),
        shape(own, embed_width, F32),
        shape(own, embed_width, BF16),
    ]
    shared = (4, 7, 8, 12)
    out_specs = [
        pl.BlockSpec((1, HEADS, rows, rows), lambda i, lens: (i, 0, 0, 0))
        if index == 3
        else (row_spec if index in shared else own_spec)(out.shape[1])
        for index, out in enumerate(out_shapes)
    ]
    aliased = [] if earlier is None else [earlier[index] for index in shared]
    return pl.pallas_call(
        functools.partial(fwd_kernel, grouped, len(aliased)),
        out_shape=out_shapes,
        grid_spec=pltpu.PrefetchScalarGridSpec(
            num_scalar_prefetch=1,
            grid=(blocks,),
            in_specs=[
                own_spec(width),
                pl.BlockSpec(vec.shape, lambda i, lens: (0, 0)),
            ]
            + [ANY] * (7 + len(aliased)),
            out_specs=out_specs,
            scratch_shapes=[pltpu.VMEM(weight.shape, BF16) for weight in weights]
            + [pltpu.SemaphoreType.DMA((7,)), pltpu.VMEM((rows, width), F32)],
        ),
        input_output_aliases={10 + index: shared[index] for index in range(len(aliased))},
        compiler_params=pltpu.CompilerParams(vmem_limit_bytes=VMEM_LIMIT),
        name="encode_queries" if grouped else "encode_passages",
    )(lens, x, vec, *weights, *aliased)


def sims_kernel(lens_ref, q_ref, p_ref, e_ref, z_ref):
    count = q_ref.shape[0]
    tokens = count * q_ref.shape[2]
    query = q_ref[...].reshape(tokens, q_ref.shape[3])
    sims = mm(p_ref[0], query, NT)
    slot = lax.broadcasted_iota(jnp.int32, sims.shape, 0)
    e = jnp.where(slot < lens_ref[pl.program_id(0)], jnp.exp(SHARP * sims - SHARP), 0.0)
    e_ref[0] = e.astype(BF16)
    z = jnp.sum(e, axis=0, keepdims=True)
    step = q_ref.shape[2]
    for index in range(count):
        z_ref[0, index : index + 1, :] = z[:, index * step : (index + 1) * step]


def sims_back_kernel(e_ref, w_ref, q_ref, p_ref, gp_ref, gq_ref):
    count = q_ref.shape[0]
    step = q_ref.shape[2]
    query = q_ref[...].reshape(count * step, q_ref.shape[3])
    weight = jnp.concatenate([w_ref[0, index : index + 1, :] for index in range(count)], axis=1)
    grads = (e_ref[0].astype(F32) * weight).astype(BF16)
    part = mm(grads, query)

    @pl.when(pl.program_id(1) == 0)
    def _():
        gp_ref[0] = part

    @pl.when(pl.program_id(1) > 0)
    def _():
        gp_ref[0] += part

    gq_ref[...] = mm(grads, p_ref[0], TN).astype(BF16).reshape(gq_ref.shape)


def similarity(queries, passages, lens):
    devices, micro, tokens, width = queries.shape
    slots = passages.shape[1]
    group = 8
    e, z = pl.pallas_call(
        sims_kernel,
        out_shape=(
            jax.ShapeDtypeStruct((micro, slots, devices * tokens), BF16),
            jax.ShapeDtypeStruct((micro, devices, tokens), F32),
        ),
        grid_spec=pltpu.PrefetchScalarGridSpec(
            num_scalar_prefetch=1,
            grid=(micro, devices // group),
            in_specs=[
                pl.BlockSpec((group, 1, tokens, width), lambda m, b, lens: (b, m, 0, 0)),
                pl.BlockSpec((1, slots, width), lambda m, b, lens: (m, 0, 0)),
            ],
            out_specs=(
                pl.BlockSpec((1, slots, group * tokens), lambda m, b, lens: (m, 0, b)),
                pl.BlockSpec((1, group, tokens), lambda m, b, lens: (m, b, 0)),
            ),
        ),
        compiler_params=pltpu.CompilerParams(vmem_limit_bytes=VMEM_LIMIT),
        name="similarity",
    )(lens, queries, passages)
    return e, z


def similarity_back(e, weights, queries, passages):
    devices, micro, tokens, width = queries.shape
    slots = passages.shape[1]
    group = 8
    return pl.pallas_call(
        sims_back_kernel,
        out_shape=(
            jax.ShapeDtypeStruct((micro, slots, width), F32),
            jax.ShapeDtypeStruct((devices, micro, tokens, width), BF16),
        ),
        grid=(micro, devices // group),
        in_specs=[
            pl.BlockSpec((1, slots, group * tokens), lambda m, b: (m, 0, b)),
            pl.BlockSpec((1, group, tokens), lambda m, b: (m, b, 0)),
            pl.BlockSpec((group, 1, tokens, width), lambda m, b: (b, m, 0, 0)),
            pl.BlockSpec((1, slots, width), lambda m, b: (m, 0, 0)),
        ],
        out_specs=(
            pl.BlockSpec((1, slots, width), lambda m, b: (m, 0, 0)),
            pl.BlockSpec((group, 1, tokens, width), lambda m, b: (b, m, 0, 0)),
        ),
        compiler_params=pltpu.CompilerParams(vmem_limit_bytes=VMEM_LIMIT),
        name="similarity_back",
    )(e, weights, queries, passages)


def accumulate(ref, row, value):
    ref[row : row + 1, :] += jnp.sum(value, axis=0, keepdims=True)


def mlp_back_kernel(alias_count, *refs):
    (
        ge_ref,
        unit_ref,
        uinv_ref,
        n2_ref,
        r2_ref,
        slope_ref,
        n1_ref,
        r1_ref,
        vec_ref,
    ) = refs[:9]
    sources = refs[9:12]
    refs = refs[12 + alias_count :]
    gp_ref, go_ref, gi_ref, gh_ref, ga_ref, sums_ref = refs[:6]
    wl, w2, wi, sem, acc_ref = refs[6:]
    loader = Loader(sources, (wl, w2, wi), sem)
    loader.start()

    @pl.when(loader.first)
    def _():
        sums_ref[...] = jnp.zeros_like(sums_ref)

    grad = ge_ref[...]
    unit = unit_ref[...]
    projected_low = (
        uinv_ref[...] * (grad - unit * jnp.sum(grad * unit, axis=-1, keepdims=True))
    ).astype(BF16)
    gp_ref[...] = projected_low
    loader.need(0)
    grad_final = mm(projected_low, wl[...], NT)
    normed = n2_ref[...].astype(F32)
    accumulate(sums_ref, ROW_G2, grad_final * normed)
    accumulate(sums_ref, ROW_S2, grad_final)
    scaled = grad_final * vec_row(vec_ref, ROW_G2)
    grad_second = r2_ref[:, :1] * (scaled - mean_row(scaled) - normed * mean_row(scaled * normed))
    outer_low = grad_second.astype(BF16)
    go_ref[...] = outer_low
    accumulate(sums_ref, ROW_B2, outer_low.astype(F32))
    acc_ref[...] = grad_second
    loader.need(1, 2)
    width = go_ref.shape[1]

    def chunk_body(chunk, carry):
        cols = pl.ds(pl.multiple_of(chunk * width, width), width)
        grad_act = mm(go_ref[...], w2[cols, :], NT)
        inner = (grad_act * slope_ref[:, cols].astype(F32)).astype(BF16)
        gi_ref[:, cols] = inner
        sums_ref[pl.ds(ROW_BI + chunk, 1), :] += jnp.sum(
            inner.astype(F32), axis=0, keepdims=True
        )
        acc_ref[...] += mm(inner, wi[:, cols], NT)
        return carry

    lax.fori_loop(0, wi.shape[1] // width, chunk_body, 0)
    grad_first = acc_ref[...]
    normed = n1_ref[...].astype(F32)
    accumulate(sums_ref, ROW_G1, grad_first * normed)
    accumulate(sums_ref, ROW_S1, grad_first)
    scaled = grad_first * vec_row(vec_ref, ROW_G1)
    hidden = r1_ref[:, :1] * (scaled - mean_row(scaled) - normed * mean_row(scaled * normed))
    gh_ref[...] = hidden
    low = hidden.astype(BF16)
    ga_ref[...] = low
    accumulate(sums_ref, ROW_BO, low.astype(F32))


def mlp_back(grad_embed, kept, vec, weights, blocks, total, offset, earlier):
    own = grad_embed.shape[0]
    rows = own // blocks
    base = offset // rows
    _, _, _, _, wi, w2, wl = weights
    width, wide = wi.shape
    embed_width = wl.shape[1]

    def row_spec(columns):
        return pl.BlockSpec((rows, columns), lambda i: (base + i, 0))

    def own_spec(columns):
        return pl.BlockSpec((rows, columns), lambda i: (i, 0))

    args = [grad_embed] + [kept[index] for index in (13, 14, 10, 11, 9, 5, 6)]
    out_shapes = [
        jax.ShapeDtypeStruct((total, embed_width), BF16),
        jax.ShapeDtypeStruct((total, width), BF16),
        jax.ShapeDtypeStruct((total, wide), BF16),
        jax.ShapeDtypeStruct((own, width), F32),
        jax.ShapeDtypeStruct((total, width), BF16),
        jax.ShapeDtypeStruct((16, width), F32),
    ]
    shared = (0, 1, 2, 4)
    out_specs = [
        (row_spec if index in shared else own_spec)(out.shape[1])
        for index, out in enumerate(out_shapes[:5])
    ] + [pl.BlockSpec((16, width), lambda i: (0, 0))]
    aliased = [] if earlier is None else [earlier[index] for index in shared]
    return pl.pallas_call(
        functools.partial(mlp_back_kernel, len(aliased)),
        out_shape=out_shapes,
        grid=(blocks,),
        in_specs=[own_spec(arg.shape[1]) for arg in args]
        + [pl.BlockSpec(vec.shape, lambda i: (0, 0))]
        + [ANY] * (3 + len(aliased)),
        out_specs=out_specs,
        scratch_shapes=[pltpu.VMEM(weight.shape, BF16) for weight in (wl, w2, wi)]
        + [pltpu.SemaphoreType.DMA((3,)), pltpu.VMEM((rows, width), F32)],
        input_output_aliases={12 + index: shared[index] for index in range(len(aliased))},
        compiler_params=pltpu.CompilerParams(vmem_limit_bytes=VMEM_LIMIT),
        name="mlp_back_queries" if earlier is not None else "mlp_back_passages",
    )(*args, vec, wl, w2, wi, *aliased)


def attention_back_kernel(alias_count, *refs):
    ga_ref, gh_ref, att_ref, q_ref, k_ref, v_ref = refs[:6]
    sources = refs[6:10]
    refs = refs[10 + alias_count :]
    gqkv_ref, gx_ref, sums_ref = refs[:3]
    wo, wq, wk, wv, sem, gc_ref = refs[3:]
    loader = Loader(sources, (wo, wq, wk, wv), sem)
    loader.start()

    @pl.when(loader.first)
    def _():
        sums_ref[...] = jnp.zeros_like(sums_ref)

    rows, width = gh_ref.shape
    scale = HEAD_DIM ** (-0.5)
    loader.need(0)
    gc_ref[...] = mm(ga_ref[...], wo[...], NT).astype(BF16)
    low_half = lax.broadcasted_iota(jnp.int32, (rows, 128), 1) < HEAD_DIM

    def pair_body(pair, carry):
        cols = pl.ds(pl.multiple_of(pair * 128, 128), 128)
        q_pair, k_pair, v_pair, gc_pair = q_ref[:, cols], k_ref[:, cols], v_ref[:, cols], gc_ref[:, cols]
        parts = []
        for half in range(2):
            mask = low_half if half == 0 else jnp.logical_not(low_half)
            low = att_ref[0, 2 * pair + half]
            att = low.astype(F32)
            grad_att = mm(jnp.where(mask, gc_pair, jnp.zeros_like(gc_pair)), v_pair, NT)
            weighted = grad_att * att
            grad_logits = (weighted - att * jnp.sum(weighted, axis=-1, keepdims=True)).astype(BF16)
            parts.append(
                (
                    mm(grad_logits, k_pair) * scale,
                    mm(grad_logits, q_pair, TN),
                    mm(low, gc_pair, TN),
                )
            )
        for index in range(3):
            gqkv_ref[:, pl.ds(pl.multiple_of(index * width + pair * 128, 128), 128)] = jnp.where(
                low_half, parts[0][index], parts[1][index]
            ).astype(BF16)
        return carry

    lax.fori_loop(0, HEADS // 2, pair_body, 0)
    loader.need(1, 2, 3)
    grad_q, grad_k, grad_v = (
        gqkv_ref[:, :width],
        gqkv_ref[:, width : 2 * width],
        gqkv_ref[:, 2 * width :],
    )
    accumulate(sums_ref, 0, grad_q.astype(F32))
    accumulate(sums_ref, 1, grad_v.astype(F32))
    gx_ref[...] = (
        gh_ref[...]
        + mm(grad_q, wq[...], NT)
        + mm(grad_k, wk[...], NT)
        + mm(grad_v, wv[...], NT)
    )


def attention_back(attended, hidden, kept, weights, blocks, total, offset, earlier):
    own, width = hidden.shape
    rows = own // blocks
    base = offset // rows
    wq, wk, wv, wo = weights[:4]

    def row_spec(columns):
        return pl.BlockSpec((rows, columns), lambda i: (base + i, 0))

    def own_spec(columns):
        return pl.BlockSpec((rows, columns), lambda i: (i, 0))

    aliased = [] if earlier is None else [earlier]
    return pl.pallas_call(
        functools.partial(attention_back_kernel, len(aliased)),
        out_shape=(
            jax.ShapeDtypeStruct((total, 3 * width), BF16),
            jax.ShapeDtypeStruct((own, width), F32),
            jax.ShapeDtypeStruct((8, width), F32),
        ),
        grid=(blocks,),
        in_specs=[
            row_spec(width),
            own_spec(width),
            pl.BlockSpec((1, HEADS, rows, rows), lambda i: (i, 0, 0, 0)),
            own_spec(width),
            own_spec(width),
            own_spec(width),
        ]
        + [ANY] * (4 + len(aliased)),
        out_specs=(
            row_spec(3 * width),
            own_spec(width),
            pl.BlockSpec((8, width), lambda i: (0, 0)),
        ),
        scratch_shapes=[pltpu.VMEM(weight.shape, BF16) for weight in weights[:4]]
        + [pltpu.SemaphoreType.DMA((4,)), pltpu.VMEM((rows, width), BF16)],
        input_output_aliases={10: 0} if aliased else {},
        compiler_params=pltpu.CompilerParams(vmem_limit_bytes=VMEM_LIMIT),
        name="attention_back_queries" if aliased else "attention_back_passages",
    )(attended, hidden, kept[3], kept[0], kept[1], kept[2], wo, wq, wk, wv, *aliased)


MESH = pl.DeviceIdType.MESH


def remote(source, target, sems, index, device):
    return pltpu.make_async_remote_copy(
        src_ref=source,
        dst_ref=target,
        send_sem=sems[0].at[index],
        recv_sem=sems[1].at[index],
        device_id=device,
        device_id_type=MESH,
    )


def share_kernel(n_wide, n_narrow, own_ref, all_ref, send_sem, recv_sem):
    me = lax.axis_index("narrow") * n_wide + lax.axis_index("wide")
    total = n_wide * n_narrow
    sems = (send_sem, recv_sem)

    def device(index):
        return (lax.rem(index, n_wide), index // n_wide)

    barrier = pltpu.get_barrier_semaphore()

    def signal(step, carry):
        pl.semaphore_signal(
            barrier, inc=1, device_id=device(lax.rem(me + step, total)), device_id_type=MESH
        )
        return carry

    def send(step, carry):
        target = device(lax.rem(me + step, total))
        remote(own_ref, all_ref.at[me], sems, step, target).start()
        return carry

    def wait(step, carry):
        source = lax.rem(me - step + total, total)
        copy = remote(own_ref, all_ref.at[source], sems, step, device(source))
        copy.wait_recv()
        copy.wait_send()
        return carry

    lax.fori_loop(1, total, signal, 0)
    all_ref[me] = own_ref[...]
    pl.semaphore_wait(barrier, total - 1)
    lax.fori_loop(1, total, send, 0)
    lax.fori_loop(1, total, wait, 0)


def share_scores(own, n_wide, n_narrow):
    total = n_wide * n_narrow
    return pl.pallas_call(
        functools.partial(share_kernel, n_wide, n_narrow),
        out_shape=jax.ShapeDtypeStruct((total,) + own.shape, own.dtype),
        in_specs=[pl.BlockSpec(memory_space=pltpu.VMEM)],
        out_specs=pl.BlockSpec(memory_space=pltpu.VMEM),
        scratch_shapes=[pltpu.SemaphoreType.DMA((total,))] * 2,
        compiler_params=pltpu.CompilerParams(collective_id=1, has_side_effects=True),
        name="share_scores",
    )(own)


def exchange_kernel(n_wide, n_narrow, g_ref, out_ref, half, arrived, inbox, *sems):
    pair_sems, far_sems = sems[:2], sems[2:]
    wide, narrow = lax.axis_index("wide"), lax.axis_index("narrow")
    core = lax.rem(narrow, 2)
    partner = (wide, narrow + 1 - 2 * core)
    rows = n_narrow // 2
    chips = n_wide * rows
    me = wide * rows + narrow // 2

    def device(chip):
        return (chip // rows, lax.rem(chip, rows) * 2 + core)

    barrier = pltpu.get_barrier_semaphore()

    def signal(step, carry):
        pl.semaphore_signal(
            barrier, inc=1, device_id=device(lax.rem(me + step, chips)), device_id_type=MESH
        )
        return carry

    pl.semaphore_signal(barrier, inc=1, device_id=partner, device_id_type=MESH)
    lax.fori_loop(1, chips, signal, 0)
    pl.semaphore_wait(barrier, chips)
    pair = remote(g_ref.at[:, 1 - core], arrived, pair_sems, 0, partner)
    pair.start()
    pair.wait_recv()

    def add(step, carry):
        chip = lax.rem(me + step, chips)
        total = g_ref[chip, core].astype(F32) + arrived[chip].astype(F32)
        half[chip] = total.astype(BF16)
        remote(half.at[chip], inbox.at[step], far_sems, step, device(chip)).start()
        return carry

    lax.fori_loop(1, chips, add, 0)
    out_ref[...] = g_ref[me, core].astype(F32) + arrived[me].astype(F32)

    def collect(step, carry):
        chip = lax.rem(me - step + chips, chips)
        copy = remote(half.at[chip], inbox.at[step], far_sems, step, device(chip))
        copy.wait_recv()
        copy.wait_send()
        out_ref[...] += inbox[step].astype(F32)
        return carry

    lax.fori_loop(1, chips, collect, 0)
    pair.wait_send()


def exchange(grads, n_wide, n_narrow):
    rows, width = grads.shape[1:]
    chips = n_wide * n_narrow // 2
    block = pltpu.VMEM((chips, rows, width), BF16)
    return pl.pallas_call(
        functools.partial(exchange_kernel, n_wide, n_narrow),
        out_shape=jax.ShapeDtypeStruct((rows, width), F32),
        in_specs=[pl.BlockSpec(memory_space=pltpu.VMEM)],
        out_specs=pl.BlockSpec(memory_space=pltpu.VMEM),
        scratch_shapes=[block, block, block]
        + [pltpu.SemaphoreType.DMA((1,))] * 2
        + [pltpu.SemaphoreType.DMA((chips,))] * 2,
        compiler_params=pltpu.CompilerParams(
            collective_id=2, has_side_effects=True, vmem_limit_bytes=VMEM_LIMIT
        ),
        name="exchange_query_gradients",
    )(grads.reshape(chips, 2, rows, width))


UNITS = ((0, 80), (160, 80), (80, 80), (240, 64))
SHARE_ROWS = 304


def tree_kernel(
    n_z, g_ref, out_ref, held, near, over_a, over_b, then_a, then_b, line, *sems
):
    (local_sem,) = sems[:1]
    core_sems, one_sems, two_sems, line_sems, copy_sems = (
        sems[1 + 2 * index : 3 + 2 * index] for index in range(5)
    )
    wide, narrow = lax.axis_index("wide"), lax.axis_index("narrow")
    z, x = wide // 2, lax.rem(wide, 2)
    y, core = narrow // 2, lax.rem(narrow, 2)
    mate = (wide, y * 2 + 1 - core)
    over_y = (wide, (1 - y) * 2 + core)
    over_x = (z * 2 + 1 - x, narrow)
    right, left = (wide + 2, narrow), (wide - 2, narrow)
    barrier = pltpu.get_barrier_semaphore()
    for device in (mate, over_y, over_x):
        pl.semaphore_signal(barrier, inc=1, device_id=device, device_id_type=MESH)

    @pl.when(z < n_z - 1)
    def _():
        pl.semaphore_signal(barrier, inc=1, device_id=right, device_id_type=MESH)

    @pl.when(z > 0)
    def _():
        pl.semaphore_signal(barrier, inc=1, device_id=left, device_id_type=MESH)

    inside = jnp.logical_and(z > 0, z < n_z - 1)
    pl.semaphore_wait(barrier, jnp.where(inside, 5, 4))

    def rows_of(unit):
        start, count = UNITS[unit]
        return pl.ds(start, count)

    def core_copy(unit):
        rows = rows_of(unit)
        return remote(
            g_ref.at[:, 1 - core, :, :, rows], near.at[:, :, :, rows], core_sems, unit, mate
        )

    def local_copy(unit):
        rows = rows_of(unit)
        return pltpu.make_async_copy(
            g_ref.at[:, core, :, :, rows], held.at[:, :, :, rows], local_sem.at[unit]
        )

    def one_copy(unit):
        rows = rows_of(unit)
        count = UNITS[unit][1]
        if unit % 2 == 0:
            return remote(
                held.at[1 - y, :, :, rows], over_a.at[unit // 2], one_sems, unit, over_y
            )
        return remote(
            held.at[:, :, 1 - x, rows],
            over_b.at[unit // 2, :, :, pl.ds(0, count)],
            one_sems,
            unit,
            over_x,
        )

    def two_copy(unit):
        rows = rows_of(unit)
        count = UNITS[unit][1]
        if unit % 2 == 0:
            return remote(held.at[y, :, 1 - x, rows], then_a.at[unit // 2], two_sems, unit, over_x)
        return remote(
            held.at[1 - y, :, x, rows],
            then_b.at[unit // 2, :, pl.ds(0, count)],
            two_sems,
            unit,
            over_y,
        )

    def line_copy(unit, target, way):
        rows = rows_of(unit)
        index = (unit * n_z + target) * 2 + way
        return remote(
            held.at[y, target, x, rows],
            line.at[way, target, rows],
            line_sems,
            index,
            right if way == 0 else left,
        )

    def add(target, extra):
        target[...] = (target[...].astype(F32) + extra[...].astype(F32)).astype(BF16)

    count_units = len(UNITS)
    for unit in range(count_units):
        core_copy(unit).start()
        local_copy(unit).start()
    for unit in range(count_units):
        rows = rows_of(unit)
        local_copy(unit).wait()
        core_copy(unit).wait_recv()

        def add_near(index, carry, rows=rows):
            row_y, rest = index // (n_z * 2), lax.rem(index, n_z * 2)
            at = (row_y, rest // 2, lax.rem(rest, 2), rows)
            add(held.at[at], near.at[at])
            return carry

        lax.fori_loop(0, 4 * n_z, add_near, 0)
        one_copy(unit).start()
    for unit in range(count_units):
        rows = rows_of(unit)
        count = UNITS[unit][1]
        copy = one_copy(unit)
        copy.wait_recv()

        def add_one(index, carry, rows=rows, unit=unit, count=count):
            first, second = index // 2, lax.rem(index, 2)
            if unit % 2 == 0:
                add(held.at[y, first, second, rows], over_a.at[unit // 2, first, second])
            else:
                add(
                    held.at[second, first, x, rows],
                    over_b.at[unit // 2, second, first, pl.ds(0, count)],
                )
            return carry

        lax.fori_loop(0, 2 * n_z, add_one, 0)
        two_copy(unit).start()
    for unit in range(count_units):
        rows = rows_of(unit)
        count = UNITS[unit][1]
        two_copy(unit).wait_recv()

        def add_two(index, carry, rows=rows, unit=unit, count=count):
            extra = then_a if unit % 2 == 0 else then_b
            add(held.at[y, index, x, rows], extra.at[unit // 2, index, pl.ds(0, count)])
            return carry

        lax.fori_loop(0, n_z, add_two, 0)
        for step in range(n_z - 1):
            for way in range(2):
                target = n_z - 1 - step if way == 0 else step
                sends = z < target if way == 0 else z > target
                edge = z > 0 if way == 0 else z < n_z - 1

                @pl.when(jnp.logical_and(sends, edge))
                def _(unit=unit, target=target, way=way, rows=rows):
                    line_copy(unit, target, way).wait_recv()
                    add(held.at[y, target, x, rows], line.at[way, target, rows])

                @pl.when(sends)
                def _(unit=unit, target=target, way=way):
                    line_copy(unit, target, way).start()

    def own_copy(unit, step):
        rows = rows_of(unit)
        index = unit * 3 + step
        slot = narrow if step < 2 else (1 - y) * 2 + core
        return remote(
            out_ref.at[slot, rows],
            out_ref.at[slot, rows],
            copy_sems,
            index,
            over_y if step == 1 else mate,
        )

    def arrived_copy(unit, step):
        rows = rows_of(unit)
        index = unit * 3 + step
        slot = (
            y * 2 + 1 - core,
            (1 - y) * 2 + core,
            (1 - y) * 2 + 1 - core,
        )[step]
        return remote(
            out_ref.at[slot, rows],
            out_ref.at[slot, rows],
            copy_sems,
            index,
            over_y if step == 1 else mate,
        )

    for unit in range(count_units):
        rows = rows_of(unit)
        for target in range(n_z):

            @pl.when(z == target)
            def _(unit=unit, target=target, rows=rows):
                if target > 0:
                    line_copy(unit, target, 0).wait_recv()
                    add(held.at[y, target, x, rows], line.at[0, target, rows])
                if target < n_z - 1:
                    line_copy(unit, target, 1).wait_recv()
                    add(held.at[y, target, x, rows], line.at[1, target, rows])

        out_ref[narrow, rows] = held[y, z, x, rows]
        own_copy(unit, 1).start()
        own_copy(unit, 0).start()
    for unit in range(count_units):
        arrived_copy(unit, 1).wait_recv()
        own_copy(unit, 2).start()
    for unit in range(count_units):
        arrived_copy(unit, 0).wait_recv()
        arrived_copy(unit, 2).wait_recv()
        for step in range(3):
            own_copy(unit, step).wait_send()
        core_copy(unit).wait_send()
        one_copy(unit).wait_send()
        two_copy(unit).wait_send()
        for target in range(n_z):
            for way in range(2):

                @pl.when(z < target if way == 0 else z > target)
                def _(unit=unit, target=target, way=way):
                    line_copy(unit, target, way).wait_send()


def tree(grads, n_wide):
    n_z = n_wide // 2
    width = grads.shape[-1]
    rows = SHARE_ROWS
    units = len(UNITS)
    sem = pltpu.SemaphoreType.DMA
    return pl.pallas_call(
        functools.partial(tree_kernel, n_z),
        out_shape=jax.ShapeDtypeStruct((4, rows, width), BF16),
        in_specs=[ANY],
        out_specs=pl.BlockSpec(memory_space=pltpu.VMEM),
        scratch_shapes=[
            pltpu.VMEM((2, n_z, 2, rows, width), BF16),
            pltpu.VMEM((2, n_z, 2, rows, width), BF16),
            pltpu.VMEM((2, n_z, 2, 80, width), BF16),
            pltpu.VMEM((2, 2, n_z, 80, width), BF16),
            pltpu.VMEM((2, n_z, 80, width), BF16),
            pltpu.VMEM((2, n_z, 80, width), BF16),
            pltpu.VMEM((2, n_z, rows, width), BF16),
            sem((units,)),
        ]
        + [sem((units,))] * 6
        + [sem((units * n_z * 2,))] * 2
        + [sem((units * 3,))] * 2,
        compiler_params=pltpu.CompilerParams(
            collective_id=3, has_side_effects=True, vmem_limit_bytes=VMEM_LIMIT
        ),
        name="sum_weight_gradients",
    )(grads.reshape(2, 2, n_z, 2, rows, width))


def outer(left, right):
    return lax.dot_general(left, right, TN, preferred_element_type=F32)


def local(
    query_states,
    passage_states,
    lengths,
    positives,
    query_weight,
    query_bias,
    key_weight,
    value_weight,
    value_bias,
    out_weight,
    out_bias,
    first_gain,
    first_shift,
    inner_weight,
    inner_bias,
    outer_weight,
    outer_bias,
    second_gain,
    second_shift,
    linear_weight,
):
    everyone = ("wide", "narrow")
    n_wide = lax.axis_size("wide")
    n_narrow = lax.axis_size("narrow")
    wide_index = lax.axis_index("wide")
    narrow_index = lax.axis_index("narrow")
    micro, own_queries, query_len, width = query_states.shape
    own_passages, slots = passage_states.shape[1:3]
    weights = (
        query_weight,
        key_weight,
        value_weight,
        out_weight,
        inner_weight,
        outer_weight,
        linear_weight,
    )
    embed_width = linear_weight.shape[1]
    vec = (
        jnp.concatenate(
            [
                query_bias,
                value_bias,
                out_bias,
                first_gain,
                first_shift,
                outer_bias,
                second_gain,
                second_shift,
                inner_bias,
            ]
        )
        .astype(F32)
        .reshape(-1, width)
    )
    vec = jnp.pad(vec, ((0, -vec.shape[0] % 8), (0, 0)))
    own_index = narrow_index * n_wide + wide_index
    own_lengths = lax.dynamic_slice_in_dim(lengths, own_index * own_passages, own_passages, axis=1)
    lens = own_lengths.reshape(-1)
    x_query = query_states.reshape(-1, width)
    x_passage = passage_states.reshape(-1, width)
    query_rows, passage_rows = x_query.shape[0], x_passage.shape[0]
    total = query_rows + passage_rows
    kept_q = encode(
        x_query, lens, vec, weights, 1, query_len, total, passage_rows, None
    )
    queries = lax.all_gather(kept_q[15].reshape(micro, -1, embed_width), everyone, axis=0)
    kept_p = encode(
        x_passage, lens, vec, weights, micro * own_passages, 0, total, 0, kept_q
    )
    ctx, first_low, act, final_low = (kept_p[index] for index in (4, 7, 8, 12))
    passages = kept_p[15].reshape(micro * own_passages, slots, embed_width)
    e, z = similarity(queries, passages, lens)
    best = SHARP + jnp.log(z)
    own_scores = jnp.sum(best.reshape(micro, -1, query_len), axis=-1) / SHARP
    full = share_scores(own_scores, n_wide, n_narrow)
    row_total = jax.nn.logsumexp(full, axis=0)
    passage_ids = jnp.arange(full.shape[0], dtype=jnp.int32)
    picked = jnp.sum(
        jnp.where(passage_ids[:, None, None] == positives[None], full, 0.0), axis=0
    )
    row_count = own_queries * n_narrow
    losses = lax.dynamic_slice_in_dim(row_total - picked, wide_index * row_count, row_count, axis=1)
    block = lax.dynamic_slice(
        full,
        (narrow_index * n_wide, 0, wide_index * row_count),
        (n_wide, micro, row_count),
    )
    scores = jnp.transpose(block, (1, 2, 0))
    grads = jnp.exp(own_scores - row_total) - (positives == own_index).astype(F32)
    token_weights = jnp.repeat(grads, query_len, axis=1).reshape(z.shape) / z
    grad_passage, grad_query = similarity_back(e, token_weights, queries, passages)
    grad_query = exchange(
        grad_query.reshape(-1, query_rows, embed_width), n_wide, n_narrow
    )
    grad_passage = grad_passage.reshape(passage_rows, embed_width)
    back_p = mlp_back(grad_passage, kept_p, vec, weights, micro * own_passages, total, 0, None)
    back_q = mlp_back(grad_query, kept_q, vec, weights, 1, total, passage_rows, back_p)
    gp, go, gi, _, ga, sums_q = back_q
    d_outer = outer(act, go)
    d_inner = outer(first_low, gi)
    d_linear = outer(final_low, gp)
    att_p = attention_back(ga, back_p[3], kept_p, weights, micro * own_passages, total, 0, None)
    att_q = attention_back(ga, back_q[3], kept_q, weights, 1, total, passage_rows, att_p[0])
    gqkv = att_q[0]
    x_all = jnp.concatenate([x_passage, x_query], axis=0)
    d_out = outer(ctx, ga)
    d_qkv = outer(x_all, gqkv)

    sums = back_p[5] + sums_q
    sums = jnp.concatenate([sums, att_p[2] + att_q[2]], axis=0)
    part = width // n_wide

    if part % 16 == 0 and n_narrow == 4:
        picks = (16, 17, ROW_BO, ROW_G1, ROW_S1, ROW_B2, ROW_G2, ROW_S2)
        vectors = jnp.concatenate(
            [sums[pick].reshape(n_wide, part) for pick in picks]
            + [sums[ROW_BI : ROW_BI + 4].reshape(n_wide, 4 * part)],
            axis=1,
        )
        vectors = jnp.pad(vectors, ((0, 0), (0, 16 * width - vectors.shape[1])))
        linear_rows = d_linear.astype(BF16).reshape(n_wide, -1, width)
        tails = jnp.stack(
            [linear_rows, vectors.astype(BF16).reshape(n_wide, 16, width)]
            + [jnp.zeros((n_wide, 16, width), BF16)] * 2
        )
        packed = jnp.concatenate(
            [
                d_outer.astype(BF16).reshape(n_wide, 4, part, width).transpose(1, 0, 2, 3),
                d_inner.astype(BF16).reshape(n_wide, part, 4, width).transpose(2, 0, 1, 3),
                jnp.stack(
                    [
                        d_qkv[:, index * width : (index + 1) * width]
                        .astype(BF16)
                        .reshape(n_wide, part, width)
                        for index in range(3)
                    ]
                    + [d_out.astype(BF16).reshape(n_wide, part, width)]
                ),
                tails,
            ],
            axis=2,
        )
        summed = tree(packed, n_wide).astype(F32)
        r_outer = summed[:, :part].reshape(4 * part, width)
        r_inner = summed[:, part : 2 * part].transpose(1, 0, 2).reshape(part, 4 * width)
        r_q, r_k, r_v, r_out = (summed[index, 2 * part : 3 * part] for index in range(4))
        r_linear = summed[0, 3 * part :].reshape(part, embed_width)
        flat = summed[1, 3 * part : 3 * part + 2].reshape(-1)
        v_q, v_v, v_o, v_g1, v_s1, v_2, v_g2, v_s2 = (
            flat[index * part : (index + 1) * part] for index in range(8)
        )
        v_i = flat[8 * part : 12 * part]
    else:

        def reduce(value):
            piece = lax.psum_scatter(value.astype(BF16), everyone, scatter_dimension=0, tiled=True)
            return lax.all_gather(piece, "narrow", axis=0, tiled=True).astype(F32)

        def vector(rows):
            flat = rows.reshape(-1)
            share = flat.shape[0] // n_wide
            return lax.dynamic_slice_in_dim(flat, wide_index * share, share)

        sums = lax.psum(sums, everyone)
        r_outer, r_inner, r_linear, r_out, r_qkv = (
            reduce(value) for value in (d_outer, d_inner, d_linear, d_out, d_qkv)
        )
        r_q, r_k, r_v = (r_qkv[:, index * width : (index + 1) * width] for index in range(3))
        v_q, v_v, v_o, v_g1, v_s1, v_2, v_g2, v_s2 = (
            vector(sums[pick])
            for pick in (16, 17, ROW_BO, ROW_G1, ROW_S1, ROW_B2, ROW_G2, ROW_S2)
        )
        v_i = vector(sums[ROW_BI : ROW_BI + 4])
    return (
        scores,
        losses,
        att_q[1].reshape(query_states.shape),
        att_p[1].reshape(passage_states.shape),
        r_q,
        v_q,
        r_k,
        r_v,
        v_v,
        r_out,
        v_o,
        v_g1,
        v_s1,
        r_inner,
        v_i,
        r_outer,
        v_2,
        v_g2,
        v_s2,
        r_linear,
    )


def solution(mesh):
    return jax.shard_map(
        local,
        mesh=mesh,
        in_specs=(
            P(None, ("wide", "narrow"), None, None),
            P(None, ("narrow", "wide"), None, None),
        )
        + (P(),) * 18,
        out_specs=(
            P(None, "wide", "narrow"),
            P(None, "wide"),
            P(None, ("wide", "narrow"), None, None),
            P(None, ("narrow", "wide"), None, None),
            P("wide", None),
            P("wide"),
            P("wide", None),
            P("wide", None),
            P("wide"),
            P("wide", None),
            P("wide"),
            P("wide"),
            P("wide"),
            P("wide", None),
            P("wide"),
            P("wide", None),
            P("wide"),
            P("wide"),
            P("wide"),
            P("wide", None),
        ),
        check_vma=False,
    )
```

time: 1250 us -> 454 us (0.36)
  waiting for transfers between devices: 557 us -> 7.47 us
  matrix products: 381 us -> 31.8 us
  Pallas kernels: 0 us -> 337 us
  other arithmetic: 97.7 us -> 23.5 us
  blocking collectives: 72 us -> 0 us
  local copies, waits for them, and re-layouts: 106 us -> 34.3 us
    reduce_scatter x8 -> x0, waiting for transfers between devices: 463 us -> none  [the longest x1 163 us: local(): lax.psum_scatter(grad_outer_weight, 'wide', scatter_dimension=0, tiled=True)]
    pallas_call x0 -> x11, Pallas kernels: none -> 337 us  [the longest x1 120 us: tree(): pl.pallas_call(functools.partial(tree_kernel, n_z), out_shape=jax.ShapeDt...]
    dot_general x110 -> x5, matrix products: 355 us -> 31.8 us  [outer(): return lax.dot_general(left, right, TN, preferred_element_type=F32)]
    unnamed x17 -> x1, waiting for transfers between devices: 49.8 us -> 0.02 us
    unnamed x627 -> x47, local copies, waits for them, and re-layouts: 55.4 us -> 10.6 us
    unnamed x1 -> x0, blocking collectives: 36.9 us -> none
    convert_element_type x36 -> x1, other arithmetic: 38.6 us -> 1.95 us  [local(): summed = tree(packed, n_wide).astype(F32)]
    psum x1 -> x0, waiting for transfers between devices: 35.1 us -> none  [local(): lax.psum(wide_query_weight.astype(jnp.bfloat16), 'narrow')]
  transfers between devices with their start and end apart: 14 -> 1, of which waited for: 9 -> 1; matrix products, arithmetic and copies ran while one was open for 29% -> 0% of each run, Pallas kernels for 0% -> 12%
where the time goes in v1:
time: 454 us; the launch traced here: 448 us
  Pallas kernels  337 us (74%)
  local copies, waits for them, and re-layouts  34.3 us (8%)
  matrix products  31.8 us (7%)
  other arithmetic  23.5 us (5%)
  between operations  14.7 us (3%)
  waiting for transfers between devices  7.47 us (2%)
    pallas_call x1, Pallas kernels, tree(): pl.pallas_call(functools.partial(tree_kernel, n_z), out_shape=jax.ShapeDt...  120 us
    pallas_call x2, Pallas kernels, encode(): pl.pallas_call(functools.partial(fwd_kernel, grouped, len(aliased)), out_...  70.4 us
    pallas_call x2, Pallas kernels, attention_back(): pl.pallas_call(functools.partial(attention_back_kernel, len(aliased)), ou...  49.7 us
    pallas_call x2, Pallas kernels, mlp_back(): pl.pallas_call(functools.partial(mlp_back_kernel, len(aliased)), out_shap...  37.6 us
    dot_general x5, matrix products, outer(): return lax.dot_general(left, right, TN, preferred_element_type=F32)  31.8 us
    pallas_call x1, Pallas kernels, exchange(): pl.pallas_call(functools.partial(exchange_kernel, n_wide, n_narrow), out_...  25.6 us
    concatenate x1, other arithmetic, local(): jnp.concatenate([d_outer.astype(BF16).reshape(n_wide, 4, part, width).tra...  14.8 us
    pallas_call x1, Pallas kernels, similarity_back(): pl.pallas_call(sims_back_kernel, out_shape=(jax.ShapeDtypeStruct((micro,...  13.8 us
  transfers between devices with their start and end apart: 1, of which 1 were waited for; matrix products, arithmetic and copies ran while one was open for 0% of the time, Pallas kernels for 12%

profile of v1, /device:TPU:0, one launch (start us, length us, event | category | flops | bytes accessed | tf_op | source)
XLA Modules:
  0.0 448.4 jit_solution(8055294258639663968)
XLA Ops:
  7.3 0.9 dynamic-update-slice
  8.1 0.8 dynamic-update-slice.1
  9.0 0.9 dynamic-update-slice.2
  9.8 0.9 dynamic-update-slice.3
  10.7 0.9 dynamic-update-slice.4
  11.5 0.8 dynamic-update-slice.5
  12.4 0.9 dynamic-update-slice.6
  13.2 0.9 dynamic-update-slice.7
  14.1 0.7 constant_dynamic-update-slice_fusion
  14.8 0.6 pad_convert_fusion.refs_2_.refs_8_
  15.5 0.7 dynamic-slice_reduce_fusion.refs_0_.lens_ref
  16.2 18.8 %encode_queries.1 = (bf16[256,768]{1,0:T(8,128)(2,1)}, bf16[256,768]{1,0:T(8,128)(2,1)}, bf16[256,768]{1,0:T(8,128)(2,1)}, bf16[1,12,256,256]{3,2,1,0:T(8,128)(2...) custom-call(s32[2]{0:T(128)} %dynamic-slice_reduce_fusion.refs_0_.le, ...), custom_call_target="tpu_custom_call" | custom-call | tf_op jit(solution)/shard_map/encode_queries/pallas_call | solution.py:213
  35.1 51.6 %encode_passages.1 = (bf16[1024,768]{1,0:T(8,128)(2,1)}, bf16[1024,768]{1,0:T(8,128)(2,1)}, bf16[1024,768]{1,0:T(8,128)(2,1)}, bf16[2,12,512,512]{3,2,1,0:T(8,12...) custom-call(s32[2]{0:T(128)} %dynamic-slice_reduce_fusion.refs_0_.le, ...), custom_call_target="tpu_custom_call", output_to_operand_aliasing={{4}: (10, {}), {7}: (11, {}), {8}: (12, {}), {12}: (13, {})} | custom-call | tf_op jit(solution)/shard_map/encode_passages/pallas_call | solution.py:213
  86.7 7.4 %all-gather.2.cloned.1.call-done.q_ref = bf16[32,2,128,128]{3,2,1,0:T(8,128)(2,1)} async-done(((bf16[1,2,128,128]{3,2,1,0:T(8,128)(2,1)}), bf16[32,2,128,128]{3,2,1,0:T(8,128)(2,1)}) %all-gather.2.cloned.1.call-update) | async-done | bytes 2097168 | tf_op jit(solution)/shard_map/all_gather | solution.py:988
  94.2 10.1 %similarity.1 = (bf16[2,512,4096]{2,1,0:T(8,128)(2,1)}, f32[2,32,128]{2,1,0:T(8,128)}) custom-call(s32[2]{0:T(128)} %dynamic-slice_reduce_fusion.refs_0_.lens_ref, bf16[32,2,128,128]{3,2,1,0:T(8,128)(2,1)} %all-gather.2.cloned.1.call-done.q_ref, bf16[2,512,128]{2,1,0:T(8,128)(2,1)} %bitcast.66), custom_call_target="tpu_custom_call" | custom-call | tf_op jit(solution)/shard_map/similarity/pallas_call | solution.py:271
  104.2 0.8 log_add_fusion
  105.1 0.1 reduce_sum.27
  105.2 0.6 broadcast_multiply_fusion.own_ref
  105.8 9.4 %share_scores.1 = f32[32,2,128]{2,1,0:T(2,128)} custom-call(f32[2,128]{1,0:T(2,128)} %broadcast_multiply_fusion.own_ref), custom_call_target="tpu_custom_call" | custom-call | tf_op jit(solution)/shard_map/share_scores/pallas_call | solution.py:591
  115.2 0.8 reduce_max.9
  116.0 0.8 exponential_reduce_fusion
  116.8 0.1 broadcast_in_dim.15
  116.9 0.1 reshape_reshape.6
  117.0 1.4 div.11.w_ref
  118.4 13.8 %similarity_back.1 = (f32[2,512,128]{2,1,0:T(8,128)}, bf16[32,2,128,128]{3,2,1,0:T(8,128)(2,1)}) custom-call(bf16[2,512,4096]{2,1,0:T(8,128)(2,1)} %get-tuple-element.81.e_ref, f32[2,32,128]{2,1,0:T(8,128)} %div.11.w_ref, bf16[32,2,128,128]{3,2,1,0:T(8,128)(2,1)} %all-gather.2.cloned.1.call-done.q_ref, bf16[2,512,128]{2,1,0:T(8,128)(2,1)} %bitcast.67), custom_call_target="tpu_custom_call" | custom-call | tf_op jit(solution)/shard_map/similarity_back/pallas_call | solution.py:299
  132.2 25.6 %exchange_query_gradients.1.refs_0_ = f32[256,128]{1,0:T(8,128)} custom-call(bf16[16,2,256,128]{3,2,1,0:T(8,128)(2,1)} %bitcast.60), custom_call_target="tpu_custom_call" | custom-call | tf_op jit(solution)/shard_map/exchange_query_gradients/pallas_call | solution.py:655
  157.8 26.5 %mlp_back_passages.1 = (bf16[1280,128]{1,0:T(8,128)(2,1)}, bf16[1280,768]{1,0:T(8,128)(2,1)}, bf16[1280,3072]{1,0:T(8,128)(2,1)}, f32[1024,768]{1,0:T(8,128)}, b...) custom-call(f32[1024,128]{1,0:T(8,128)} %bitcast.69, f32[1024,128]{1,0:T(8,128)} %get-tuple-element.91.refs_1_, ...), custom_call_target="tpu_custom_call" | custom-call | tf_op jit(solution)/shard_map/mlp_back_passages/pallas_call | solution.py:421
  184.3 11.0 %mlp_back_queries.1 = (bf16[1280,128]{1,0:T(8,128)(2,1)}, bf16[1280,768]{1,0:T(8,128)(2,1)}, bf16[1280,3072]{1,0:T(8,128)(2,1)}, f32[256,768]{1,0:T(8,128)}, bf1...) custom-call(f32[256,128]{1,0:T(8,128)} %exchange_query_gradients.1.r, ...), custom_call_target="tpu_custom_call", output_to_operand_aliasing={{0}: (12, {}), {1}: (13, {}), {2}: (14, {}), {4}: (15, {})} | custom-call | tf_op jit(solution)/shard_map/mlp_back_queries/pallas_call | solution.py:421
  195.4 0.8 add_convert_fusion
  196.3 38.0 %attention_back_passages.1 = (bf16[1280,2304]{1,0:T(8,128)(2,1)}, f32[1024,768]{1,0:T(8,128)}, f32[8,768]{1,0:T(8,128)}) custom-call(bf16[1280,768]{1,0:T(8,128)(2,1)} %get-tuple-element.102.refs_0_, f32[1024,768]{1,0:T(8,128)} %get-tuple-element.108.refs_1_, bf16[2,12,512,512]{3,2,1,0:T(8,128)(2,1)} %get-tuple-element.109.refs_2_, ...), custom_call_target="tpu_custom_call" | custom-call | tf_op jit(solution)/shard_map/attention_back_passages/pallas_call | solution.py:510
  234.3 11.7 %attention_back_queries.1 = (bf16[1280,2304]{1,0:T(8,128)(2,1)}, f32[256,768]{1,0:T(8,128)}, f32[8,768]{1,0:T(8,128)}) custom-call(bf16[1280,768]{1,0:T(8,128)(2,1)} %get-tuple-element.102.refs_0_, f32[256,768]{1,0:T(8,128)} %get-tuple-element.103.refs_1_, bf16[1,12,256,256]{3,2,1,0:T(8,128)(2,1)} %get-tuple-element.104.refs_2_, ...), custom_call_target="tpu_custom_call", output_to_operand_aliasing={{0}: (10, {})} | custom-call | tf_op jit(solution)/shard_map/attention_back_queries/pallas_call | solution.py:510
  246.0 0.9 add_convert_fusion.1
  246.9 0.1 reshape_squeeze.38
  247.0 0.1 reshape_squeeze.39
  247.1 0.1 reshape_squeeze.40
  247.2 0.1 reshape_squeeze.41
  247.6 0.1 concatenate.15
  247.8 0.7 copy.70
  248.5 2.3 convolution_convert_fusion.4
  250.8 0.9 stack_reshape.22
  251.6 4.5 convolution_convert_fusion.3
  256.1 7.9 %convolution_convert_fusion = bf16[768,2304]{1,0:T(8,128)(2,1)S(1)} fusion(bf16[1280,2304]{1,0:T(8,128)(2,1)} %get-tuple-element.120, bf16[256,768]{1,0:T(8,128)(2,1)S(1)} %bitcast.71, bf16[1024,768]{1,0:T(8,128)(2,1)S(1)} %bitcast.62), kind=kOutput, calls=%fused_computation.1 | convolution fusion | flops 4535549952 | bytes 11403264 | tf_op jit(solution)/shard_map/dot_general | solution.py:918
  264.0 0.2 fusion.7
  264.3 1.3 copy-done.4
  265.6 8.0 %convolution_convert_fusion.2 = bf16[768,3072]{1,0:T(8,128)(2,1)} fusion(bf16[1280,768]{1,0:T(8,128)(2,1)S(1)} %copy-done.4, bf16[1280,3072]{1,0:T(8,128)(2,1)S(1)} %bitcast.55), kind=kOutput, calls=%fused_computation.3 | convolution fusion | flops 6042157056 | bytes 14548992 | tf_op jit(solution)/shard_map/dot_general | solution.py:918
  273.6 9.8 %reshape.101 = bf16[8,96,4,768]{3,2,1,0:T(4,128)(2,1)} reshape(bf16[768,3072]{1,0:T(8,128)(2,1)} %convolution_convert_fusion.2) | data formatting | bytes 9437184 | tf_op jit(solution)/shard_map/reshape | solution.py:1051
  283.4 3.3 copy.68
  286.7 9.1 %convolution_convert_fusion.1 = bf16[3072,768]{1,0:T(8,128)(2,1)S(1)} fusion(bf16[1280,3072]{1,0:T(8,128)(2,1)} %get-tuple-element.116, bf16[1280,768]{1,0:T(8,128)(2,1)S(1)} %copy-done.5), kind=kOutput, calls=%fused_computation.2 | convolution fusion | flops 6042157056 | bytes 14548992 | tf_op jit(solution)/shard_map/dot_general | solution.py:918
  295.8 0.4 copy.69
  296.2 0.9 copy-done.7
  297.1 14.8 %maximum_maximum_fusion = bf16[4,8,304,768]{3,2,1,0:T(8,128)(2,1)} fusion(bf16[1,8,16,768]{3,2,1,0:T(8,128)(2,1)S(1)} %copy-done.8, bf16[1,8,16,768]{3,2,1,0:T(8,128)(2,1)S(1)} %copy-done.9, bf16[1,8,96,768]{3,2,1,0:T(8,128)(2,1)S(1)} %bitcast.63, bf16[1,8,96,768]{3,2,1,0:T(8,128)(2,1)S(1)} %bitcast.57, bf16[1,8,96,768]{3,2,1,0:T(8,128)(2,1)S(1)} %bitcast.58, ...), kind=kLoop, calls=%fused_computation | loop fusion | flops 134479872 | bytes 29493632 | tf_op jit(solution)/shard_map/concatenate | solution.py:1048
  311.9 120.1 %sum_weight_gradients.1 = bf16[4,304,768]{2,1,0:T(8,128)(2,1)} custom-call(bf16[2,2,4,2,304,768]{5,4,3,2,1,0:T(8,128)(2,1)} %bitcast.51), custom_call_target="tpu_custom_call" | custom-call | tf_op jit(solution)/shard_map/sum_weight_gradients/pallas_call | solution.py:892
  432.0 1.9 convert_element_type.37
  434.0 0.1 copy-done.3
  434.1 1.0 slice_bitcast_fusion.1
  435.1 0.1 slice_bitcast_fusion
  435.3 0.6 fusion.8
  435.9 0.6 slice.151
  436.4 1.1 slice.152
  437.5 0.8 dynamic-slice_bitcast_fusion
  438.3 0.6 copy.61
  438.9 0.6 constant_dynamic-slice_fusion
  439.6 1.1 copy.63
  440.7 0.6 reshape_squeeze.47
  (56 shorter events, 0.9 us)
Async XLA Ops:
  7.2 8.3 %copy-start = (s32[2,32]{1,0:T(2,128)S(1)}, s32[2,32]{1,0:T(2,128)}, u32[]{:S(2)}) copy-start(s32[2,32]{1,0:T(2,128)} %param.22) | copy-start | bytes 772
  7.2 87.0 %all-gather.2.cloned.1.call-start = ((), (), s32[]{:S(2)}) async-start(), calls=%async_computation | async-start | bytes 2162688 | tf_op jit(solution)/shard_map/all_gather | solution.py:988
  35.1 80.9 %copy-start.15 = (s32[2,128]{1,0:T(2,128)S(1)}, s32[2,128]{1,0:T(2,128)}, u32[]{:S(2)}) copy-start(s32[2,128]{1,0:T(2,128)} %param.23) | copy-start | bytes 3076
  184.3 11.0 %copy-start.13 = (f32[16,768]{1,0:T(8,128)S(1)}, f32[16,768]{1,0:T(8,128)}, u32[]{:S(2)}) copy-start(f32[16,768]{1,0:T(8,128)} %get-tuple-element.126) | copy-start | bytes 147460
  196.2 38.1 %copy-start.12 = (bf16[16,768]{1,0:T(8,128)(2,1)}, bf16[16,768]{1,0:T(8,128)(2,1)S(1)}, u32[]{:S(2)}) copy-start(bf16[16,768]{1,0:T(8,128)(2,1)S(1)} %add_convert_fusion) | copy-start | bytes 73732
  234.3 11.7 %copy-start.14 = (f32[8,768]{1,0:T(8,128)S(1)}, f32[8,768]{1,0:T(8,128)}, u32[]{:S(2)}) copy-start(f32[8,768]{1,0:T(8,128)} %get-tuple-element.124) | copy-start | bytes 73732
  234.3 13.3 %slice-start.2 = ((bf16[16,768]{1,0:T(8,128)(2,1)}), bf16[4,768]{1,0:T(4,128)(2,1)S(1)}, s32[]{:S(2)}) async-start(bf16[16,768]{1,0:T(8,128)(2,1)} %copy-done.12), calls=%async_computation.3 | async-start | bytes 12288 | tf_op jit(solution)/shard_map/slice | solution.py:1039
  234.3 14.2 %copy-start.11 = (bf16[1280,128]{1,0:T(8,128)(2,1)S(1)}, bf16[1280,128]{1,0:T(8,128)(2,1)}, u32[]{:S(2)}) copy-start(bf16[1280,128]{1,0:T(8,128)(2,1)} %get-tuple-element.123) | copy-start | bytes 983044
  246.0 5.6 %copy-start.2 = (bf16[1280,768]{1,0:T(8,128)(2,1)S(1)}, bf16[1280,768]{1,0:T(8,128)(2,1)}, u32[]{:S(2)}) copy-start(bf16[1280,768]{1,0:T(8,128)(2,1)} %get-tuple-element.102.refs_0_) | copy-start | bytes 5898244
  251.6 4.5 %copy-start.6 = (bf16[2,1,512,768]{3,2,1,0:T(8,128)(2,1)S(1)}, bf16[2,1,512,768]{3,2,1,0:T(8,128)(2,1)}, u32[]{:S(2)}) copy-start(bf16[2,1,512,768]{3,2,1,0:T(8,128)(2,1)} %param.21) | copy-start | bytes 4718596
  251.6 4.5 %copy-start.10 = (bf16[2,4,32,768]{3,2,1,0:T(8,128)(2,1)S(1)}, bf16[2,4,32,768]{3,2,1,0:T(8,128)(2,1)}, u32[]{:S(2)}) copy-start(bf16[2,4,32,768]{3,2,1,0:T(8,128)(2,1)} %param.20) | copy-start | bytes 1179652
  251.6 12.6 %slice-start = ((s8[7864320]{0:T(1024)(128)(4,1)}), s8[4194304]{0:T(1024)(128)(4,1)S(1)}, s32[]{:S(2)}) async-start(s8[7864320]{0:T(1024)(128)(4,1)} %bitcast.54), calls=%async_computation.1 | async-start | bytes 8388608
  256.1 8.2 %slice-start.1 = ((s8[7864320]{0:T(1024)(128)(4,1)}), s8[3670016]{0:T(1024)(128)(4,1)S(1)}, s32[]{:S(2)}) async-start(s8[7864320]{0:T(1024)(128)(4,1)} %bitcast.54), calls=%async_computation.2 | async-start | bytes 7340032
  264.0 1.5 copy-start.4
  283.4 3.3 copy-start.5
  295.8 1.3 copy-start.7
  295.8 1.3 copy-start.8
  295.8 1.3 copy-start.9
  432.0 2.1 copy-start.3
  434.1 7.2 %copy-start.1 = (s32[2,32]{1,0:T(2,128)S(1)}, s32[2,32]{1,0:T(2,128)}, u32[]{:S(2)}) copy-start(s32[2,32]{1,0:T(2,128)} %param.22) | copy-start | bytes 772
Sparse Core Ops, SparseCore 0:
  35.2 58.9 all-gather.1

commit v2 on v1

--- a/solution.py
+++ b/solution.py
@@ -62,10 +62,157 @@
                 self.copies[index].wait()
 
 
-def fwd_kernel(grouped, alias_count, *refs):
+MESH = pl.DeviceIdType.MESH
+
+
+def remote(source, target, sems, index, device):
+    return pltpu.make_async_remote_copy(
+        src_ref=source,
+        dst_ref=target,
+        send_sem=sems[0].at[index],
+        recv_sem=sems[1].at[index],
+        device_id=device,
+        device_id_type=MESH,
+    )
+
+
+class Chips:
+    def __init__(self, n_wide, n_narrow):
+        self.wide, self.narrow = lax.axis_index("wide"), lax.axis_index("narrow")
+        self.core = lax.rem(self.narrow, 2)
+        self.rows = n_narrow // 2
+        self.count = n_wide * self.rows
+        self.me = self.wide * self.rows + self.narrow // 2
+        self.mate = (self.wide, self.narrow + 1 - 2 * self.core)
+
+    def at(self, step):
+        return lax.rem(self.me + step + self.count, self.count)
+
+    def device(self, chip):
+        return (chip // self.rows, lax.rem(chip, self.rows) * 2 + self.core)
+
+    def loop(self, body):
+        def step_body(step, carry):
+            body(step)
+            return carry
+
+        lax.fori_loop(1, self.count, step_body, 0)
+
+    def barrier(self):
+        barrier = pltpu.get_barrier_semaphore()
+
+        def signal(step):
+            pl.semaphore_signal(
+                barrier, inc=1, device_id=self.device(self.at(step)), device_id_type=MESH
+            )
+
+        pl.semaphore_signal(barrier, inc=1, device_id=self.mate, device_id_type=MESH)
+        self.loop(signal)
+        pl.semaphore_wait(barrier, self.count)
+
+
+class Gather:
+    def __init__(self, chips, own, out, sems):
+        self.chips, self.own, self.out = chips, own, out
+        self.far, self.pair, self.local = sems[:2], sems[2:4], sems[4]
+
+    def far_copy(self, step, chip):
+        slot = self.out.at[chip, self.chips.core]
+        return remote(self.own, slot, self.far, step, self.chips.device(self.chips.at(step)))
+
+    def mate_copy(self, core):
+        block = self.out.at[:, core]
+        return remote(block, block, self.pair, 0, self.chips.mate)
+
+    def local_copy(self):
+        slot = self.out.at[self.chips.me, self.chips.core]
+        return pltpu.make_async_copy(self.own, slot, self.local.at[0])
+
+    def start(self):
+        self.local_copy().start()
+        self.chips.barrier()
+        self.chips.loop(lambda step: self.far_copy(step, self.chips.me).start())
+
+    def forward(self):
+        self.local_copy().wait()
+        self.chips.loop(lambda step: self.far_copy(step, self.chips.at(-step)).wait_recv())
+        self.mate_copy(self.chips.core).start()
+
+    def finish(self):
+        self.chips.loop(lambda step: self.far_copy(step, self.chips.me).wait_send())
+        self.mate_copy(1 - self.chips.core).wait_recv()
+        self.mate_copy(self.chips.core).wait_send()
+
+
+class Exchange:
+    def __init__(self, chips, grads, out, scratch):
+        self.chips, self.grads, self.out = chips, grads, out
+        self.half, self.arrived, self.inbox = scratch[:3]
+        self.pair, self.far, self.local = scratch[3:5], scratch[5:7], scratch[7]
+
+    def pair_copy(self):
+        away = self.grads.at[:, 1 - self.chips.core]
+        return remote(away, self.arrived, self.pair, 0, self.chips.mate)
+
+    def local_copy(self):
+        mine = self.grads.at[:, self.chips.core]
+        return pltpu.make_async_copy(mine, self.half, self.local.at[0])
+
+    def far_copy(self, step):
+        chip = self.chips.at(step)
+        return remote(
+            self.half.at[chip], self.inbox.at[step], self.far, step, self.chips.device(chip)
+        )
+
+    def start(self):
+        self.local_copy().start()
+        self.chips.barrier()
+        self.pair_copy().start()
+
+    def push(self):
+        self.local_copy().wait()
+        self.pair_copy().wait_recv()
+
+        def add(step):
+            chip = self.chips.at(step)
+            total = self.half[chip].astype(F32) + self.arrived[chip].astype(F32)
+            self.half[chip] = total.astype(BF16)
+            self.far_copy(step).start()
+
+        self.chips.loop(add)
+        me = self.chips.me
+        self.out[...] = self.half[me].astype(F32) + self.arrived[me].astype(F32)
+
+    def finish(self):
+        def collect(step):
+            copy = self.far_copy(step)
+            copy.wait_recv()
+            copy.wait_send()
+            self.out[...] += self.inbox[step].astype(F32)
+
+        self.chips.loop(collect)
+        self.pair_copy().wait_send()
+
+
+def exchange_scratch(chips, rows, width):
+    sem = pltpu.SemaphoreType.DMA
+    return [pltpu.VMEM((chips, rows, width), BF16)] * 3 + [
+        sem((1,)),
+        sem((1,)),
+        sem((chips,)),
+        sem((chips,)),
+        sem((1,)),
+    ]
+
+
+def fwd_kernel(grouped, alias_count, sizes, *refs):
     lens_ref, x_ref, vec_ref = refs[:3]
     sources = refs[3:10]
     refs = refs[10 + alias_count :]
+    gather = None
+    if sizes:
+        gather = Gather(Chips(*sizes), refs[0], refs[17], refs[-5:])
+        refs = refs[1:17] + refs[18:-5]
     (
         q_ref,
         k_ref,
@@ -87,6 +234,10 @@
     wq, wk, wv, wo, wi, w2, wl, sem, acc_ref = refs[16:]
     loader = Loader(sources, (wq, wk, wv, wo, wi, w2, wl), sem)
     loader.start()
+    if gather:
+        last = pl.program_id(0) == pl.num_programs(0) - 1
+        pl.when(loader.first)(gather.start)
+        pl.when(last)(gather.forward)
     rows = x_ref.shape[0]
     x = x_ref[...]
     scale = HEAD_DIM ** (-0.5)
@@ -165,9 +316,11 @@
     unit_ref[...] = unit
     uinv_ref[...] = jnp.broadcast_to(uinv, uinv_ref.shape)
     embed_ref[...] = unit.astype(BF16)
-
-
-def encode(x, lens, vec, weights, blocks, grouped, total, offset, earlier):
+    if gather:
+        pl.when(last)(gather.finish)
+
+
+def encode(x, lens, vec, weights, blocks, grouped, total, offset, earlier, sizes):
     rows = x.shape[0] // blocks
     width = x.shape[1]
     wide = weights[4].shape[1]
@@ -210,8 +363,17 @@
         for index, out in enumerate(out_shapes)
     ]
     aliased = [] if earlier is None else [earlier[index] for index in shared]
+    sends, sem_shapes, params = [], [], {}
+    if sizes:
+        sends = [earlier[15]]
+        chips = sizes[0] * sizes[1] // 2
+        out_shapes.append(jax.ShapeDtypeStruct((chips, 2) + earlier[15].shape, BF16))
+        out_specs.append(ANY)
+        sem = pltpu.SemaphoreType.DMA
+        sem_shapes = [sem((chips,)), sem((chips,)), sem((1,)), sem((1,)), sem((1,))]
+        params = {"collective_id": 4, "has_side_effects": True}
     return pl.pallas_call(
-        functools.partial(fwd_kernel, grouped, len(aliased)),
+        functools.partial(fwd_kernel, grouped, len(aliased), sizes),
         out_shape=out_shapes,
         grid_spec=pltpu.PrefetchScalarGridSpec(
             num_scalar_prefetch=1,
@@ -220,15 +382,16 @@
                 own_spec(width),
                 pl.BlockSpec(vec.shape, lambda i, lens: (0, 0)),
             ]
-            + [ANY] * (7 + len(aliased)),
+            + [ANY] * (7 + len(aliased) + len(sends)),
             out_specs=out_specs,
             scratch_shapes=[pltpu.VMEM(weight.shape, BF16) for weight in weights]
-            + [pltpu.SemaphoreType.DMA((7,)), pltpu.VMEM((rows, width), F32)],
+            + [pltpu.SemaphoreType.DMA((7,)), pltpu.VMEM((rows, width), F32)]
+            + sem_shapes,
         ),
         input_output_aliases={10 + index: shared[index] for index in range(len(aliased))},
-        compiler_params=pltpu.CompilerParams(vmem_limit_bytes=VMEM_LIMIT),
+        compiler_params=pltpu.CompilerParams(vmem_limit_bytes=VMEM_LIMIT, **params),
         name="encode_queries" if grouped else "encode_passages",
-    )(lens, x, vec, *weights, *aliased)
+    )(lens, x, vec, *weights, *aliased, *sends)
 
 
 def sims_kernel(lens_ref, q_ref, p_ref, e_ref, z_ref):
@@ -322,7 +485,7 @@
     ref[row : row + 1, :] += jnp.sum(value, axis=0, keepdims=True)
 
 
-def mlp_back_kernel(alias_count, *refs):
+def mlp_back_kernel(alias_count, sizes, *refs):
     (
         ge_ref,
         unit_ref,
@@ -336,10 +499,16 @@
     ) = refs[:9]
     sources = refs[9:12]
     refs = refs[12 + alias_count :]
+    swap = None
+    if sizes:
+        swap = Exchange(Chips(*sizes), refs[0], refs[7], refs[-8:])
+        refs = refs[1:7] + refs[8:-8]
     gp_ref, go_ref, gi_ref, gh_ref, ga_ref, sums_ref = refs[:6]
     wl, w2, wi, sem, acc_ref = refs[6:]
     loader = Loader(sources, (wl, w2, wi), sem)
     loader.start()
+    if swap:
+        pl.when(loader.first)(swap.start)
 
     @pl.when(loader.first)
     def _():
@@ -362,6 +531,8 @@
     go_ref[...] = outer_low
     accumulate(sums_ref, ROW_B2, outer_low.astype(F32))
     acc_ref[...] = grad_second
+    if swap:
+        pl.when(loader.first)(swap.push)
     loader.need(1, 2)
     width = go_ref.shape[1]
 
@@ -387,9 +558,11 @@
     low = hidden.astype(BF16)
     ga_ref[...] = low
     accumulate(sums_ref, ROW_BO, low.astype(F32))
-
-
-def mlp_back(grad_embed, kept, vec, weights, blocks, total, offset, earlier):
+    if swap:
+        pl.when(pl.program_id(0) == pl.num_programs(0) - 1)(swap.finish)
+
+
+def mlp_back(grad_embed, kept, vec, weights, blocks, total, offset, earlier, sent, sizes):
     own = grad_embed.shape[0]
     rows = own // blocks
     base = offset // rows
@@ -418,20 +591,28 @@
         for index, out in enumerate(out_shapes[:5])
     ] + [pl.BlockSpec((16, width), lambda i: (0, 0))]
     aliased = [] if earlier is None else [earlier[index] for index in shared]
+    sends, scratch, params = [], [], {}
+    if sizes:
+        sends = [sent]
+        out_shapes.append(jax.ShapeDtypeStruct(sent.shape[2:], F32))
+        out_specs.append(pl.BlockSpec(sent.shape[2:], lambda i: (0, 0)))
+        scratch = exchange_scratch(sent.shape[0], *sent.shape[2:])
+        params = {"collective_id": 2, "has_side_effects": True}
     return pl.pallas_call(
-        functools.partial(mlp_back_kernel, len(aliased)),
+        functools.partial(mlp_back_kernel, len(aliased), sizes),
         out_shape=out_shapes,
         grid=(blocks,),
         in_specs=[own_spec(arg.shape[1]) for arg in args]
         + [pl.BlockSpec(vec.shape, lambda i: (0, 0))]
-        + [ANY] * (3 + len(aliased)),
+        + [ANY] * (3 + len(aliased) + len(sends)),
         out_specs=out_specs,
         scratch_shapes=[pltpu.VMEM(weight.shape, BF16) for weight in (wl, w2, wi)]
-        + [pltpu.SemaphoreType.DMA((3,)), pltpu.VMEM((rows, width), F32)],
+        + [pltpu.SemaphoreType.DMA((3,)), pltpu.VMEM((rows, width), F32)]
+        + scratch,
         input_output_aliases={12 + index: shared[index] for index in range(len(aliased))},
-        compiler_params=pltpu.CompilerParams(vmem_limit_bytes=VMEM_LIMIT),
+        compiler_params=pltpu.CompilerParams(vmem_limit_bytes=VMEM_LIMIT, **params),
         name="mlp_back_queries" if earlier is not None else "mlp_back_passages",
-    )(*args, vec, wl, w2, wi, *aliased)
+    )(*args, vec, wl, w2, wi, *aliased, *sends)
 
 
 def attention_back_kernel(alias_count, *refs):
@@ -537,20 +718,6 @@
     )(attended, hidden, kept[3], kept[0], kept[1], kept[2], wo, wq, wk, wv, *aliased)
 
 
-MESH = pl.DeviceIdType.MESH
-
-
-def remote(source, target, sems, index, device):
-    return pltpu.make_async_remote_copy(
-        src_ref=source,
-        dst_ref=target,
-        send_sem=sems[0].at[index],
-        recv_sem=sems[1].at[index],
-        device_id=device,
-        device_id_type=MESH,
-    )
-
-
 def share_kernel(n_wide, n_narrow, own_ref, all_ref, send_sem, recv_sem):
     me = lax.axis_index("narrow") * n_wide + lax.axis_index("wide")
     total = n_wide * n_narrow
@@ -599,84 +766,42 @@
     )(own)
 
 
-def exchange_kernel(n_wide, n_narrow, g_ref, out_ref, half, arrived, inbox, *sems):
-    pair_sems, far_sems = sems[:2], sems[2:]
-    wide, narrow = lax.axis_index("wide"), lax.axis_index("narrow")
-    core = lax.rem(narrow, 2)
-    partner = (wide, narrow + 1 - 2 * core)
-    rows = n_narrow // 2
-    chips = n_wide * rows
-    me = wide * rows + narrow // 2
-
-    def device(chip):
-        return (chip // rows, lax.rem(chip, rows) * 2 + core)
-
-    barrier = pltpu.get_barrier_semaphore()
-
-    def signal(step, carry):
-        pl.semaphore_signal(
-            barrier, inc=1, device_id=device(lax.rem(me + step, chips)), device_id_type=MESH
-        )
-        return carry
-
-    pl.semaphore_signal(barrier, inc=1, device_id=partner, device_id_type=MESH)
-    lax.fori_loop(1, chips, signal, 0)
-    pl.semaphore_wait(barrier, chips)
-    pair = remote(g_ref.at[:, 1 - core], arrived, pair_sems, 0, partner)
-    pair.start()
-    pair.wait_recv()
-
-    def add(step, carry):
-        chip = lax.rem(me + step, chips)
-        total = g_ref[chip, core].astype(F32) + arrived[chip].astype(F32)
-        half[chip] = total.astype(BF16)
-        remote(half.at[chip], inbox.at[step], far_sems, step, device(chip)).start()
-        return carry
-
-    lax.fori_loop(1, chips, add, 0)
-    out_ref[...] = g_ref[me, core].astype(F32) + arrived[me].astype(F32)
-
-    def collect(step, carry):
-        chip = lax.rem(me - step + chips, chips)
-        copy = remote(half.at[chip], inbox.at[step], far_sems, step, device(chip))
-        copy.wait_recv()
-        copy.wait_send()
-        out_ref[...] += inbox[step].astype(F32)
-        return carry
-
-    lax.fori_loop(1, chips, collect, 0)
-    pair.wait_send()
+def exchange_kernel(n_wide, n_narrow, g_ref, out_ref, *scratch):
+    swap = Exchange(Chips(n_wide, n_narrow), g_ref, out_ref, scratch)
+    swap.start()
+    swap.push()
+    swap.finish()
 
 
 def exchange(grads, n_wide, n_narrow):
-    rows, width = grads.shape[1:]
-    chips = n_wide * n_narrow // 2
-    block = pltpu.VMEM((chips, rows, width), BF16)
+    chips, _, rows, width = grads.shape
     return pl.pallas_call(
         functools.partial(exchange_kernel, n_wide, n_narrow),
         out_shape=jax.ShapeDtypeStruct((rows, width), F32),
-        in_specs=[pl.BlockSpec(memory_space=pltpu.VMEM)],
+        in_specs=[ANY],
         out_specs=pl.BlockSpec(memory_space=pltpu.VMEM),
-        scratch_shapes=[block, block, block]
-        + [pltpu.SemaphoreType.DMA((1,))] * 2
-        + [pltpu.SemaphoreType.DMA((chips,))] * 2,
+        scratch_shapes=exchange_scratch(chips, rows, width),
         compiler_params=pltpu.CompilerParams(
             collective_id=2, has_side_effects=True, vmem_limit_bytes=VMEM_LIMIT
         ),
         name="exchange_query_gradients",
-    )(grads.reshape(chips, 2, rows, width))
-
-
-UNITS = ((0, 80), (160, 80), (80, 80), (240, 64))
+    )(grads)
+
+
+UNITS = ((0, 48), (48, 48), (96, 48), (144, 48), (192, 48), (240, 64))
 SHARE_ROWS = 304
-
-
-def tree_kernel(
-    n_z, g_ref, out_ref, held, near, over_a, over_b, then_a, then_b, line, *sems
-):
-    (local_sem,) = sems[:1]
+HALF = 64
+TILES = 12
+
+
+def weights_kernel(n_z, part, *refs):
+    act, go, first, gi, x_p, x_q, gqkv, ctx, ga, final, gp = refs[:11]
+    sums = refs[11:15]
+    out_ref = refs[15]
+    both, near, over_a, over_b, then_a, then_b, line, left_buf, right_buf, thin_buf = refs[16:26]
+    load_sem = refs[26]
     core_sems, one_sems, two_sems, line_sems, copy_sems = (
-        sems[1 + 2 * index : 3 + 2 * index] for index in range(5)
+        refs[27 + 2 * index : 29 + 2 * index] for index in range(5)
     )
     wide, narrow = lax.axis_index("wide"), lax.axis_index("narrow")
     z, x = wide // 2, lax.rem(wide, 2)
@@ -685,20 +810,41 @@
     over_y = (wide, (1 - y) * 2 + core)
     over_x = (z * 2 + 1 - x, narrow)
     right, left = (wide + 2, narrow), (wide - 2, narrow)
-    barrier = pltpu.get_barrier_semaphore()
-    for device in (mate, over_y, over_x):
-        pl.semaphore_signal(barrier, inc=1, device_id=device, device_id_type=MESH)
-
-    @pl.when(z < n_z - 1)
-    def _():
-        pl.semaphore_signal(barrier, inc=1, device_id=right, device_id_type=MESH)
-
-    @pl.when(z > 0)
-    def _():
-        pl.semaphore_signal(barrier, inc=1, device_id=left, device_id_type=MESH)
-
-    inside = jnp.logical_and(z > 0, z < n_z - 1)
-    pl.semaphore_wait(barrier, jnp.where(inside, 5, 4))
+    width = go.shape[1]
+    p_rows = x_p.shape[0]
+    count_units = len(UNITS)
+    held = both.at[core]
+
+    def load(tile, wait):
+        slot = lax.rem(tile, 2)
+        block = pl.ds(pl.multiple_of(lax.rem(tile, 4) * width, width), width)
+
+        def copy(source, target, sem):
+            made = pltpu.make_async_copy(source, target, sem)
+            if wait:
+                made.wait()
+            else:
+                made.start()
+
+        def pair(source, other):
+            copy(source, left_buf.at[slot], load_sem.at[slot, 0])
+            copy(other, right_buf.at[slot], load_sem.at[slot, 1])
+
+        pl.when(tile < 4)(lambda: pair(act.at[:, block], go))
+        pl.when(jnp.logical_and(tile >= 4, tile < 8))(lambda: pair(first, gi.at[:, block]))
+
+        @pl.when(jnp.logical_and(tile >= 8, tile < 11))
+        def _():
+            copy(x_p, left_buf.at[slot, pl.ds(0, p_rows)], load_sem.at[slot, 0])
+            copy(x_q, left_buf.at[slot, pl.ds(p_rows, x_q.shape[0])], load_sem.at[slot, 2])
+            copy(gqkv.at[:, block], right_buf.at[slot], load_sem.at[slot, 1])
+
+        pl.when(tile == 11)(lambda: pair(ctx, ga))
+
+        @pl.when(tile == TILES)
+        def _():
+            copy(final, left_buf.at[slot], load_sem.at[slot, 0])
+            copy(gp, thin_buf, load_sem.at[slot, 1])
 
     def rows_of(unit):
         start, count = UNITS[unit]
@@ -707,13 +853,7 @@
     def core_copy(unit):
         rows = rows_of(unit)
         return remote(
-            g_ref.at[:, 1 - core, :, :, rows], near.at[:, :, :, rows], core_sems, unit, mate
-        )
-
-    def local_copy(unit):
-        rows = rows_of(unit)
-        return pltpu.make_async_copy(
-            g_ref.at[:, core, :, :, rows], held.at[:, :, :, rows], local_sem.at[unit]
+            both.at[1 - core, :, :, :, rows], near.at[:, :, :, rows], core_sems, unit, mate
         )
 
     def one_copy(unit):
@@ -755,56 +895,65 @@
             right if way == 0 else left,
         )
 
+    def share_copy(unit, step, arriving):
+        rows = rows_of(unit)
+        slots = (
+            (y * 2 + 1 - core, (1 - y) * 2 + core, (1 - y) * 2 + 1 - core)
+            if arriving
+            else (narrow, narrow, (1 - y) * 2 + core)
+        )
+        block = out_ref.at[slots[step], rows]
+        return remote(block, block, copy_sems, unit * 3 + step, over_y if step == 1 else mate)
+
     def add(target, extra):
         target[...] = (target[...].astype(F32) + extra[...].astype(F32)).astype(BF16)
 
-    count_units = len(UNITS)
-    for unit in range(count_units):
+    def start_core(unit):
         core_copy(unit).start()
-        local_copy(unit).start()
-    for unit in range(count_units):
+
+    def start_one(unit):
         rows = rows_of(unit)
-        local_copy(unit).wait()
         core_copy(unit).wait_recv()
 
-        def add_near(index, carry, rows=rows):
+        def body(index, carry):
             row_y, rest = index // (n_z * 2), lax.rem(index, n_z * 2)
             at = (row_y, rest // 2, lax.rem(rest, 2), rows)
             add(held.at[at], near.at[at])
             return carry
 
-        lax.fori_loop(0, 4 * n_z, add_near, 0)
+        lax.fori_loop(0, 4 * n_z, body, 0)
         one_copy(unit).start()
-    for unit in range(count_units):
+
+    def start_two(unit):
         rows = rows_of(unit)
         count = UNITS[unit][1]
-        copy = one_copy(unit)
-        copy.wait_recv()
-
-        def add_one(index, carry, rows=rows, unit=unit, count=count):
-            first, second = index // 2, lax.rem(index, 2)
+        one_copy(unit).wait_recv()
+
+        def body(index, carry):
+            outer_at, inner_at = index // 2, lax.rem(index, 2)
             if unit % 2 == 0:
-                add(held.at[y, first, second, rows], over_a.at[unit // 2, first, second])
+                add(held.at[y, outer_at, inner_at, rows], over_a.at[unit // 2, outer_at, inner_at])
             else:
                 add(
-                    held.at[second, first, x, rows],
-                    over_b.at[unit // 2, second, first, pl.ds(0, count)],
+                    held.at[inner_at, outer_at, x, rows],
+                    over_b.at[unit // 2, inner_at, outer_at, pl.ds(0, count)],
                 )
             return carry
 
-        lax.fori_loop(0, 2 * n_z, add_one, 0)
+        lax.fori_loop(0, 2 * n_z, body, 0)
         two_copy(unit).start()
-    for unit in range(count_units):
+
+    def start_line(unit):
         rows = rows_of(unit)
         count = UNITS[unit][1]
         two_copy(unit).wait_recv()
 
-        def add_two(index, carry, rows=rows, unit=unit, count=count):
+        def body(index, carry):
             extra = then_a if unit % 2 == 0 else then_b
             add(held.at[y, index, x, rows], extra.at[unit // 2, index, pl.ds(0, count)])
             return carry
 
-        lax.fori_loop(0, n_z, add_two, 0)
+        lax.fori_loop(0, n_z, body, 0)
         for step in range(n_z - 1):
             for way in range(2):
                 target = n_z - 1 - step if way == 0 else step
@@ -812,97 +961,161 @@
                 edge = z > 0 if way == 0 else z < n_z - 1
 
                 @pl.when(jnp.logical_and(sends, edge))
-                def _(unit=unit, target=target, way=way, rows=rows):
+                def _(target=target, way=way):
                     line_copy(unit, target, way).wait_recv()
                     add(held.at[y, target, x, rows], line.at[way, target, rows])
 
-                @pl.when(sends)
-                def _(unit=unit, target=target, way=way):
-                    line_copy(unit, target, way).start()
-
-    def own_copy(unit, step):
-        rows = rows_of(unit)
-        index = unit * 3 + step
-        slot = narrow if step < 2 else (1 - y) * 2 + core
-        return remote(
-            out_ref.at[slot, rows],
-            out_ref.at[slot, rows],
-            copy_sems,
-            index,
-            over_y if step == 1 else mate,
-        )
-
-    def arrived_copy(unit, step):
-        rows = rows_of(unit)
-        index = unit * 3 + step
-        slot = (
-            y * 2 + 1 - core,
-            (1 - y) * 2 + core,
-            (1 - y) * 2 + 1 - core,
-        )[step]
-        return remote(
-            out_ref.at[slot, rows],
-            out_ref.at[slot, rows],
-            copy_sems,
-            index,
-            over_y if step == 1 else mate,
-        )
-
-    for unit in range(count_units):
+                pl.when(sends)(line_copy(unit, target, way).start)
+
+    def start_share(unit):
         rows = rows_of(unit)
         for target in range(n_z):
 
             @pl.when(z == target)
-            def _(unit=unit, target=target, rows=rows):
-                if target > 0:
-                    line_copy(unit, target, 0).wait_recv()
-                    add(held.at[y, target, x, rows], line.at[0, target, rows])
-                if target < n_z - 1:
-                    line_copy(unit, target, 1).wait_recv()
-                    add(held.at[y, target, x, rows], line.at[1, target, rows])
-
-        out_ref[narrow, rows] = held[y, z, x, rows]
-        own_copy(unit, 1).start()
-        own_copy(unit, 0).start()
-    for unit in range(count_units):
-        arrived_copy(unit, 1).wait_recv()
-        own_copy(unit, 2).start()
-    for unit in range(count_units):
-        arrived_copy(unit, 0).wait_recv()
-        arrived_copy(unit, 2).wait_recv()
+            def _(target=target):
+                for way in range(2):
+                    if target > 0 if way == 0 else target < n_z - 1:
+                        line_copy(unit, target, way).wait_recv()
+                        add(held.at[y, target, x, rows], line.at[way, target, rows])
+
+        out_ref[narrow, rows] = both[core, y, z, x, rows]
+        share_copy(unit, 1, False).start()
+        share_copy(unit, 0, False).start()
+
+    def forward(unit):
+        share_copy(unit, 1, True).wait_recv()
+        share_copy(unit, 2, False).start()
+
+    def finish(unit):
+        share_copy(unit, 0, True).wait_recv()
+        share_copy(unit, 2, True).wait_recv()
         for step in range(3):
-            own_copy(unit, step).wait_send()
+            share_copy(unit, step, False).wait_send()
         core_copy(unit).wait_send()
         one_copy(unit).wait_send()
         two_copy(unit).wait_send()
         for target in range(n_z):
             for way in range(2):
-
-                @pl.when(z < target if way == 0 else z > target)
-                def _(unit=unit, target=target, way=way):
-                    line_copy(unit, target, way).wait_send()
-
-
-def tree(grads, n_wide):
+                pl.when(z < target if way == 0 else z > target)(
+                    line_copy(unit, target, way).wait_send
+                )
+
+    barrier = pltpu.get_barrier_semaphore()
+    load(0, False)
+    for device in (mate, over_y, over_x):
+        pl.semaphore_signal(barrier, inc=1, device_id=device, device_id_type=MESH)
+
+    @pl.when(z < n_z - 1)
+    def _():
+        pl.semaphore_signal(barrier, inc=1, device_id=right, device_id_type=MESH)
+
+    @pl.when(z > 0)
+    def _():
+        pl.semaphore_signal(barrier, inc=1, device_id=left, device_id_type=MESH)
+
+    pl.semaphore_wait(barrier, jnp.where(jnp.logical_and(z > 0, z < n_z - 1), 5, 4))
+
+    def tile_body(tile, carry):
+        slot = lax.rem(tile, 2)
+        load(tile, True)
+        load(tile + 1, False)
+        kind, owner = tile // 4, lax.rem(tile, 4)
+
+        def half_body(half, carry):
+            cols = pl.ds(pl.multiple_of(half * 4 * part, 4 * part), 4 * part)
+            made = mm(left_buf[slot, :, cols], right_buf[slot], TN).astype(BF16)
+
+            @pl.when(kind == 0)
+            def _():
+                for index in range(4):
+                    both[index % 2, index // 2, owner, half, :part] = made[
+                        index * part : (index + 1) * part
+                    ]
+
+            @pl.when(kind > 0)
+            def _():
+                rows = pl.ds(pl.multiple_of(kind * part, part), part)
+                for index in range(4):
+                    both[lax.rem(owner, 2), owner // 2, 2 * half + index // 2, index % 2, rows] = (
+                        made[index * part : (index + 1) * part]
+                    )
+
+            return carry
+
+        lax.fori_loop(0, 2, half_body, 0)
+        for when_tile, step, units in (
+            (3, start_core, (0, 1)),
+            (6, start_one, (0, 1)),
+            (7, start_core, (2, 3)),
+            (10, start_one, (2, 3)),
+        ):
+
+            @pl.when(tile == when_tile)
+            def _(step=step, units=units):
+                for unit in units:
+                    step(unit)
+
+        return carry
+
+    lax.fori_loop(0, TILES, tile_body, 0)
+    load(TILES, True)
+    made = mm(left_buf[TILES % 2], thin_buf[...], TN).astype(BF16)
+    lanes = thin_buf.shape[1]
+    top = sums[0][:8] + sums[1][:8] + sums[2][...] + sums[3][...]
+    tail = jnp.concatenate([top, sums[0][8:] + sums[1][8:]], axis=0).astype(BF16)
+    zeros = jnp.zeros_like(tail)
+    last = pl.ds(3 * part, 16)
+    for shard in range(2 * n_z):
+        at_z, at_x = shard // 2, shard % 2
+        for block in range(width // lanes):
+            row = shard * part + block * 16
+            both[0, 0, at_z, at_x, last, block * lanes : (block + 1) * lanes] = made[row : row + 16]
+        both[1, 0, at_z, at_x, last] = tail
+        both[0, 1, at_z, at_x, last] = zeros
+        both[1, 1, at_z, at_x, last] = zeros
+    for step, units in (
+        (start_core, (4, 5)),
+        (start_two, (0, 1)),
+        (start_one, (4, 5)),
+        (start_two, (2, 3)),
+        (start_line, (0, 1)),
+        (start_two, (4, 5)),
+        (start_line, (2, 3)),
+        (start_share, (0, 1, 2, 3)),
+        (start_line, (4, 5)),
+        (start_share, (4, 5)),
+        (forward, range(count_units)),
+        (finish, range(count_units)),
+    ):
+        for unit in units:
+            step(unit)
+
+
+def weight_gradients(arrays, sums, n_wide):
     n_z = n_wide // 2
-    width = grads.shape[-1]
-    rows = SHARE_ROWS
+    act, go, final, gp = arrays[0], arrays[1], arrays[9], arrays[10]
+    total, width = go.shape
+    part = width // n_wide
     units = len(UNITS)
     sem = pltpu.SemaphoreType.DMA
+    vmem = pl.BlockSpec(memory_space=pltpu.VMEM)
     return pl.pallas_call(
-        functools.partial(tree_kernel, n_z),
-        out_shape=jax.ShapeDtypeStruct((4, rows, width), BF16),
-        in_specs=[ANY],
-        out_specs=pl.BlockSpec(memory_space=pltpu.VMEM),
+        functools.partial(weights_kernel, n_z, part),
+        out_shape=jax.ShapeDtypeStruct((4, SHARE_ROWS, width), BF16),
+        in_specs=[ANY] * 11 + [vmem] * 4,
+        out_specs=vmem,
         scratch_shapes=[
-            pltpu.VMEM((2, n_z, 2, rows, width), BF16),
-            pltpu.VMEM((2, n_z, 2, rows, width), BF16),
-            pltpu.VMEM((2, n_z, 2, 80, width), BF16),
-            pltpu.VMEM((2, 2, n_z, 80, width), BF16),
-            pltpu.VMEM((2, n_z, 80, width), BF16),
-            pltpu.VMEM((2, n_z, 80, width), BF16),
-            pltpu.VMEM((2, n_z, rows, width), BF16),
-            sem((units,)),
+            pltpu.VMEM((2, 2, n_z, 2, SHARE_ROWS, width), BF16),
+            pltpu.VMEM((2, n_z, 2, SHARE_ROWS, width), BF16),
+            pltpu.VMEM((units // 2, n_z, 2, 48, width), BF16),
+            pltpu.VMEM((units // 2, 2, n_z, HALF, width), BF16),
+            pltpu.VMEM((units // 2, n_z, 48, width), BF16),
+            pltpu.VMEM((units // 2, n_z, HALF, width), BF16),
+            pltpu.VMEM((2, n_z, SHARE_ROWS, width), BF16),
+            pltpu.VMEM((2, total, width), BF16),
+            pltpu.VMEM((2, total, width), BF16),
+            pltpu.VMEM(gp.shape, BF16),
+            sem((2, 3)),
         ]
         + [sem((units,))] * 6
         + [sem((units * n_z * 2,))] * 2
@@ -910,8 +1123,8 @@
         compiler_params=pltpu.CompilerParams(
             collective_id=3, has_side_effects=True, vmem_limit_bytes=VMEM_LIMIT
         ),
-        name="sum_weight_gradients",
-    )(grads.reshape(2, 2, n_z, 2, rows, width))
+        name="weight_gradients",
+    )(*arrays, *sums)
 
 
 def outer(left, right):
@@ -983,12 +1196,13 @@
     query_rows, passage_rows = x_query.shape[0], x_passage.shape[0]
     total = query_rows + passage_rows
     kept_q = encode(
-        x_query, lens, vec, weights, 1, query_len, total, passage_rows, None
+        x_query, lens, vec, weights, 1, query_len, total, passage_rows, None, None
     )
-    queries = lax.all_gather(kept_q[15].reshape(micro, -1, embed_width), everyone, axis=0)
+    sizes = (n_wide, n_narrow)
     kept_p = encode(
-        x_passage, lens, vec, weights, micro * own_passages, 0, total, 0, kept_q
+        x_passage, lens, vec, weights, micro * own_passages, 0, total, 0, kept_q, sizes
     )
+    queries = kept_p[16].reshape(n_wide * n_narrow, micro, -1, embed_width)
     ctx, first_low, act, final_low = (kept_p[index] for index in (4, 7, 8, 12))
     passages = kept_p[15].reshape(micro * own_passages, slots, embed_width)
     e, z = similarity(queries, passages, lens)
@@ -1011,67 +1225,49 @@
     grads = jnp.exp(own_scores - row_total) - (positives == own_index).astype(F32)
     token_weights = jnp.repeat(grads, query_len, axis=1).reshape(z.shape) / z
     grad_passage, grad_query = similarity_back(e, token_weights, queries, passages)
-    grad_query = exchange(
-        grad_query.reshape(-1, query_rows, embed_width), n_wide, n_narrow
+    grad_query = grad_query.reshape(-1, 2, query_rows, embed_width)
+    grad_passage = grad_passage.reshape(passage_rows, embed_width)
+    together = grad_query.size <= 4 * total * width
+    back_p = mlp_back(
+        grad_passage,
+        kept_p,
+        vec,
+        weights,
+        micro * own_passages,
+        total,
+        0,
+        None,
+        grad_query if together else None,
+        sizes if together else None,
     )
-    grad_passage = grad_passage.reshape(passage_rows, embed_width)
-    back_p = mlp_back(grad_passage, kept_p, vec, weights, micro * own_passages, total, 0, None)
-    back_q = mlp_back(grad_query, kept_q, vec, weights, 1, total, passage_rows, back_p)
-    gp, go, gi, _, ga, sums_q = back_q
-    d_outer = outer(act, go)
-    d_inner = outer(first_low, gi)
-    d_linear = outer(final_low, gp)
+    grad_query = back_p[6] if together else exchange(grad_query, n_wide, n_narrow)
+    back_q = mlp_back(
+        grad_query, kept_q, vec, weights, 1, total, passage_rows, back_p, None, None
+    )
+    gp, go, gi, _, ga, sums_q = back_q[:6]
     att_p = attention_back(ga, back_p[3], kept_p, weights, micro * own_passages, total, 0, None)
     att_q = attention_back(ga, back_q[3], kept_q, weights, 1, total, passage_rows, att_p[0])
     gqkv = att_q[0]
-    x_all = jnp.concatenate([x_passage, x_query], axis=0)
-    d_out = outer(ctx, ga)
-    d_qkv = outer(x_all, gqkv)
-
-    sums = back_p[5] + sums_q
-    sums = jnp.concatenate([sums, att_p[2] + att_q[2]], axis=0)
     part = width // n_wide
-
-    if part % 16 == 0 and n_narrow == 4:
-        picks = (16, 17, ROW_BO, ROW_G1, ROW_S1, ROW_B2, ROW_G2, ROW_S2)
-        vectors = jnp.concatenate(
-            [sums[pick].reshape(n_wide, part) for pick in picks]
-            + [sums[ROW_BI : ROW_BI + 4].reshape(n_wide, 4 * part)],
-            axis=1,
-        )
-        vectors = jnp.pad(vectors, ((0, 0), (0, 16 * width - vectors.shape[1])))
-        linear_rows = d_linear.astype(BF16).reshape(n_wide, -1, width)
-        tails = jnp.stack(
-            [linear_rows, vectors.astype(BF16).reshape(n_wide, 16, width)]
-            + [jnp.zeros((n_wide, 16, width), BF16)] * 2
-        )
-        packed = jnp.concatenate(
-            [
-                d_outer.astype(BF16).reshape(n_wide, 4, part, width).transpose(1, 0, 2, 3),
-                d_inner.astype(BF16).reshape(n_wide, part, 4, width).transpose(2, 0, 1, 3),
-                jnp.stack(
-                    [
-                        d_qkv[:, index * width : (index + 1) * width]
-                        .astype(BF16)
-                        .reshape(n_wide, part, width)
-                        for index in range(3)
-                    ]
-                    + [d_out.astype(BF16).reshape(n_wide, part, width)]
-                ),
-                tails,
-            ],
-            axis=2,
-        )
-        summed = tree(packed, n_wide).astype(F32)
+    if part == 96 and n_narrow == 4 and act.shape[1] == 4 * width:
+        summed = weight_gradients(
+            (act, go, first_low, gi, x_passage, x_query, gqkv, ctx, ga, final_low, gp),
+            (back_p[5], sums_q, att_p[2], att_q[2]),
+            n_wide,
+        ).astype(F32)
         r_outer = summed[:, :part].reshape(4 * part, width)
         r_inner = summed[:, part : 2 * part].transpose(1, 0, 2).reshape(part, 4 * width)
         r_q, r_k, r_v, r_out = (summed[index, 2 * part : 3 * part] for index in range(4))
-        r_linear = summed[0, 3 * part :].reshape(part, embed_width)
-        flat = summed[1, 3 * part : 3 * part + 2].reshape(-1)
+        thin = summed[0, 3 * part :].reshape(16, -1, embed_width)
+        r_linear = thin.transpose(1, 0, 2).reshape(part, embed_width)
+        vectors = summed[1, 3 * part :]
+        own = lax.dynamic_slice_in_dim(vectors[:8], wide_index * part, part, axis=1)
         v_q, v_v, v_o, v_g1, v_s1, v_2, v_g2, v_s2 = (
-            flat[index * part : (index + 1) * part] for index in range(8)
-        )
-        v_i = flat[8 * part : 12 * part]
+            own[row] for row in (0, 1, ROW_BO, ROW_G1, ROW_S1, ROW_B2, ROW_G2, ROW_S2)
+        )
+        v_i = lax.dynamic_slice_in_dim(
+            vectors[ROW_BI : ROW_BI + 4].reshape(-1), wide_index * 4 * part, 4 * part
+        )
     else:
 
         def reduce(value):
@@ -1083,9 +1279,12 @@
             share = flat.shape[0] // n_wide
             return lax.dynamic_slice_in_dim(flat, wide_index * share, share)
 
+        sums = jnp.concatenate([back_p[5] + sums_q, att_p[2] + att_q[2]], axis=0)
         sums = lax.psum(sums, everyone)
+        x_all = jnp.concatenate([x_passage, x_query], axis=0)
+        pairs = ((act, go), (first_low, gi), (final_low, gp), (ctx, ga), (x_all, gqkv))
         r_outer, r_inner, r_linear, r_out, r_qkv = (
-            reduce(value) for value in (d_outer, d_inner, d_linear, d_out, d_qkv)
+            reduce(outer(*pair)) for pair in pairs
         )
         r_q, r_k, r_v = (r_qkv[:, index * width : (index + 1) * width] for index in range(3))
         v_q, v_v, v_o, v_g1, v_s1, v_2, v_g2, v_s2 = (

time: 454 us -> 370 us (0.81)
  matrix products: 31.8 us -> 0 us
  other arithmetic: 23.5 us -> 6.92 us
  between operations: 14.7 us -> 0.83 us
  local copies, waits for them, and re-layouts: 34.3 us -> 20.5 us
  waiting for transfers between devices: 7.47 us -> 0 us
    dot_general x5 -> x0, matrix products: 31.8 us -> none  [outer(): return lax.dot_general(left, right, TN, preferred_element_type=F32)]
    concatenate x1 -> x0, other arithmetic: 14.8 us -> none  [local(): jnp.concatenate([d_outer.astype(BF16).reshape(n_wide, 4, part, width).tra...]
    reshape x4 -> x1, local copies, waits for them, and re-layouts: 13.4 us -> 0.01 us  [local(): vectors[ROW_BI:ROW_BI + 4].reshape(-1)]
    all_gather x1 -> x0, waiting for transfers between devices: 7.45 us -> none  [local(): lax.all_gather(kept_q[15].reshape(micro, -1, embed_width), everyone, axis=0)]
    unnamed x47 -> x20, local copies, waits for them, and re-layouts: 10.6 us -> 12.1 us
    pallas_call x6 -> x5, Pallas kernels: 254 us -> 255 us  [the longest x1 134 us: weight_gradients(): pl.pallas_call(functools.partial(weights_kernel, n_z, part), out_shape=ja...]
  transfers between devices with their start and end apart: 1 -> 0, of which waited for: 1 -> 0; matrix products, arithmetic and copies ran while one was open for 0% -> 0% of each run, Pallas kernels for 12% -> 0%
where the time goes in v2:
time: 370 us; the launch traced here: 368 us
  Pallas kernels  340 us (92%)
  local copies, waits for them, and re-layouts  20.5 us (6%)
  other arithmetic  6.92 us (2%)
    pallas_call x1, Pallas kernels, weight_gradients(): pl.pallas_call(functools.partial(weights_kernel, n_z, part), out_shape=ja...  134 us
    pallas_call x2, Pallas kernels, encode(): pl.pallas_call(functools.partial(fwd_kernel, grouped, len(aliased), sizes...  76.7 us
    pallas_call x2, Pallas kernels, attention_back(): pl.pallas_call(functools.partial(attention_back_kernel, len(aliased)), ou...  49.4 us
    pallas_call x2, Pallas kernels, mlp_back(): pl.pallas_call(functools.partial(mlp_back_kernel, len(aliased), sizes), o...  43.9 us
    pallas_call x1, Pallas kernels, similarity_back(): pl.pallas_call(sims_back_kernel, out_shape=(jax.ShapeDtypeStruct((micro,...  13.8 us
    unnamed x20, local copies, waits for them, and re-layouts  12.1 us
    pallas_call x1, Pallas kernels, share_scores(): pl.pallas_call(functools.partial(share_kernel, n_wide, n_narrow), out_sha...  12.1 us
    pallas_call x1, Pallas kernels, similarity(): pl.pallas_call(sims_kernel, out_shape=(jax.ShapeDtypeStruct((micro, slots...  10.2 us

profile of v2, /device:TPU:0, one launch (start us, length us, event | category | flops | bytes accessed | tf_op | source)
XLA Modules:
  0.0 368.3 jit_solution(14966260532577510953)
XLA Ops:
  0.7 0.0 copy-start
  0.7 0.7 copy-done
  1.3 0.7 dynamic-slice_reduce_fusion.refs_0_.lens_ref
  2.0 0.8 dynamic-update-slice
  2.9 0.8 dynamic-update-slice.1
  3.7 0.9 dynamic-update-slice.2
  4.6 0.9 dynamic-update-slice.3
  5.4 0.9 dynamic-update-slice.4
  6.3 0.8 dynamic-update-slice.5
  7.1 0.9 dynamic-update-slice.6
  8.0 0.9 dynamic-update-slice.7
  8.8 0.7 constant_dynamic-update-slice_fusion
  9.6 0.6 pad_convert_fusion.refs_2_.refs_8_
  10.2 18.8 %encode_queries.1 = (bf16[256,768]{1,0:T(8,128)(2,1)}, bf16[256,768]{1,0:T(8,128)(2,1)}, bf16[256,768]{1,0:T(8,128)(2,1)}, bf16[1,12,256,256]{3,2,1,0:T(8,128)(2...) custom-call(s32[2]{0:T(128)} %dynamic-slice_reduce_fusion.refs_0_.le, ...), custom_call_target="tpu_custom_call" | custom-call | tf_op jit(solution)/shard_map/encode_queries/pallas_call | solution.py:375
  29.1 57.8 %encode_passages.1 = (bf16[1024,768]{1,0:T(8,128)(2,1)}, bf16[1024,768]{1,0:T(8,128)(2,1)}, bf16[1024,768]{1,0:T(8,128)(2,1)}, bf16[2,12,512,512]{3,2,1,0:T(8,12...) custom-call(s32[2]{0:T(128)} %dynamic-slice_reduce_fusion.refs_0_.le, ...), custom_call_target="tpu_custom_call", output_to_operand_aliasing={{4}: (10, {}), {7}: (11, {}), {8}: (12, {}), {12}: (13, {})} | custom-call | tf_op jit(solution)/shard_map/encode_passages/pallas_call | solution.py:375
  86.9 0.0 copy-start.4
  86.9 10.2 %similarity.1 = (bf16[2,512,4096]{2,1,0:T(8,128)(2,1)}, f32[2,32,128]{2,1,0:T(8,128)}) custom-call(s32[2]{0:T(128)} %dynamic-slice_reduce_fusion.refs_0_.lens_ref, bf16[32,2,128,128]{3,2,1,0:T(8,128)(2,1)} %bitcast.43, bf16[2,512,128]{2,1,0:T(8,128)(2,1)} %bitcast.52), custom_call_target="tpu_custom_call" | custom-call | tf_op jit(solution)/shard_map/similarity/pallas_call | solution.py:434
  97.1 0.8 log_add_fusion
  97.9 0.1 reshape.116
  97.9 0.1 reduce_sum.27
  98.1 0.6 broadcast_multiply_fusion.own_ref
  98.6 12.1 %share_scores.1 = f32[32,2,128]{2,1,0:T(2,128)} custom-call(f32[2,128]{1,0:T(2,128)} %broadcast_multiply_fusion.own_ref), custom_call_target="tpu_custom_call" | custom-call | tf_op jit(solution)/shard_map/share_scores/pallas_call | solution.py:758
  110.8 0.8 dynamic-slice_bitcast_fusion
  111.5 0.6 copy.57
  112.1 0.8 reduce_max.9
  113.0 0.0 copy-done.4
  113.0 0.8 exponential_reduce_fusion
  113.8 0.6 constant_dynamic-slice_fusion.1
  114.4 0.1 broadcast_in_dim.15
  114.5 0.1 reshape_reshape.3
  114.6 1.4 div.11.w_ref
  116.0 13.8 %similarity_back.1 = (f32[2,512,128]{2,1,0:T(8,128)}, bf16[32,2,128,128]{3,2,1,0:T(8,128)(2,1)}) custom-call(bf16[2,512,4096]{2,1,0:T(8,128)(2,1)} %get-tuple-element.84.e_ref, f32[2,32,128]{2,1,0:T(8,128)} %div.11.w_ref, bf16[32,2,128,128]{3,2,1,0:T(8,128)(2,1)} %bitcast.44, bf16[2,512,128]{2,1,0:T(8,128)(2,1)} %bitcast.53), custom_call_target="tpu_custom_call" | custom-call | tf_op jit(solution)/shard_map/similarity_back/pallas_call | solution.py:462
  129.8 32.8 %mlp_back_passages.1 = (bf16[1280,128]{1,0:T(8,128)(2,1)}, bf16[1280,768]{1,0:T(8,128)(2,1)}, bf16[1280,3072]{1,0:T(8,128)(2,1)}, f32[1024,768]{1,0:T(8,128)}, b...) custom-call(f32[1024,128]{1,0:T(8,128)} %bitcast.54, f32[1024,128]{1,0:T(8,128)} %get-tuple-element.86.refs_1_, ...), custom_call_target="tpu_custom_call" | custom-call | tf_op jit(solution)/shard_map/mlp_back_passages/pallas_call | solution.py:601
  162.6 11.0 %mlp_back_queries.1 = (bf16[1280,128]{1,0:T(8,128)(2,1)}, bf16[1280,768]{1,0:T(8,128)(2,1)}, bf16[1280,3072]{1,0:T(8,128)(2,1)}, f32[256,768]{1,0:T(8,128)}, bf1...) custom-call(f32[256,128]{1,0:T(8,128)} %get-tuple-element.94.refs_0_, ...), custom_call_target="tpu_custom_call", output_to_operand_aliasing={{0}: (12, {}), {1}: (13, {}), {2}: (14, {}), {4}: (15, {})} | custom-call | tf_op jit(solution)/shard_map/mlp_back_queries/pallas_call | solution.py:601
  173.7 38.0 %attention_back_passages.1 = (bf16[1280,2304]{1,0:T(8,128)(2,1)}, f32[1024,768]{1,0:T(8,128)}, f32[8,768]{1,0:T(8,128)}) custom-call(bf16[1280,768]{1,0:T(8,128)(2,1)} %get-tuple-element.106.refs_0_.refs_8_, f32[1024,768]{1,0:T(8,128)} %get-tuple-element.112.refs_1_, bf16[2,12,512,512]{3,2,1,0:T(8,128)(2,1)} %get-tuple-element.113.refs_2_, ...), custom_call_target="tpu_custom_call" | custom-call | tf_op jit(solution)/shard_map/attention_back_passages/pallas_call | solution.py:691
  211.7 11.4 %attention_back_queries.1 = (bf16[1280,2304]{1,0:T(8,128)(2,1)}, f32[256,768]{1,0:T(8,128)}, f32[8,768]{1,0:T(8,128)}) custom-call(bf16[1280,768]{1,0:T(8,128)(2,1)} %get-tuple-element.106.refs_0_.refs_8_, f32[256,768]{1,0:T(8,128)} %get-tuple-element.107.refs_1_, ...), custom_call_target="tpu_custom_call", output_to_operand_aliasing={{0}: (10, {})} | custom-call | tf_op jit(solution)/shard_map/attention_back_queries/pallas_call | solution.py:691
  223.1 134.1 %weight_gradients.1 = bf16[4,304,768]{2,1,0:T(8,128)(2,1)} custom-call(bf16[1280,3072]{1,0:T(8,128)(2,1)} %get-tuple-element.120.refs_0_, bf16[1280,768]{1,0:T(8,128)(2,1)} %get-tuple-element.121.refs_1_, bf16[1280,768]{1,0:T(8,128)(2,1)} %get-tuple-element.122.refs_2_, bf16[1280,3072]{1,0:T(8,128)(2,1)} %get-tuple-element.123.refs_3_, ...), custom_call_target="tpu_custom_call" | custom-call | tf_op jit(solution)/shard_map/weight_gradients/pallas_call | solution.py:1102
  357.2 1.8 convert_element_type.15
  359.0 0.0 copy-start.3
  359.1 1.8 copy-done.3
  360.9 0.0 copy-start.2
  360.9 1.0 slice_bitcast_fusion.1
  361.9 0.9 copy-done.2
  362.8 0.1 constant_dynamic-slice_fusion
  362.9 0.5 slice_bitcast_fusion.5
  363.4 1.3 slice_bitcast_fusion
  364.8 0.0 copy-start.1
  364.8 1.1 copy.59
  365.9 0.7 dynamic_slice.19
  366.6 1.1 slice.88
  367.7 0.6 copy.56
  368.3 0.0 copy-done.1
  (9 shorter events, 0.1 us)
Async XLA Ops:
  0.7 0.7 copy-start
  86.9 26.0 %copy-start.4 = (s32[2,128]{1,0:T(2,128)S(1)}, s32[2,128]{1,0:T(2,128)}, u32[]{:S(2)}) copy-start(s32[2,128]{1,0:T(2,128)} %param.23) | copy-start | bytes 3076
  359.0 1.8 copy-start.3
  360.9 1.9 copy-start.2
  364.8 3.6 copy-start.1

commit v3 on v2

--- a/solution.py
+++ b/solution.py
@@ -237,7 +237,6 @@
     if gather:
         last = pl.program_id(0) == pl.num_programs(0) - 1
         pl.when(loader.first)(gather.start)
-        pl.when(last)(gather.forward)
     rows = x_ref.shape[0]
     x = x_ref[...]
     scale = HEAD_DIM ** (-0.5)
@@ -275,6 +274,8 @@
         return carry
 
     lax.fori_loop(0, HEADS // 2, pair_body, 0)
+    if gather:
+        pl.when(last)(gather.forward)
     loader.need(3)
     field = x.astype(F32) + (mm(ctx_ref[...], wo[...]) + vec_row(vec_ref, ROW_BO))
     center = field - mean_row(field)
@@ -718,6 +719,17 @@
     )(attended, hidden, kept[3], kept[0], kept[1], kept[2], wo, wq, wk, wv, *aliased)
 
 
+def pack(vectors, width):
+    count = sum(vector.shape[0] for vector in vectors)
+    total = -(-count // (8 * width)) * 8 * width
+    start, packed = 0, 0.0
+    for vector in vectors:
+        size = vector.shape[0]
+        packed = packed + jnp.pad(vector.astype(F32), (start, total - start - size))
+        start += size
+    return packed.reshape(-1, width)
+
+
 def share_kernel(n_wide, n_narrow, own_ref, all_ref, send_sem, recv_sem):
     me = lax.axis_index("narrow") * n_wide + lax.axis_index("wide")
     total = n_wide * n_narrow
@@ -788,20 +800,36 @@
     )(grads)
 
 
-UNITS = ((0, 48), (48, 48), (96, 48), (144, 48), (192, 48), (240, 64))
+UNITS = (
+    (0, 48, 0),
+    (48, 48, 0),
+    (96, 48, 48),
+    (144, 48, 48),
+    (192, 16, 96),
+    (240, 16, 96),
+    (208, 16, 112),
+    (256, 16, 112),
+    (224, 16, 128),
+    (272, 32, 128),
+)
+EARLY = (0, 1, 2, 3)
+LATE = (4, 5, 6, 7, 8, 9)
 SHARE_ROWS = 304
-HALF = 64
-TILES = 12
-
-
-def weights_kernel(n_z, part, *refs):
-    act, go, first, gi, x_p, x_q, gqkv, ctx, ga, final, gp = refs[:11]
-    sums = refs[11:15]
-    out_ref = refs[15]
-    both, near, over_a, over_b, then_a, then_b, line, left_buf, right_buf, thin_buf = refs[16:26]
-    load_sem = refs[26]
+ROWS_A, ROWS_B = 144, 160
+TILES = 9
+
+
+def tail_kernel(n_z, part, *refs):
+    act, go, first, gi, x_p, x_q, ctx, ga, final, gp = refs[:10]
+    kept = (refs[10:15], refs[15:20])
+    sources = refs[20:24]
+    sums = refs[24:26]
+    out_ref, gx_p, gx_q = refs[26:29]
+    both, near, over_a, over_b, then_a, then_b, line, left_buf, right_buf, thin_buf = refs[29:39]
+    wo, wq, wk, wv, att_buf, hidden, thin_hidden, grads, att_sums = refs[39:48]
+    load_sem, weight_sem, block_sem, att_sem, gx_sem = refs[48:53]
     core_sems, one_sems, two_sems, line_sems, copy_sems = (
-        refs[27 + 2 * index : 29 + 2 * index] for index in range(5)
+        refs[53 + 2 * index : 55 + 2 * index] for index in range(5)
     )
     wide, narrow = lax.axis_index("wide"), lax.axis_index("narrow")
     z, x = wide // 2, lax.rem(wide, 2)
@@ -810,45 +838,37 @@
     over_y = (wide, (1 - y) * 2 + core)
     over_x = (z * 2 + 1 - x, narrow)
     right, left = (wide + 2, narrow), (wide - 2, narrow)
-    width = go.shape[1]
+    total, width = go.shape
     p_rows = x_p.shape[0]
-    count_units = len(UNITS)
     held = both.at[core]
 
     def load(tile, wait):
         slot = lax.rem(tile, 2)
         block = pl.ds(pl.multiple_of(lax.rem(tile, 4) * width, width), width)
 
-        def copy(source, target, sem):
-            made = pltpu.make_async_copy(source, target, sem)
-            if wait:
-                made.wait()
-            else:
-                made.start()
-
-        def pair(source, other):
-            copy(source, left_buf.at[slot], load_sem.at[slot, 0])
-            copy(other, right_buf.at[slot], load_sem.at[slot, 1])
-
-        pl.when(tile < 4)(lambda: pair(act.at[:, block], go))
-        pl.when(jnp.logical_and(tile >= 4, tile < 8))(lambda: pair(first, gi.at[:, block]))
-
-        @pl.when(jnp.logical_and(tile >= 8, tile < 11))
-        def _():
-            copy(x_p, left_buf.at[slot, pl.ds(0, p_rows)], load_sem.at[slot, 0])
-            copy(x_q, left_buf.at[slot, pl.ds(p_rows, x_q.shape[0])], load_sem.at[slot, 2])
-            copy(gqkv.at[:, block], right_buf.at[slot], load_sem.at[slot, 1])
-
-        pl.when(tile == 11)(lambda: pair(ctx, ga))
-
-        @pl.when(tile == TILES)
-        def _():
-            copy(final, left_buf.at[slot], load_sem.at[slot, 0])
-            copy(gp, thin_buf, load_sem.at[slot, 1])
+        def pair(source, other, target):
+            for made in (
+                pltpu.make_async_copy(source, left_buf.at[slot], load_sem.at[slot, 0]),
+                pltpu.make_async_copy(other, target, load_sem.at[slot, 1]),
+            ):
+                if wait:
+                    made.wait()
+                else:
+                    made.start()
+
+        place = right_buf.at[slot]
+        pl.when(tile < 4)(lambda: pair(act.at[:, block], go, place))
+        pl.when(jnp.logical_and(tile >= 4, tile < 8))(lambda: pair(first, gi.at[:, block], place))
+        pl.when(tile == 8)(lambda: pair(ctx, ga, place))
+        pl.when(tile == TILES)(lambda: pair(final, gp, thin_buf))
 
     def rows_of(unit):
-        start, count = UNITS[unit]
+        start, count, _ = UNITS[unit]
         return pl.ds(start, count)
+
+    def place_of(unit):
+        _, count, place = UNITS[unit]
+        return pl.ds(place, count)
 
     def core_copy(unit):
         rows = rows_of(unit)
@@ -858,14 +878,18 @@
 
     def one_copy(unit):
         rows = rows_of(unit)
-        count = UNITS[unit][1]
+        place = place_of(unit)
         if unit % 2 == 0:
             return remote(
-                held.at[1 - y, :, :, rows], over_a.at[unit // 2], one_sems, unit, over_y
+                held.at[1 - y, :, :, rows],
+                over_a.at[:, :, place],
+                one_sems,
+                unit,
+                over_y,
             )
         return remote(
             held.at[:, :, 1 - x, rows],
-            over_b.at[unit // 2, :, :, pl.ds(0, count)],
+            over_b.at[:, :, place],
             one_sems,
             unit,
             over_x,
@@ -873,12 +897,18 @@
 
     def two_copy(unit):
         rows = rows_of(unit)
-        count = UNITS[unit][1]
+        place = place_of(unit)
         if unit % 2 == 0:
-            return remote(held.at[y, :, 1 - x, rows], then_a.at[unit // 2], two_sems, unit, over_x)
+            return remote(
+                held.at[y, :, 1 - x, rows],
+                then_a.at[:, place],
+                two_sems,
+                unit,
+                over_x,
+            )
         return remote(
             held.at[1 - y, :, x, rows],
-            then_b.at[unit // 2, :, pl.ds(0, count)],
+            then_b.at[:, place],
             two_sems,
             unit,
             over_y,
@@ -906,7 +936,7 @@
         return remote(block, block, copy_sems, unit * 3 + step, over_y if step == 1 else mate)
 
     def add(target, extra):
-        target[...] = (target[...].astype(F32) + extra[...].astype(F32)).astype(BF16)
+        target[...] = target[...] + extra[...]
 
     def start_core(unit):
         core_copy(unit).start()
@@ -926,46 +956,51 @@
 
     def start_two(unit):
         rows = rows_of(unit)
-        count = UNITS[unit][1]
+        place = place_of(unit)
         one_copy(unit).wait_recv()
 
         def body(index, carry):
             outer_at, inner_at = index // 2, lax.rem(index, 2)
             if unit % 2 == 0:
-                add(held.at[y, outer_at, inner_at, rows], over_a.at[unit // 2, outer_at, inner_at])
+                add(
+                    held.at[y, outer_at, inner_at, rows],
+                    over_a.at[outer_at, inner_at, place],
+                )
             else:
                 add(
                     held.at[inner_at, outer_at, x, rows],
-                    over_b.at[unit // 2, inner_at, outer_at, pl.ds(0, count)],
+                    over_b.at[inner_at, outer_at, place],
                 )
             return carry
 
         lax.fori_loop(0, 2 * n_z, body, 0)
         two_copy(unit).start()
 
-    def start_line(unit):
-        rows = rows_of(unit)
-        count = UNITS[unit][1]
-        two_copy(unit).wait_recv()
-
-        def body(index, carry):
+    def line_phase(phase):
+        def run(unit):
+            rows = rows_of(unit)
+            place = place_of(unit)
             extra = then_a if unit % 2 == 0 else then_b
-            add(held.at[y, index, x, rows], extra.at[unit // 2, index, pl.ds(0, count)])
-            return carry
-
-        lax.fori_loop(0, n_z, body, 0)
-        for step in range(n_z - 1):
-            for way in range(2):
-                target = n_z - 1 - step if way == 0 else step
-                sends = z < target if way == 0 else z > target
-                edge = z > 0 if way == 0 else z < n_z - 1
-
-                @pl.when(jnp.logical_and(sends, edge))
-                def _(target=target, way=way):
-                    line_copy(unit, target, way).wait_recv()
-                    add(held.at[y, target, x, rows], line.at[way, target, rows])
-
-                pl.when(sends)(line_copy(unit, target, way).start)
+
+            def body(index, carry):
+                add(held.at[y, index, x, rows], extra.at[index, place])
+                return carry
+
+            if phase == 0:
+                two_copy(unit).wait_recv()
+                lax.fori_loop(0, n_z, body, 0)
+            for way, at in ((0, phase), (1, n_z - 1 - phase)):
+
+                @pl.when(z == at)
+                def _(way=way, at=at):
+                    for target in range(n_z - 1, at, -1) if way == 0 else range(at):
+                        copy = line_copy(unit, target, way)
+                        if phase > 0:
+                            copy.wait_recv()
+                            add(held.at[y, target, x, rows], line.at[way, target, rows])
+                        copy.start()
+
+        return run
 
     def start_share(unit):
         rows = rows_of(unit)
@@ -1015,16 +1050,37 @@
 
     pl.semaphore_wait(barrier, jnp.where(jnp.logical_and(z > 0, z < n_z - 1), 5, 4))
 
+    def put(kind, owner, half, made):
+        rows = pl.ds(pl.multiple_of(kind * part, part), part)
+        for index in range(4):
+            both[lax.rem(owner, 2), owner // 2, 2 * half + index // 2, index % 2, rows] = made[
+                index * part : (index + 1) * part
+            ]
+
+    def halves(left_ref, right_ref, store):
+        def half_body(half, carry):
+            cols = pl.ds(pl.multiple_of(half * 4 * part, 4 * part), 4 * part)
+            store(half, mm(left_ref[:, cols], right_ref[...], TN).astype(BF16))
+            return carry
+
+        lax.fori_loop(0, 2, half_body, 0)
+
+    def hooks(now, plan):
+        for at, step, units in plan:
+
+            @pl.when(now == at)
+            def _(step=step, units=units):
+                for unit in units:
+                    step(unit)
+
     def tile_body(tile, carry):
         slot = lax.rem(tile, 2)
         load(tile, True)
         load(tile + 1, False)
-        kind, owner = tile // 4, lax.rem(tile, 4)
-
-        def half_body(half, carry):
-            cols = pl.ds(pl.multiple_of(half * 4 * part, 4 * part), 4 * part)
-            made = mm(left_buf[slot, :, cols], right_buf[slot], TN).astype(BF16)
-
+        kind = tile // 4
+        owner = jnp.where(tile == 8, 3, lax.rem(tile, 4))
+
+        def store(half, made):
             @pl.when(kind == 0)
             def _():
                 for index in range(4):
@@ -1032,90 +1088,262 @@
                         index * part : (index + 1) * part
                     ]
 
-            @pl.when(kind > 0)
-            def _():
-                rows = pl.ds(pl.multiple_of(kind * part, part), part)
-                for index in range(4):
-                    both[lax.rem(owner, 2), owner // 2, 2 * half + index // 2, index % 2, rows] = (
-                        made[index * part : (index + 1) * part]
+            pl.when(kind > 0)(lambda: put(kind, owner, half, made))
+
+        halves(left_buf.at[slot], right_buf.at[slot], store)
+        hooks(
+            tile, ((3, start_core, (0, 1)), (6, start_one, (0, 1)), (7, start_core, (2, 3)))
+        )
+        return carry
+
+    def hidden_of(block):
+        return thin_hidden if blocks[block][2] else hidden.at[block]
+
+    def block_copies(block):
+        rows, base, source = blocks[block]
+        q, k, v, gh, _ = kept[source]
+        buf = left_buf if block % 2 == 0 else right_buf
+        own = pl.ds(base - (p_rows if source else 0), rows)
+        low, high = pl.ds(0, rows), pl.ds(span, rows)
+        pairs = (
+            (q.at[own], buf.at[0, low]),
+            (k.at[own], buf.at[0, high]),
+            (v.at[own], buf.at[1, low]),
+            (ga.at[pl.ds(base, rows)], buf.at[1, high]),
+            (gh.at[own], hidden_of(block)),
+        )
+        return [
+            pltpu.make_async_copy(*pair, block_sem.at[block % 2, index])
+            for index, pair in enumerate(pairs)
+        ]
+
+    def gx_copy(block):
+        rows, base, source = blocks[block]
+        target = gx_q if source else gx_p
+        own = pl.ds(base - (p_rows if source else 0), rows)
+        return pltpu.make_async_copy(hidden_of(block), target.at[own], gx_sem.at[block])
+
+    def states(block):
+        rows, base, _ = blocks[block]
+        own = pl.ds(base, rows)
+        hidden_of(block)[...] += (
+            mm(grads[0, own], wq[...], NT)
+            + mm(grads[1, own], wk[...], NT)
+            + mm(grads[2, own], wv[...], NT)
+        )
+        gx_copy(block).start()
+
+    def attention(block, plan):
+        rows, base, source = blocks[block]
+        buf = left_buf if block % 2 == 0 else right_buf
+        low, high, own = pl.ds(0, rows), pl.ds(span, rows), pl.ds(base, rows)
+        att = kept[source][4]
+        q_ref, k_ref, v_ref, ga_ref = (
+            buf.at[0, low],
+            buf.at[0, high],
+            buf.at[1, low],
+            buf.at[1, high],
+        )
+        entry = 0 if source else block
+        size = pl.ds(0, rows)
+
+        def att_copy(pair):
+            slot = lax.rem(pair, 2)
+            return pltpu.make_async_copy(
+                att.at[entry, pl.ds(2 * pair, 2)],
+                att_buf.at[slot, :, size, size],
+                att_sem.at[slot],
+            )
+
+        att_copy(0).start()
+        for copy in block_copies(block):
+            copy.wait()
+        grads[2, own] = mm(ga_ref[...], wo[...], NT).astype(BF16)
+        low_half = lax.broadcasted_iota(jnp.int32, (rows, 128), 1) < HEAD_DIM
+        scale = HEAD_DIM ** (-0.5)
+
+        def pair_body(pair, carry):
+            cols = pl.ds(pl.multiple_of(pair * 128, 128), 128)
+            slot = lax.rem(pair, 2)
+            att_copy(pair).wait()
+            pl.when(pair < HEADS // 2 - 1)(lambda: att_copy(pair + 1).start())
+            q_pair, k_pair, v_pair = q_ref[:, cols], k_ref[:, cols], v_ref[:, cols]
+            gc_pair = grads[2, own, cols]
+            parts = []
+            for half in range(2):
+                mask = low_half if half == 0 else jnp.logical_not(low_half)
+                low_att = att_buf[slot, half, size, size]
+                wide_att = low_att.astype(F32)
+                grad_att = mm(jnp.where(mask, gc_pair, jnp.zeros_like(gc_pair)), v_pair, NT)
+                weighted = grad_att * wide_att
+                grad_logits = (
+                    weighted - wide_att * jnp.sum(weighted, axis=-1, keepdims=True)
+                ).astype(BF16)
+                parts.append(
+                    (
+                        mm(grad_logits, k_pair) * scale,
+                        mm(grad_logits, q_pair, TN),
+                        mm(low_att, gc_pair, TN),
                     )
-
+                )
+            for index in range(3):
+                grads[index, own, cols] = jnp.where(
+                    low_half, parts[0][index], parts[1][index]
+                ).astype(BF16)
+            hooks(pair, plan)
             return carry
 
-        lax.fori_loop(0, 2, half_body, 0)
-        for when_tile, step, units in (
-            (3, start_core, (0, 1)),
-            (6, start_one, (0, 1)),
-            (7, start_core, (2, 3)),
-            (10, start_one, (2, 3)),
-        ):
-
-            @pl.when(tile == when_tile)
-            def _(step=step, units=units):
-                for unit in units:
-                    step(unit)
-
-        return carry
-
+        lax.fori_loop(0, HEADS // 2, pair_body, 0)
+        accumulate(att_sums, 0, grads[0, own].astype(F32))
+        accumulate(att_sums, 1, grads[2, own].astype(F32))
+
+    def weight_copies():
+        return [
+            pltpu.make_async_copy(source, target, weight_sem.at[index])
+            for index, (source, target) in enumerate(zip(sources, (wo, wq, wk, wv)))
+        ]
+
+    span = kept[0][4].shape[-1]
+    blocks = [(span, base, 0) for base in range(0, p_rows, span)] + [(x_q.shape[0], p_rows, 1)]
+    for copy in weight_copies():
+        copy.start()
+    att_sums[...] = jnp.zeros_like(att_sums)
     lax.fori_loop(0, TILES, tile_body, 0)
     load(TILES, True)
-    made = mm(left_buf[TILES % 2], thin_buf[...], TN).astype(BF16)
+    slot = TILES % 2
+    made = mm(left_buf[slot], thin_buf[...], TN).astype(BF16)
+    for copy in block_copies(0):
+        copy.start()
     lanes = thin_buf.shape[1]
-    top = sums[0][:8] + sums[1][:8] + sums[2][...] + sums[3][...]
-    tail = jnp.concatenate([top, sums[0][8:] + sums[1][8:]], axis=0).astype(BF16)
-    zeros = jnp.zeros_like(tail)
     last = pl.ds(3 * part, 16)
     for shard in range(2 * n_z):
-        at_z, at_x = shard // 2, shard % 2
         for block in range(width // lanes):
             row = shard * part + block * 16
-            both[0, 0, at_z, at_x, last, block * lanes : (block + 1) * lanes] = made[row : row + 16]
+            both[0, 0, shard // 2, shard % 2, last, block * lanes : (block + 1) * lanes] = made[
+                row : row + 16
+            ]
+    for copy in weight_copies():
+        copy.wait()
+    for unit in (2, 3):
+        start_one(unit)
+    line_a, line_b, line_c = (line_phase(phase) for phase in range(3))
+    for copy in block_copies(1):
+        copy.start()
+    attention(0, ((1, start_two, (0, 1)),))
+    for copy in block_copies(2):
+        copy.start()
+    attention(
+        1,
+        (
+            (0, start_two, (2, 3)),
+            (1, line_a, (0, 1)),
+            (2, line_b, (0, 1)),
+            (3, line_c, (0, 1)),
+            (4, line_a, (2, 3)),
+            (5, line_b, (2, 3)),
+        ),
+    )
+    x_copies = [
+        pltpu.make_async_copy(x_p, right_buf.at[0, pl.ds(0, p_rows)], load_sem.at[0, 0]),
+        pltpu.make_async_copy(
+            x_q, right_buf.at[0, pl.ds(p_rows, total - p_rows)], load_sem.at[0, 1]
+        ),
+    ]
+    for copy in x_copies:
+        copy.start()
+    attention(2, ((1, line_c, (2, 3)), (4, start_share, EARLY)))
+    for copy in x_copies:
+        copy.wait()
+
+    def late_body(tile, carry):
+        halves(right_buf.at[0], grads.at[tile], lambda half, made: put(2, tile, half, made))
+        return carry
+
+    lax.fori_loop(0, 3, late_body, 0)
+    top = sums[0][:8] + sums[1][:8] + att_sums[...]
+    tail = jnp.concatenate([top, sums[0][8:] + sums[1][8:]], axis=0).astype(BF16)
+    for shard in range(2 * n_z):
+        at_z, at_x = shard // 2, shard % 2
         both[1, 0, at_z, at_x, last] = tail
-        both[0, 1, at_z, at_x, last] = zeros
-        both[1, 1, at_z, at_x, last] = zeros
+        both[0, 1, at_z, at_x, last] = jnp.zeros_like(tail)
+        both[1, 1, at_z, at_x, last] = jnp.zeros_like(tail)
     for step, units in (
-        (start_core, (4, 5)),
-        (start_two, (0, 1)),
-        (start_one, (4, 5)),
-        (start_two, (2, 3)),
-        (start_line, (0, 1)),
+        (start_core, LATE),
+        (forward, EARLY),
+        (start_one, LATE),
+        (states, (0,)),
         (start_two, (4, 5)),
-        (start_line, (2, 3)),
-        (start_share, (0, 1, 2, 3)),
-        (start_line, (4, 5)),
+        (states, (1,)),
+        (start_two, (6, 7)),
+        (line_a, (4, 5)),
+        (states, (2,)),
+        (line_b, (4, 5)),
+        (start_two, (8,)),
+        (line_c, (4, 5)),
+        (line_a, (6,)),
+        (start_two, (9,)),
+        (line_a, (7,)),
+        (line_b, (6, 7)),
         (start_share, (4, 5)),
-        (forward, range(count_units)),
-        (finish, range(count_units)),
+        (line_c, (6, 7)),
+        (line_a, (8,)),
+        (line_b, (8,)),
+        (line_a, (9,)),
+        (line_c, (8,)),
+        (line_b, (9,)),
+        (start_share, (6, 7)),
+        (line_c, (9,)),
+        (start_share, (8, 9)),
+        (forward, LATE),
+        (finish, EARLY + LATE),
+        (lambda block: gx_copy(block).wait(), range(len(blocks))),
     ):
         for unit in units:
             step(unit)
 
 
-def weight_gradients(arrays, sums, n_wide):
+def backward_tail(arrays, passage_kept, query_kept, weights, sums, n_wide):
     n_z = n_wide // 2
-    act, go, final, gp = arrays[0], arrays[1], arrays[9], arrays[10]
+    go, x_p, x_q, gp = arrays[1], arrays[4], arrays[5], arrays[9]
     total, width = go.shape
     part = width // n_wide
     units = len(UNITS)
+    span = passage_kept[4].shape[-1]
     sem = pltpu.SemaphoreType.DMA
     vmem = pl.BlockSpec(memory_space=pltpu.VMEM)
     return pl.pallas_call(
-        functools.partial(weights_kernel, n_z, part),
-        out_shape=jax.ShapeDtypeStruct((4, SHARE_ROWS, width), BF16),
-        in_specs=[ANY] * 11 + [vmem] * 4,
-        out_specs=vmem,
+        functools.partial(tail_kernel, n_z, part),
+        out_shape=(
+            jax.ShapeDtypeStruct((4, SHARE_ROWS, width), BF16),
+            jax.ShapeDtypeStruct(x_p.shape, F32),
+            jax.ShapeDtypeStruct(x_q.shape, F32),
+        ),
+        in_specs=[ANY] * 24 + [vmem] * 2,
+        out_specs=(vmem, ANY, ANY),
         scratch_shapes=[
             pltpu.VMEM((2, 2, n_z, 2, SHARE_ROWS, width), BF16),
             pltpu.VMEM((2, n_z, 2, SHARE_ROWS, width), BF16),
-            pltpu.VMEM((units // 2, n_z, 2, 48, width), BF16),
-            pltpu.VMEM((units // 2, 2, n_z, HALF, width), BF16),
-            pltpu.VMEM((units // 2, n_z, 48, width), BF16),
-            pltpu.VMEM((units // 2, n_z, HALF, width), BF16),
+            pltpu.VMEM((n_z, 2, ROWS_A, width), BF16),
+            pltpu.VMEM((2, n_z, ROWS_B, width), BF16),
+            pltpu.VMEM((n_z, ROWS_A, width), BF16),
+            pltpu.VMEM((n_z, ROWS_B, width), BF16),
             pltpu.VMEM((2, n_z, SHARE_ROWS, width), BF16),
             pltpu.VMEM((2, total, width), BF16),
             pltpu.VMEM((2, total, width), BF16),
             pltpu.VMEM(gp.shape, BF16),
-            sem((2, 3)),
+        ]
+        + [pltpu.VMEM((width, width), BF16)] * 4
+        + [
+            pltpu.VMEM((2, 2, span, span), BF16),
+            pltpu.VMEM((2, span, width), F32),
+            pltpu.VMEM(x_q.shape, F32),
+            pltpu.VMEM((3, total, width), BF16),
+            pltpu.VMEM((8, width), F32),
+            sem((2, 2)),
+            sem((4,)),
+            sem((2, 5)),
+            sem((2,)),
+            sem((3,)),
         ]
         + [sem((units,))] * 6
         + [sem((units * n_z * 2,))] * 2
@@ -1123,8 +1351,42 @@
         compiler_params=pltpu.CompilerParams(
             collective_id=3, has_side_effects=True, vmem_limit_bytes=VMEM_LIMIT
         ),
-        name="weight_gradients",
-    )(*arrays, *sums)
+        name="backward_tail",
+    )(*arrays, *passage_kept, *query_kept, *weights, *sums)
+
+
+def unpack_kernel(part, sums_ref, q_ref, k_ref, v_ref, o_ref, inner_ref, outer_ref, thin_ref, vec_ref):
+    width = q_ref.shape[1]
+    lanes = thin_ref.shape[1]
+    for owner, ref in enumerate((q_ref, k_ref, v_ref, o_ref)):
+        ref[...] = sums_ref[owner, 2 * part : 3 * part].astype(F32)
+        inner_ref[:, owner * width : (owner + 1) * width] = sums_ref[
+            owner, part : 2 * part
+        ].astype(F32)
+        outer_ref[owner * part : (owner + 1) * part] = sums_ref[owner, :part].astype(F32)
+    tail = sums_ref[0, 3 * part :].astype(F32)
+    for block in range(width // lanes):
+        thin_ref[block * 16 : (block + 1) * 16] = tail[:, block * lanes : (block + 1) * lanes]
+    vec_ref[...] = sums_ref[1, 3 * part :].astype(F32)
+
+
+def unpack(summed, part, embed_width):
+    width = summed.shape[-1]
+    vmem = pl.BlockSpec(memory_space=pltpu.VMEM)
+    shapes = [(part, width)] * 4 + [
+        (part, 4 * width),
+        (4 * part, width),
+        (part, embed_width),
+        (16, width),
+    ]
+    return pl.pallas_call(
+        functools.partial(unpack_kernel, part),
+        out_shape=[jax.ShapeDtypeStruct(shape, F32) for shape in shapes],
+        in_specs=[vmem],
+        out_specs=[vmem] * len(shapes),
+        compiler_params=pltpu.CompilerParams(vmem_limit_bytes=VMEM_LIMIT),
+        name="unpack_gradients",
+    )(summed)
 
 
 def outer(left, right):
@@ -1170,24 +1432,20 @@
         linear_weight,
     )
     embed_width = linear_weight.shape[1]
-    vec = (
-        jnp.concatenate(
-            [
-                query_bias,
-                value_bias,
-                out_bias,
-                first_gain,
-                first_shift,
-                outer_bias,
-                second_gain,
-                second_shift,
-                inner_bias,
-            ]
-        )
-        .astype(F32)
-        .reshape(-1, width)
+    vec = pack(
+        (
+            query_bias,
+            value_bias,
+            out_bias,
+            first_gain,
+            first_shift,
+            outer_bias,
+            second_gain,
+            second_shift,
+            inner_bias,
+        ),
+        width,
     )
-    vec = jnp.pad(vec, ((0, -vec.shape[0] % 8), (0, 0)))
     own_index = narrow_index * n_wide + wide_index
     own_lengths = lax.dynamic_slice_in_dim(lengths, own_index * own_passages, own_passages, axis=1)
     lens = own_lengths.reshape(-1)
@@ -1245,22 +1503,19 @@
         grad_query, kept_q, vec, weights, 1, total, passage_rows, back_p, None, None
     )
     gp, go, gi, _, ga, sums_q = back_q[:6]
-    att_p = attention_back(ga, back_p[3], kept_p, weights, micro * own_passages, total, 0, None)
-    att_q = attention_back(ga, back_q[3], kept_q, weights, 1, total, passage_rows, att_p[0])
-    gqkv = att_q[0]
     part = width // n_wide
-    if part == 96 and n_narrow == 4 and act.shape[1] == 4 * width:
-        summed = weight_gradients(
-            (act, go, first_low, gi, x_passage, x_query, gqkv, ctx, ga, final_low, gp),
-            (back_p[5], sums_q, att_p[2], att_q[2]),
+    if part == 96 and n_narrow == 4 and micro * own_passages == 2 and act.shape[1] == 4 * width:
+        summed, grad_p, grad_q = backward_tail(
+            (act, go, first_low, gi, x_passage, x_query, ctx, ga, final_low, gp),
+            (*kept_p[:3], back_p[3], kept_p[3]),
+            (*kept_q[:3], back_q[3], kept_q[3]),
+            (out_weight, query_weight, key_weight, value_weight),
+            (back_p[5], sums_q),
             n_wide,
-        ).astype(F32)
-        r_outer = summed[:, :part].reshape(4 * part, width)
-        r_inner = summed[:, part : 2 * part].transpose(1, 0, 2).reshape(part, 4 * width)
-        r_q, r_k, r_v, r_out = (summed[index, 2 * part : 3 * part] for index in range(4))
-        thin = summed[0, 3 * part :].reshape(16, -1, embed_width)
-        r_linear = thin.transpose(1, 0, 2).reshape(part, embed_width)
-        vectors = summed[1, 3 * part :]
+        )
+        r_q, r_k, r_v, r_out, r_inner, r_outer, r_linear, vectors = unpack(
+            summed, part, embed_width
+        )
         own = lax.dynamic_slice_in_dim(vectors[:8], wide_index * part, part, axis=1)
         v_q, v_v, v_o, v_g1, v_s1, v_2, v_g2, v_s2 = (
             own[row] for row in (0, 1, ROW_BO, ROW_G1, ROW_S1, ROW_B2, ROW_G2, ROW_S2)
@@ -1269,6 +1524,11 @@
             vectors[ROW_BI : ROW_BI + 4].reshape(-1), wide_index * 4 * part, 4 * part
         )
     else:
+        att_p = attention_back(
+            ga, back_p[3], kept_p, weights, micro * own_passages, total, 0, None
+        )
+        att_q = attention_back(ga, back_q[3], kept_q, weights, 1, total, passage_rows, att_p[0])
+        gqkv, grad_p, grad_q = att_q[0], att_p[1], att_q[1]
 
         def reduce(value):
             piece = lax.psum_scatter(value.astype(BF16), everyone, scatter_dimension=0, tiled=True)
@@ -1295,8 +1555,8 @@
     return (
         scores,
         losses,
-        att_q[1].reshape(query_states.shape),
-        att_p[1].reshape(passage_states.shape),
+        grad_q.reshape(query_states.shape),
+        grad_p.reshape(passage_states.shape),
         r_q,
         v_q,
         r_k,

time: 370 us -> 318 us (0.86)
  Pallas kernels: 340 us -> 299 us
  local copies, waits for them, and re-layouts: 20.5 us -> 11.7 us
    pallas_call x3 -> x2, Pallas kernels: 184 us -> 147 us  [the longest x1 143 us: backward_tail(): pl.pallas_call(functools.partial(tail_kernel, n_z, part), out_shape=(jax....]
    unnamed x20 -> x11, local copies, waits for them, and re-layouts: 12.1 us -> 5.93 us
where the time goes in v3:
time: 318 us; the launch traced here: 317 us
  Pallas kernels  299 us (94%)
  local copies, waits for them, and re-layouts  11.7 us (4%)
  other arithmetic  5.3 us (2%)
    pallas_call x1, Pallas kernels, backward_tail(): pl.pallas_call(functools.partial(tail_kernel, n_z, part), out_shape=(jax....  143 us
    pallas_call x2, Pallas kernels, encode(): pl.pallas_call(functools.partial(fwd_kernel, grouped, len(aliased), sizes...  76.2 us
    pallas_call x2, Pallas kernels, mlp_back(): pl.pallas_call(functools.partial(mlp_back_kernel, len(aliased), sizes), o...  42.4 us
    pallas_call x1, Pallas kernels, similarity_back(): pl.pallas_call(sims_back_kernel, out_shape=(jax.ShapeDtypeStruct((micro,...  13.8 us
    pallas_call x1, Pallas kernels, similarity(): pl.pallas_call(sims_kernel, out_shape=(jax.ShapeDtypeStruct((micro, slots...  10.1 us
    pallas_call x1, Pallas kernels, share_scores(): pl.pallas_call(functools.partial(share_kernel, n_wide, n_narrow), out_sha...  9.36 us

profile of v3, /device:TPU:0, one launch (start us, length us, event | category | flops | bytes accessed | tf_op | source)
XLA Modules:
  0.0 316.5 jit_solution(15343723281575070355)
XLA Ops:
  0.7 0.0 copy-start
  0.7 0.7 copy-done
  1.3 0.7 dynamic-slice_reduce_fusion.refs_0_.lens_ref
  2.0 0.8 convert_add_fusion
  2.9 0.6 reshape.83.refs_2_.refs_8_
  3.5 18.8 %encode_queries.1 = (bf16[256,768]{1,0:T(8,128)(2,1)}, bf16[256,768]{1,0:T(8,128)(2,1)}, bf16[256,768]{1,0:T(8,128)(2,1)}, bf16[1,12,256,256]{3,2,1,0:T(8,128)(2...) custom-call(s32[2]{0:T(128)} %dynamic-slice_reduce_fusion.refs_0_.le, ...), custom_call_target="tpu_custom_call" | custom-call | tf_op jit(solution)/shard_map/encode_queries/pallas_call | solution.py:376
  22.3 57.4 %encode_passages.1 = (bf16[1024,768]{1,0:T(8,128)(2,1)}, bf16[1024,768]{1,0:T(8,128)(2,1)}, bf16[1024,768]{1,0:T(8,128)(2,1)}, bf16[2,12,512,512]{3,2,1,0:T(8,12...) custom-call(s32[2]{0:T(128)} %dynamic-slice_reduce_fusion.refs_0_.le, ...), custom_call_target="tpu_custom_call", output_to_operand_aliasing={{4}: (10, {}), {7}: (11, {}), {8}: (12, {}), {12}: (13, {})} | custom-call | tf_op jit(solution)/shard_map/encode_passages/pallas_call | solution.py:376
  79.7 0.0 copy-start.3
  79.8 10.1 %similarity.1 = (bf16[2,512,4096]{2,1,0:T(8,128)(2,1)}, f32[2,32,128]{2,1,0:T(8,128)}) custom-call(s32[2]{0:T(128)} %dynamic-slice_reduce_fusion.refs_0_.lens_ref, bf16[32,2,128,128]{3,2,1,0:T(8,128)(2,1)} %bitcast.28, bf16[2,512,128]{2,1,0:T(8,128)(2,1)} %bitcast.36), custom_call_target="tpu_custom_call" | custom-call | tf_op jit(solution)/shard_map/similarity/pallas_call | solution.py:435
  89.8 0.8 log_add_fusion
  90.6 0.1 reshape.87
  90.7 0.1 reduce_sum.27
  90.8 0.6 broadcast_multiply_fusion.own_ref
  91.4 9.4 %share_scores.1 = f32[32,2,128]{2,1,0:T(2,128)} custom-call(f32[2,128]{1,0:T(2,128)} %broadcast_multiply_fusion.own_ref), custom_call_target="tpu_custom_call" | custom-call | tf_op jit(solution)/shard_map/share_scores/pallas_call | solution.py:770
  100.7 0.8 dynamic-slice_bitcast_fusion
  101.5 0.6 copy.50
  102.1 0.8 reduce_max.9
  102.9 0.0 copy-done.3
  102.9 0.8 exponential_reduce_fusion
  103.8 0.6 constant_dynamic-slice_fusion.1
  104.4 0.1 broadcast_in_dim.15
  104.5 0.1 reshape_reshape.3
  104.6 1.4 div.11.w_ref
  106.0 13.8 %similarity_back.1 = (f32[2,512,128]{2,1,0:T(8,128)}, bf16[32,2,128,128]{3,2,1,0:T(8,128)(2,1)}) custom-call(bf16[2,512,4096]{2,1,0:T(8,128)(2,1)} %get-tuple-element.90.e_ref, f32[2,32,128]{2,1,0:T(8,128)} %div.11.w_ref, bf16[32,2,128,128]{3,2,1,0:T(8,128)(2,1)} %bitcast.29, bf16[2,512,128]{2,1,0:T(8,128)(2,1)} %bitcast.37), custom_call_target="tpu_custom_call" | custom-call | tf_op jit(solution)/shard_map/similarity_back/pallas_call | solution.py:463
  119.7 31.4 %mlp_back_passages.1 = (bf16[1280,128]{1,0:T(8,128)(2,1)}, bf16[1280,768]{1,0:T(8,128)(2,1)}, bf16[1280,3072]{1,0:T(8,128)(2,1)}, f32[1024,768]{1,0:T(8,128)}, b...) custom-call(f32[1024,128]{1,0:T(8,128)} %bitcast.39, f32[1024,128]{1,0:T(8,128)} %get-tuple-element.92.refs_1_, ...), custom_call_target="tpu_custom_call" | custom-call | tf_op jit(solution)/shard_map/mlp_back_passages/pallas_call | solution.py:602
  151.2 11.0 %mlp_back_queries.1 = (bf16[1280,128]{1,0:T(8,128)(2,1)}, bf16[1280,768]{1,0:T(8,128)(2,1)}, bf16[1280,3072]{1,0:T(8,128)(2,1)}, f32[256,768]{1,0:T(8,128)}, bf1...) custom-call(f32[256,128]{1,0:T(8,128)} %get-tuple-element.100.refs_0, ...), custom_call_target="tpu_custom_call", output_to_operand_aliasing={{0}: (12, {}), {1}: (13, {}), {2}: (14, {}), {4}: (15, {})} | custom-call | tf_op jit(solution)/shard_map/mlp_back_queries/pallas_call | solution.py:602
  162.2 143.5 %backward_tail.1 = (bf16[4,304,768]{2,1,0:T(8,128)(2,1)}, f32[1024,768]{1,0:T(8,128)}, f32[256,768]{1,0:T(8,128)}) custom-call(bf16[1280,3072]{1,0:T(8,128)(2,1)} %get-tuple-element.89.refs_0_, bf16[1280,768]{1,0:T(8,128)(2,1)} %get-tuple-element.112.refs_1_, bf16[1280,768]{1,0:T(8,128)(2,1)} %get-tuple-element.113.refs_2_, ...), custom_call_target="tpu_custom_call" | custom-call | tf_op jit(solution)/shard_map/backward_tail/pallas_call | solution.py:1314
  305.7 0.0 copy-start.2
  305.7 3.4 %unpack_gradients.1 = (f32[96,768]{1,0:T(8,128)}, f32[96,768]{1,0:T(8,128)}, f32[96,768]{1,0:T(8,128)}, f32[96,768]{1,0:T(8,128)}, f32[96,3072]{1,0:T(8,128)}, /...) custom-call(bf16[4,304,768]{2,1,0:T(8,128)(2,1)} %get-tuple-element.133.sums_ref), custom_call_target="tpu_custom_call" | custom-call | tf_op jit(solution)/shard_map/unpack_gradients/pallas_call | solution.py:1382
  309.1 0.7 slice.30
  309.8 0.1 constant_dynamic-slice_fusion
  309.9 0.5 slice_bitcast_fusion
  310.5 0.7 slice.36
  311.2 0.7 dynamic_slice.19
  311.9 0.0 copy-done.2
  311.9 0.0 copy-start.1
  311.9 0.9 copy.62
  312.8 3.8 %copy.63 = f32[2,1,512,768]{3,2,1,0:T(8,128)} copy(f32[2,1,512,768]{3,2,1,0:T(8,128)} %bitcast.32) | data formatting | bytes 6291456
  316.5 0.0 copy-done.1
  (3 shorter events, 0.0 us)
Async XLA Ops:
  0.7 0.7 copy-start
  79.7 23.2 %copy-start.3 = (s32[2,128]{1,0:T(2,128)S(1)}, s32[2,128]{1,0:T(2,128)}, u32[]{:S(2)}) copy-start(s32[2,128]{1,0:T(2,128)} %param.23) | copy-start | bytes 3076
  305.7 6.2 %copy-start.2 = (f32[256,768]{1,0:T(8,128)S(1)}, f32[256,768]{1,0:T(8,128)}, u32[]{:S(2)}) copy-start(f32[256,768]{1,0:T(8,128)} %get-tuple-element.131) | copy-start | bytes 2359300
  311.9 4.6 %copy-start.1 = (s32[2,32]{1,0:T(2,128)S(1)}, s32[2,32]{1,0:T(2,128)}, u32[]{:S(2)}) copy-start(s32[2,32]{1,0:T(2,128)} %param.22) | copy-start | bytes 772

commit v4 on v3

--- a/solution.py
+++ b/solution.py
@@ -192,6 +192,45 @@
 
         self.chips.loop(collect)
         self.pair_copy().wait_send()
+
+
+class Push:
+    def __init__(self, chips, half, out, scratch):
+        self.chips, self.half, self.out = chips, half, out
+        self.inbox, self.far, self.own = scratch[0], scratch[1:3], scratch[3]
+
+    def far_copy(self, step):
+        chip = self.chips.at(step)
+        return remote(
+            self.half.at[chip], self.inbox.at[step], self.far, step, self.chips.device(chip)
+        )
+
+    def own_copy(self):
+        return pltpu.make_async_copy(
+            self.half.at[self.chips.me], self.inbox.at[0], self.own.at[0]
+        )
+
+    def start(self):
+        self.own_copy().start()
+        self.chips.barrier()
+        self.chips.loop(lambda step: self.far_copy(step).start())
+
+    def finish(self):
+        self.own_copy().wait()
+        self.out[...] = self.inbox[0].astype(F32)
+
+        def collect(step):
+            copy = self.far_copy(step)
+            copy.wait_recv()
+            copy.wait_send()
+            self.out[...] += self.inbox[step].astype(F32)
+
+        self.chips.loop(collect)
+
+
+def push_scratch(chips, rows, width):
+    sem = pltpu.SemaphoreType.DMA
+    return [pltpu.VMEM((chips, rows, width), BF16), sem((chips,)), sem((chips,)), sem((1,))]
 
 
 def exchange_scratch(chips, rows, width):
@@ -482,6 +521,161 @@
     )(e, weights, queries, passages)
 
 
+def match_kernel(n_wide, n_narrow, group, query_len, *refs):
+    lens_ref, q_ref, p_ref, pos_ref = refs[:4]
+    all_ref, loss_ref, gp_ref, half_ref = refs[4:8]
+    e_buf, z_buf, own_buf, grad_buf, near, share_send, share_recv, pair_send, pair_recv = refs[8:]
+    devices, micro, tokens, width = q_ref.shape
+    chips = Chips(n_wide, n_narrow)
+    me = chips.narrow * n_wide + chips.wide
+    share_sems, pair_sems = (share_send, share_recv), (pair_send, pair_recv)
+    pairs = group // 2
+
+    def device(index):
+        return (lax.rem(index, n_wide), index // n_wide)
+
+    def each(body):
+        def step_body(step, carry):
+            body(step)
+            return carry
+
+        lax.fori_loop(1, devices, step_body, 0)
+
+    barrier = pltpu.get_barrier_semaphore()
+    each(
+        lambda step: pl.semaphore_signal(
+            barrier, inc=1, device_id=device(lax.rem(me + step, devices)), device_id_type=MESH
+        )
+    )
+
+    def query_rows(block, m):
+        at = pl.ds(block * group, group)
+        return q_ref[at, m].reshape(group * tokens, width)
+
+    def forward(block, carry):
+        for m in range(micro):
+            sims = mm(p_ref[m], query_rows(block, m), NT)
+            slot = lax.broadcasted_iota(jnp.int32, sims.shape, 0)
+            e = jnp.where(slot < lens_ref[m], jnp.exp(SHARP * sims - SHARP), 0.0)
+            e_buf[m, block] = e.astype(BF16)
+            z = jnp.sum(e, axis=0, keepdims=True)
+            for index in range(group):
+                z_buf[m, pl.ds(block * group + index, 1)] = z[
+                    :, index * tokens : (index + 1) * tokens
+                ]
+        return carry
+
+    lax.fori_loop(0, devices // group, forward, 0)
+    pl.semaphore_wait(barrier, devices - 1)
+    best = SHARP + jnp.log(z_buf[...].reshape(micro * devices, tokens))
+    member = (
+        lax.broadcasted_iota(jnp.int32, (8, tokens), 0)
+        == lax.broadcasted_iota(jnp.int32, (8, tokens), 1) // query_len
+    ).astype(F32)
+    own = (
+        lax.dot_general(
+            member, best, NT, precision=lax.Precision.HIGHEST, preferred_element_type=F32
+        )
+        / SHARP
+    )
+    own_buf[...] = own
+    all_ref[me] = own
+
+    def share(step, source):
+        target = device(lax.rem(me + step, devices))
+        return remote(own_buf, all_ref.at[source], share_sems, step, target)
+
+    each(lambda step: share(step, me).start())
+    each(lambda step: share(step, lax.rem(me - step + devices, devices)).wait_recv())
+    each(lambda step: share(step, me).wait_send())
+    full = all_ref[...]
+    peak = jnp.max(full, axis=0)
+    total = peak + jnp.log(jnp.sum(jnp.exp(full - peak[None]), axis=0))
+    positive = pos_ref[...]
+    passage = lax.broadcasted_iota(jnp.int32, full.shape, 0)
+    picked = jnp.sum(jnp.where(passage == positive[None], full, 0.0), axis=0)
+    loss_ref[...] = total - picked
+    grads = jnp.exp(own - total) - (positive == me).astype(F32)
+    spread = lax.dot_general(
+        grads, member, TN, precision=lax.Precision.HIGHEST, preferred_element_type=F32
+    )
+    z_buf[...] = (spread / z_buf[...].reshape(micro * devices, tokens)).reshape(z_buf.shape)
+    gp_ref[...] = jnp.zeros_like(gp_ref)
+
+    def pair_copy(block):
+        at = pl.ds(block * pairs, pairs)
+        return remote(
+            grad_buf.at[at, 1 - chips.core], near.at[at], pair_sems, block, chips.mate
+        )
+
+    def backward(block, carry):
+        for m in range(micro):
+            weight = jnp.concatenate(
+                [z_buf[m, pl.ds(block * group + index, 1)] for index in range(group)], axis=1
+            )
+            grads = (e_buf[m, block].astype(F32) * weight).astype(BF16)
+            gp_ref[m] += mm(grads, query_rows(block, m))
+            part = mm(grads, p_ref[m], TN).astype(BF16)
+            for index in range(group):
+                grad_buf[block * pairs + index // 2, index % 2, m * tokens : (m + 1) * tokens] = (
+                    part[index * tokens : (index + 1) * tokens]
+                )
+        pair_copy(block).start()
+        return carry
+
+    lax.fori_loop(0, devices // group, backward, 0)
+
+    def join(block, carry):
+        copy = pair_copy(block)
+        copy.wait_recv()
+        copy.wait_send()
+        at = pl.ds(block * pairs, pairs)
+        half_ref[at] = (
+            grad_buf[at, chips.core].astype(F32) + near[at].astype(F32)
+        ).astype(BF16)
+        return carry
+
+    lax.fori_loop(0, devices // group, join, 0)
+
+
+def match(queries, passages, lens, positives, n_wide, n_narrow, query_len):
+    devices, micro, tokens, width = queries.shape
+    slots = passages.shape[1]
+    group = 8
+    own = tokens // query_len
+    placed = positives.reshape(micro, devices, own).transpose(2, 0, 1).reshape(own, -1)
+    placed = jnp.pad(placed, ((0, 8 - own), (0, 0)))
+    sem = pltpu.SemaphoreType.DMA
+    vmem = pl.BlockSpec(memory_space=pltpu.VMEM)
+    columns = micro * devices
+    return pl.pallas_call(
+        functools.partial(match_kernel, n_wide, n_narrow, group, query_len),
+        out_shape=(
+            jax.ShapeDtypeStruct((devices, 8, columns), F32),
+            jax.ShapeDtypeStruct((8, columns), F32),
+            jax.ShapeDtypeStruct((micro, slots, width), F32),
+            jax.ShapeDtypeStruct((devices // 2, micro * tokens, width), BF16),
+        ),
+        in_specs=[pl.BlockSpec(memory_space=pltpu.SMEM), vmem, vmem, vmem],
+        out_specs=(vmem,) * 4,
+        scratch_shapes=[
+            pltpu.VMEM((micro, devices // group, slots, group * tokens), BF16),
+            pltpu.VMEM((micro, devices, tokens), F32),
+            pltpu.VMEM((8, columns), F32),
+            pltpu.VMEM((devices // 2, 2, micro * tokens, width), BF16),
+            pltpu.VMEM((devices // 2, micro * tokens, width), BF16),
+            sem((devices,)),
+            sem((devices,)),
+            sem((devices // group,)),
+            sem((devices // group,)),
+        ],
+        compiler_params=pltpu.CompilerParams(
+            collective_id=1, has_side_effects=True, vmem_limit_bytes=VMEM_LIMIT
+        ),
+        name="match",
+    )(lens, queries, passages, placed)
+
+
 def accumulate(ref, row, value):
     ref[row : row + 1, :] += jnp.sum(value, axis=0, keepdims=True)
 
@@ -502,8 +696,8 @@
     refs = refs[12 + alias_count :]
     swap = None
     if sizes:
-        swap = Exchange(Chips(*sizes), refs[0], refs[7], refs[-8:])
-        refs = refs[1:7] + refs[8:-8]
+        swap = Push(Chips(*sizes), refs[0], refs[7], refs[-4:])
+        refs = refs[1:7] + refs[8:-4]
     gp_ref, go_ref, gi_ref, gh_ref, ga_ref, sums_ref = refs[:6]
     wl, w2, wi, sem, acc_ref = refs[6:]
     loader = Loader(sources, (wl, w2, wi), sem)
@@ -532,8 +726,6 @@
     go_ref[...] = outer_low
     accumulate(sums_ref, ROW_B2, outer_low.astype(F32))
     acc_ref[...] = grad_second
-    if swap:
-        pl.when(loader.first)(swap.push)
     loader.need(1, 2)
     width = go_ref.shape[1]
 
@@ -595,10 +787,10 @@
     sends, scratch, params = [], [], {}
     if sizes:
         sends = [sent]
-        out_shapes.append(jax.ShapeDtypeStruct(sent.shape[2:], F32))
-        out_specs.append(pl.BlockSpec(sent.shape[2:], lambda i: (0, 0)))
-        scratch = exchange_scratch(sent.shape[0], *sent.shape[2:])
-        params = {"collective_id": 2, "has_side_effects": True}
+        out_shapes.append(jax.ShapeDtypeStruct(sent.shape[1:], F32))
+        out_specs.append(pl.BlockSpec(sent.shape[1:], lambda i: (0, 0)))
+        scratch = push_scratch(*sent.shape)
+        params = {"collective_id": 5, "has_side_effects": True}
     return pl.pallas_call(
         functools.partial(mlp_back_kernel, len(aliased), sizes),
         out_shape=out_shapes,
@@ -815,6 +1007,7 @@
 EARLY = (0, 1, 2, 3)
 LATE = (4, 5, 6, 7, 8, 9)
 SHARE_ROWS = 304
+LATE_B = 240
 ROWS_A, ROWS_B = 144, 160
 TILES = 9
 
@@ -837,7 +1030,6 @@
     mate = (wide, y * 2 + 1 - core)
     over_y = (wide, (1 - y) * 2 + core)
     over_x = (z * 2 + 1 - x, narrow)
-    right, left = (wide + 2, narrow), (wide - 2, narrow)
     total, width = go.shape
     p_rows = x_p.shape[0]
     held = both.at[core]
@@ -874,6 +1066,17 @@
         rows = rows_of(unit)
         return remote(
             both.at[1 - core, :, :, :, rows], near.at[:, :, :, rows], core_sems, unit, mate
+        )
+
+    def late_copy(index):
+        row_y, start, count = ((0, 2 * part, part + 16), (1, LATE_B, 64), (1, 2 * part, 48))[index]
+        rows = pl.ds(start, count)
+        return remote(
+            both.at[1 - core, row_y, :, :, rows],
+            near.at[row_y, :, :, rows],
+            core_sems,
+            len(EARLY) + index,
+            mate,
         )
 
     def one_copy(unit):
@@ -914,15 +1117,15 @@
             over_y,
         )
 
-    def line_copy(unit, target, way):
+    def far_copy(unit, step):
         rows = rows_of(unit)
-        index = (unit * n_z + target) * 2 + way
+        target = lax.rem(z + step, n_z)
         return remote(
             held.at[y, target, x, rows],
-            line.at[way, target, rows],
+            line.at[step - 1, rows],
             line_sems,
-            index,
-            right if way == 0 else left,
+            unit * n_z + step,
+            (target * 2 + x, narrow),
         )
 
     def share_copy(unit, step, arriving):
@@ -943,7 +1146,8 @@
 
     def start_one(unit):
         rows = rows_of(unit)
-        core_copy(unit).wait_recv()
+        if unit in EARLY:
+            core_copy(unit).wait_recv()
 
         def body(index, carry):
             row_y, rest = index // (n_z * 2), lax.rem(index, n_z * 2)
@@ -976,43 +1180,25 @@
         lax.fori_loop(0, 2 * n_z, body, 0)
         two_copy(unit).start()
 
-    def line_phase(phase):
-        def run(unit):
-            rows = rows_of(unit)
-            place = place_of(unit)
-            extra = then_a if unit % 2 == 0 else then_b
-
-            def body(index, carry):
-                add(held.at[y, index, x, rows], extra.at[index, place])
-                return carry
-
-            if phase == 0:
-                two_copy(unit).wait_recv()
-                lax.fori_loop(0, n_z, body, 0)
-            for way, at in ((0, phase), (1, n_z - 1 - phase)):
-
-                @pl.when(z == at)
-                def _(way=way, at=at):
-                    for target in range(n_z - 1, at, -1) if way == 0 else range(at):
-                        copy = line_copy(unit, target, way)
-                        if phase > 0:
-                            copy.wait_recv()
-                            add(held.at[y, target, x, rows], line.at[way, target, rows])
-                        copy.start()
-
-        return run
+    def start_far(unit):
+        rows = rows_of(unit)
+        place = place_of(unit)
+        extra = then_a if unit % 2 == 0 else then_b
+        two_copy(unit).wait_recv()
+
+        def body(index, carry):
+            add(held.at[y, index, x, rows], extra.at[index, place])
+            return carry
+
+        lax.fori_loop(0, n_z, body, 0)
+        for step in range(1, n_z):
+            far_copy(unit, step).start()
 
     def start_share(unit):
         rows = rows_of(unit)
-        for target in range(n_z):
-
-            @pl.when(z == target)
-            def _(target=target):
-                for way in range(2):
-                    if target > 0 if way == 0 else target < n_z - 1:
-                        line_copy(unit, target, way).wait_recv()
-                        add(held.at[y, target, x, rows], line.at[way, target, rows])
-
+        for step in range(1, n_z):
+            far_copy(unit, step).wait_recv()
+            add(held.at[y, z, x, rows], line.at[step - 1, rows])
         out_ref[narrow, rows] = both[core, y, z, x, rows]
         share_copy(unit, 1, False).start()
         share_copy(unit, 0, False).start()
@@ -1026,29 +1212,21 @@
         share_copy(unit, 2, True).wait_recv()
         for step in range(3):
             share_copy(unit, step, False).wait_send()
-        core_copy(unit).wait_send()
+        if unit in EARLY:
+            core_copy(unit).wait_send()
         one_copy(unit).wait_send()
         two_copy(unit).wait_send()
-        for target in range(n_z):
-            for way in range(2):
-                pl.when(z < target if way == 0 else z > target)(
-                    line_copy(unit, target, way).wait_send
-                )
+        for step in range(1, n_z):
+            far_copy(unit, step).wait_send()
 
     barrier = pltpu.get_barrier_semaphore()
     load(0, False)
-    for device in (mate, over_y, over_x):
+    partners = [mate, over_y, over_x] + [
+        (lax.rem(z + step, n_z) * 2 + x, narrow) for step in range(1, n_z)
+    ]
+    for device in partners:
         pl.semaphore_signal(barrier, inc=1, device_id=device, device_id_type=MESH)
-
-    @pl.when(z < n_z - 1)
-    def _():
-        pl.semaphore_signal(barrier, inc=1, device_id=right, device_id_type=MESH)
-
-    @pl.when(z > 0)
-    def _():
-        pl.semaphore_signal(barrier, inc=1, device_id=left, device_id_type=MESH)
-
-    pl.semaphore_wait(barrier, jnp.where(jnp.logical_and(z > 0, z < n_z - 1), 5, 4))
+    pl.semaphore_wait(barrier, len(partners))
 
     def put(kind, owner, half, made):
         rows = pl.ds(pl.multiple_of(kind * part, part), part)
@@ -1092,7 +1270,13 @@
 
         halves(left_buf.at[slot], right_buf.at[slot], store)
         hooks(
-            tile, ((3, start_core, (0, 1)), (6, start_one, (0, 1)), (7, start_core, (2, 3)))
+            tile,
+            (
+                (3, start_core, (0, 1)),
+                (5, start_one, (0,)),
+                (6, start_one, (1,)),
+                (7, start_core, (2, 3)),
+            ),
         )
         return carry
 
@@ -1224,23 +1408,17 @@
             ]
     for copy in weight_copies():
         copy.wait()
-    for unit in (2, 3):
-        start_one(unit)
-    line_a, line_b, line_c = (line_phase(phase) for phase in range(3))
     for copy in block_copies(1):
         copy.start()
-    attention(0, ((1, start_two, (0, 1)),))
+    attention(0, ((0, start_one, (2, 3)), (3, start_two, (0, 1))))
     for copy in block_copies(2):
         copy.start()
     attention(
         1,
         (
-            (0, start_two, (2, 3)),
-            (1, line_a, (0, 1)),
-            (2, line_b, (0, 1)),
-            (3, line_c, (0, 1)),
-            (4, line_a, (2, 3)),
-            (5, line_b, (2, 3)),
+            (0, start_far, (0, 1)),
+            (2, start_two, (2, 3)),
+            (5, start_far, (2, 3)),
         ),
     )
     x_copies = [
@@ -1251,15 +1429,7 @@
     ]
     for copy in x_copies:
         copy.start()
-    attention(2, ((1, line_c, (2, 3)), (4, start_share, EARLY)))
-    for copy in x_copies:
-        copy.wait()
-
-    def late_body(tile, carry):
-        halves(right_buf.at[0], grads.at[tile], lambda half, made: put(2, tile, half, made))
-        return carry
-
-    lax.fori_loop(0, 3, late_body, 0)
+    attention(2, ((2, start_share, (0, 1)),))
     top = sums[0][:8] + sums[1][:8] + att_sums[...]
     tail = jnp.concatenate([top, sums[0][8:] + sums[1][8:]], axis=0).astype(BF16)
     for shard in range(2 * n_z):
@@ -1267,35 +1437,51 @@
         both[1, 0, at_z, at_x, last] = tail
         both[0, 1, at_z, at_x, last] = jnp.zeros_like(tail)
         both[1, 1, at_z, at_x, last] = jnp.zeros_like(tail)
+    for copy in x_copies:
+        copy.wait()
+
+    def late_body(tile, carry):
+        halves(right_buf.at[0], grads.at[tile], lambda half, made: put(2, tile, half, made))
+        pl.when(tile == 1)(lambda: late_copy(0).start())
+        return carry
+
+    lax.fori_loop(0, 3, late_body, 0)
+
+    def start_late(index):
+        late_copy(index).start()
+
+    def wait_late(index):
+        late_copy(index).wait_recv()
+
+    def end_late(index):
+        late_copy(index).wait_send()
+
     for step, units in (
-        (start_core, LATE),
+        (start_late, (1, 2)),
+        (start_share, (2, 3)),
+        (wait_late, (0, 1)),
+        (start_one, (5, 7, 9)),
+        (wait_late, (2,)),
+        (start_one, (4, 6, 8)),
         (forward, EARLY),
-        (start_one, LATE),
         (states, (0,)),
-        (start_two, (4, 5)),
+        (start_two, (5, 4)),
         (states, (1,)),
-        (start_two, (6, 7)),
-        (line_a, (4, 5)),
+        (start_two, (7, 6)),
+        (start_far, (5, 4)),
         (states, (2,)),
-        (line_b, (4, 5)),
         (start_two, (8,)),
-        (line_c, (4, 5)),
-        (line_a, (6,)),
+        (start_far, (7, 6)),
         (start_two, (9,)),
-        (line_a, (7,)),
-        (line_b, (6, 7)),
-        (start_share, (4, 5)),
-        (line_c, (6, 7)),
-        (line_a, (8,)),
-        (line_b, (8,)),
-        (line_a, (9,)),
-        (line_c, (8,)),
-        (line_b, (9,)),
-        (start_share, (6, 7)),
-        (line_c, (9,)),
-        (start_share, (8, 9)),
-        (forward, LATE),
+        (start_far, (8,)),
+        (start_share, (5, 4)),
+        (start_far, (9,)),
+        (start_share, (7, 6, 8)),
+        (forward, (5, 4, 7, 6)),
+        (start_share, (9,)),
+        (forward, (8, 9)),
         (finish, EARLY + LATE),
+        (end_late, (0, 1, 2)),
         (lambda block: gx_copy(block).wait(), range(len(blocks))),
     ):
         for unit in units:
@@ -1327,7 +1513,7 @@
             pltpu.VMEM((2, n_z, ROWS_B, width), BF16),
             pltpu.VMEM((n_z, ROWS_A, width), BF16),
             pltpu.VMEM((n_z, ROWS_B, width), BF16),
-            pltpu.VMEM((2, n_z, SHARE_ROWS, width), BF16),
+            pltpu.VMEM((n_z - 1, SHARE_ROWS, width), BF16),
             pltpu.VMEM((2, total, width), BF16),
             pltpu.VMEM((2, total, width), BF16),
             pltpu.VMEM(gp.shape, BF16),
@@ -1346,7 +1532,7 @@
             sem((3,)),
         ]
         + [sem((units,))] * 6
-        + [sem((units * n_z * 2,))] * 2
+        + [sem((units * n_z,))] * 2
         + [sem((units * 3,))] * 2,
         compiler_params=pltpu.CompilerParams(
             collective_id=3, has_side_effects=True, vmem_limit_bytes=VMEM_LIMIT
@@ -1463,29 +1649,50 @@
     queries = kept_p[16].reshape(n_wide * n_narrow, micro, -1, embed_width)
     ctx, first_low, act, final_low = (kept_p[index] for index in (4, 7, 8, 12))
     passages = kept_p[15].reshape(micro * own_passages, slots, embed_width)
-    e, z = similarity(queries, passages, lens)
-    best = SHARP + jnp.log(z)
-    own_scores = jnp.sum(best.reshape(micro, -1, query_len), axis=-1) / SHARP
-    full = share_scores(own_scores, n_wide, n_narrow)
-    row_total = jax.nn.logsumexp(full, axis=0)
-    passage_ids = jnp.arange(full.shape[0], dtype=jnp.int32)
-    picked = jnp.sum(
-        jnp.where(passage_ids[:, None, None] == positives[None], full, 0.0), axis=0
-    )
     row_count = own_queries * n_narrow
-    losses = lax.dynamic_slice_in_dim(row_total - picked, wide_index * row_count, row_count, axis=1)
-    block = lax.dynamic_slice(
-        full,
-        (narrow_index * n_wide, 0, wide_index * row_count),
-        (n_wide, micro, row_count),
-    )
-    scores = jnp.transpose(block, (1, 2, 0))
-    grads = jnp.exp(own_scores - row_total) - (positives == own_index).astype(F32)
-    token_weights = jnp.repeat(grads, query_len, axis=1).reshape(z.shape) / z
-    grad_passage, grad_query = similarity_back(e, token_weights, queries, passages)
-    grad_query = grad_query.reshape(-1, 2, query_rows, embed_width)
+    together = queries.size * slots <= 8 * 1024 * 1024 * embed_width
+    if together:
+        full, loss, grad_passage, grad_query = match(
+            queries, passages, lens, positives, n_wide, n_narrow, query_len
+        )
+        block = lax.dynamic_slice_in_dim(full, narrow_index * n_wide, n_wide, axis=0)
+        block = lax.dynamic_slice_in_dim(
+            block[:, :own_queries].reshape(n_wide, own_queries, micro, -1),
+            wide_index * n_narrow,
+            n_narrow,
+            axis=3,
+        )
+        scores = block.transpose(2, 3, 1, 0).reshape(micro, row_count, n_wide)
+        losses = lax.dynamic_slice_in_dim(
+            loss[:own_queries].reshape(own_queries, micro, -1),
+            wide_index * n_narrow,
+            n_narrow,
+            axis=2,
+        )
+        losses = losses.transpose(1, 2, 0).reshape(micro, row_count)
+    else:
+        e, z = similarity(queries, passages, lens)
+        best = SHARP + jnp.log(z)
+        own_scores = jnp.sum(best.reshape(micro, -1, query_len), axis=-1) / SHARP
+        full = share_scores(own_scores, n_wide, n_narrow)
+        row_total = jax.nn.logsumexp(full, axis=0)
+        passage_ids = jnp.arange(full.shape[0], dtype=jnp.int32)
+        picked = jnp.sum(
+            jnp.where(passage_ids[:, None, None] == positives[None], full, 0.0), axis=0
+        )
+        row_count = own_queries * n_narrow
+        losses = lax.dynamic_slice_in_dim(row_total - picked, wide_index * row_count, row_count, axis=1)
+        block = lax.dynamic_slice(
+            full,
+            (narrow_index * n_wide, 0, wide_index * row_count),
+            (n_wide, micro, row_count),
+        )
+        scores = jnp.transpose(block, (1, 2, 0))
+        grads = jnp.exp(own_scores - row_total) - (positives == own_index).astype(F32)
+        token_weights = jnp.repeat(grads, query_len, axis=1).reshape(z.shape) / z
+        grad_passage, grad_query = similarity_back(e, token_weights, queries, passages)
+        grad_query = grad_query.reshape(-1, 2, query_rows, embed_width)
     grad_passage = grad_passage.reshape(passage_rows, embed_width)
-    together = grad_query.size <= 4 * total * width
     back_p = mlp_back(
         grad_passage,
         kept_p,

time: 318 us -> 286 us (0.90)
  Pallas kernels: 299 us -> 270 us
  other arithmetic: 5.3 us -> 0.82 us
    pallas_call x3 -> x1, Pallas kernels: 33.2 us -> 19.9 us  [match(): pl.pallas_call(functools.partial(match_kernel, n_wide, n_narrow, group, q...]
    pallas_call x1, Pallas kernels: 143 us -> 131 us  [backward_tail(): pl.pallas_call(functools.partial(tail_kernel, n_z, part), out_shape=(jax....]
where the time goes in v4:
time: 286 us; the launch traced here: 285 us
  Pallas kernels  270 us (94%)
  local copies, waits for them, and re-layouts  13.2 us (5%)
    pallas_call x1, Pallas kernels, backward_tail(): pl.pallas_call(functools.partial(tail_kernel, n_z, part), out_shape=(jax....  131 us
    pallas_call x2, Pallas kernels, encode(): pl.pallas_call(functools.partial(fwd_kernel, grouped, len(aliased), sizes...  76.2 us
    pallas_call x2, Pallas kernels, mlp_back(): pl.pallas_call(functools.partial(mlp_back_kernel, len(aliased), sizes), o...  40 us
    pallas_call x1, Pallas kernels, match(): pl.pallas_call(functools.partial(match_kernel, n_wide, n_narrow, group, q...  19.9 us
    unnamed x11, local copies, waits for them, and re-layouts  5.99 us

profile of v4, /device:TPU:0, one launch (start us, length us, event | category | flops | bytes accessed | tf_op | source)
XLA Modules:
  0.0 285.0 jit_solution(225668178813636623)
XLA Ops:
  0.7 0.0 copy-start
  0.7 0.7 copy-done
  1.3 0.7 fusion.refs_0_
  2.0 0.8 convert_add_fusion
  2.9 0.6 reshape.90.refs_2_.refs_8_
  3.5 18.8 %encode_queries.1 = (bf16[256,768]{1,0:T(8,128)(2,1)}, bf16[256,768]{1,0:T(8,128)(2,1)}, bf16[256,768]{1,0:T(8,128)(2,1)}, bf16[1,12,256,256]{3,2,1,0:T(8,128)(2...) custom-call(s32[2]{0:T(128)} %fusion.refs_0_, ...), custom_call_target="tpu_custom_call" | custom-call | tf_op jit(solution)/shard_map/encode_queries/pallas_call | solution.py:415
  22.3 0.0 copy-start.3
  22.3 57.4 %encode_passages.1 = (bf16[1024,768]{1,0:T(8,128)(2,1)}, bf16[1024,768]{1,0:T(8,128)(2,1)}, bf16[1024,768]{1,0:T(8,128)(2,1)}, bf16[2,12,512,512]{3,2,1,0:T(8,12...) custom-call(s32[2]{0:T(128)} %fusion.refs_0_, ...), custom_call_target="tpu_custom_call", output_to_operand_aliasing={{4}: (10, {}), {7}: (11, {}), {8}: (12, {}), {12}: (13, {})} | custom-call | tf_op jit(solution)/shard_map/encode_passages/pallas_call | solution.py:415
  79.7 0.0 copy-done.3
  79.7 0.1 reshape.94
  79.8 0.1 copy.57
  79.9 0.6 pad.85.refs_3_
  80.5 19.9 %match.1 = (f32[32,8,64]{2,1,0:T(8,128)}, f32[8,64]{1,0:T(8,128)}, f32[2,512,128]{2,1,0:T(8,128)}, bf16[16,256,128]{2,1,0:T(8,128)(2,1)}) custom-call(s32[2]{0:T(128)} %fusion.refs_0_, bf16[32,2,128,128]{3,2,1,0:T(8,128)(2,1)} %bitcast.38, bf16[2,512,128]{2,1,0:T(8,128)(2,1)} %bitcast.43, s32[8,64]{1,0:T(8,128)} %pad.85.refs_3_), custom_call_target="tpu_custom_call" | custom-call | tf_op jit(solution)/shard_map/match/pallas_call | solution.py:651
  100.4 0.8 constant_dynamic-slice_fusion.2
  101.2 0.1 copy.58
  101.3 0.7 copy.55
  102.0 0.7 slice.37
  102.6 0.1 copy.59
  102.8 0.6 reshape.99
  103.4 29.0 %mlp_back_passages.1 = (bf16[1280,128]{1,0:T(8,128)(2,1)}, bf16[1280,768]{1,0:T(8,128)(2,1)}, bf16[1280,3072]{1,0:T(8,128)(2,1)}, f32[1024,768]{1,0:T(8,128)}, b...) custom-call(f32[1024,128]{1,0:T(8,128)} %bitcast.42, f32[1024,128]{1,0:T(8,128)} %get-tuple-element.92.refs_1_, ...), custom_call_target="tpu_custom_call" | custom-call | tf_op jit(solution)/shard_map/mlp_back_passages/pallas_call | solution.py:794
  132.4 11.0 %mlp_back_queries.1 = (bf16[1280,128]{1,0:T(8,128)(2,1)}, bf16[1280,768]{1,0:T(8,128)(2,1)}, bf16[1280,3072]{1,0:T(8,128)(2,1)}, f32[256,768]{1,0:T(8,128)}, bf1...) custom-call(f32[256,128]{1,0:T(8,128)} %get-tuple-element.100.refs_0, ...), custom_call_target="tpu_custom_call", output_to_operand_aliasing={{0}: (12, {}), {1}: (13, {}), {2}: (14, {}), {4}: (15, {})} | custom-call | tf_op jit(solution)/shard_map/mlp_back_queries/pallas_call | solution.py:794
  143.4 130.7 %backward_tail.1 = (bf16[4,304,768]{2,1,0:T(8,128)(2,1)}, f32[1024,768]{1,0:T(8,128)}, f32[256,768]{1,0:T(8,128)}) custom-call(bf16[1280,3072]{1,0:T(8,128)(2,1)} %get-tuple-element.90.refs_0_, bf16[1280,768]{1,0:T(8,128)(2,1)} %get-tuple-element.112.refs_1_, bf16[1280,768]{1,0:T(8,128)(2,1)} %get-tuple-element.113.refs_2_, ...), custom_call_target="tpu_custom_call" | custom-call | tf_op jit(solution)/shard_map/backward_tail/pallas_call | solution.py:1500
  274.1 0.0 copy-start.2
  274.2 3.4 %unpack_gradients.1 = (f32[96,768]{1,0:T(8,128)}, f32[96,768]{1,0:T(8,128)}, f32[96,768]{1,0:T(8,128)}, f32[96,768]{1,0:T(8,128)}, f32[96,3072]{1,0:T(8,128)}, /...) custom-call(bf16[4,304,768]{2,1,0:T(8,128)(2,1)} %get-tuple-element.133.sums_ref), custom_call_target="tpu_custom_call" | custom-call | tf_op jit(solution)/shard_map/unpack_gradients/pallas_call | solution.py:1568
  277.6 0.7 slice.38
  278.3 0.1 constant_dynamic-slice_fusion
  278.4 0.5 slice_bitcast_fusion
  278.9 0.7 slice.44
  279.7 0.7 dynamic_slice.23
  280.3 0.0 copy-done.2
  280.4 0.0 copy-start.1
  280.4 0.9 copy.70
  281.2 3.8 %copy.71 = f32[2,1,512,768]{3,2,1,0:T(8,128)} copy(f32[2,1,512,768]{3,2,1,0:T(8,128)} %bitcast.37) | data formatting | bytes 6291456
  285.0 0.0 copy-done.1
  (3 shorter events, 0.0 us)
Async XLA Ops:
  0.7 0.7 copy-start
  22.3 57.4 %copy-start.3 = (s32[2,128]{1,0:T(2,128)S(1)}, s32[2,128]{1,0:T(2,128)}, u32[]{:S(2)}) copy-start(s32[2,128]{1,0:T(2,128)} %param.23) | copy-start | bytes 3076
  274.1 6.2 %copy-start.2 = (f32[256,768]{1,0:T(8,128)S(1)}, f32[256,768]{1,0:T(8,128)}, u32[]{:S(2)}) copy-start(f32[256,768]{1,0:T(8,128)} %get-tuple-element.131) | copy-start | bytes 2359300
  280.4 4.6 %copy-start.1 = (s32[2,32]{1,0:T(2,128)S(1)}, s32[2,32]{1,0:T(2,128)}, u32[]{:S(2)}) copy-start(s32[2,32]{1,0:T(2,128)} %param.22) | copy-start | bytes 772

commit v5 on v4

--- a/solution.py
+++ b/solution.py
@@ -244,7 +244,7 @@
     ]
 
 
-def fwd_kernel(grouped, alias_count, sizes, *refs):
+def fwd_kernel(grouped, alias_count, sizes, offset, *refs):
     lens_ref, x_ref, vec_ref = refs[:3]
     sources = refs[3:10]
     refs = refs[10 + alias_count :]
@@ -270,8 +270,9 @@
         uinv_ref,
         embed_ref,
     ) = refs[:16]
-    wq, wk, wv, wo, wi, w2, wl, sem, acc_ref = refs[16:]
+    wq, wk, wv, wo, wi, w2, wl, sem, acc_ref, att_buf, act_buf, slope_buf, out_sem = refs[16:]
     loader = Loader(sources, (wq, wk, wv, wo, wi, w2, wl), sem)
+    block_id = pl.program_id(0)
     loader.start()
     if gather:
         last = pl.program_id(0) == pl.num_programs(0) - 1
@@ -296,8 +297,16 @@
     bias = jnp.where(valid, 0.0, MASKED)
     low_half = lax.broadcasted_iota(jnp.int32, (rows, 128), 1) < HEAD_DIM
 
+    def att_copy(pair):
+        slot = lax.rem(pair, 2)
+        return pltpu.make_async_copy(
+            att_buf.at[slot], att_ref.at[block_id, pl.ds(2 * pair, 2)], out_sem.at[slot]
+        )
+
     def pair_body(pair, carry):
         cols = pl.ds(pl.multiple_of(pair * 128, 128), 128)
+        slot = lax.rem(pair, 2)
+        pl.when(pair >= 2)(lambda: att_copy(pair - 2).wait())
         q_pair, k_pair, v_pair = q_ref[:, cols], k_ref[:, cols], v_ref[:, cols]
         parts = []
         for half in range(2):
@@ -307,8 +316,9 @@
             e = jnp.exp(logits - peak)
             inv = 1.0 / jnp.sum(e, axis=-1, keepdims=True)
             low = (e * inv).astype(BF16)
-            att_ref[0, 2 * pair + half] = low
+            att_buf[slot, half] = low
             parts.append(mm(low, v_pair))
+        att_copy(pair).start()
         ctx_ref[:, cols] = jnp.where(low_half, parts[0], parts[1]).astype(BF16)
         return carry
 
@@ -328,19 +338,43 @@
     loader.need(4, 5)
     width = x.shape[1]
 
+    base = block_id * rows if offset is None else offset
+
+    def chunk_copies(chunk):
+        slot = lax.rem(chunk, 2)
+        cols = pl.ds(pl.multiple_of(chunk * width, width), width)
+        return (
+            pltpu.make_async_copy(
+                act_buf.at[slot], act_ref.at[pl.ds(base, rows), cols], out_sem.at[2 + slot]
+            ),
+            pltpu.make_async_copy(
+                slope_buf.at[slot],
+                slope_ref.at[pl.ds(block_id * rows, rows), cols],
+                out_sem.at[4 + slot],
+            ),
+        )
+
     def chunk_body(chunk, carry):
         cols = pl.ds(pl.multiple_of(chunk * width, width), width)
+        slot = lax.rem(chunk, 2)
+
+        @pl.when(chunk >= 2)
+        def _():
+            for copy in chunk_copies(chunk - 2):
+                copy.wait()
+
         inner = mm(first_ref[...], wi[:, cols]) + vec_ref[pl.ds(ROW_BI + chunk, 1), :]
         phi = 0.5 * (1.0 + lax.erf(inner * ROOT_HALF))
         activated = (inner * phi).astype(BF16)
-        act_ref[:, cols] = activated
-        slope_ref[:, cols] = (phi + inner * jnp.exp(-0.5 * inner * inner) * SLOPE_CONST).astype(
-            BF16
-        )
+        act_buf[slot] = activated
+        slope_buf[slot] = (phi + inner * jnp.exp(-0.5 * inner * inner) * SLOPE_CONST).astype(BF16)
+        for copy in chunk_copies(chunk):
+            copy.start()
         acc_ref[...] += mm(activated, w2[cols, :])
         return carry
 
-    lax.fori_loop(0, wi.shape[1] // width, chunk_body, 0)
+    chunks = wi.shape[1] // width
+    lax.fori_loop(0, chunks, chunk_body, 0)
     field = acc_ref[...]
     center = field - mean_row(field)
     inverse = lax.rsqrt(mean_row(center * center) + LAYER_EPS)
@@ -356,6 +390,10 @@
     unit_ref[...] = unit
     uinv_ref[...] = jnp.broadcast_to(uinv, uinv_ref.shape)
     embed_ref[...] = unit.astype(BF16)
+    for back in (2, 1):
+        att_copy(HEADS // 2 - back).wait()
+        for copy in chunk_copies(chunks - back):
+            copy.wait()
     if gather:
         pl.when(last)(gather.finish)
 
@@ -397,8 +435,8 @@
     ]
     shared = (4, 7, 8, 12)
     out_specs = [
-        pl.BlockSpec((1, HEADS, rows, rows), lambda i, lens: (i, 0, 0, 0))
-        if index == 3
+        ANY
+        if index in (3, 8, 9)
         else (row_spec if index in shared else own_spec)(out.shape[1])
         for index, out in enumerate(out_shapes)
     ]
@@ -413,7 +451,7 @@
         sem_shapes = [sem((chips,)), sem((chips,)), sem((1,)), sem((1,)), sem((1,))]
         params = {"collective_id": 4, "has_side_effects": True}
     return pl.pallas_call(
-        functools.partial(fwd_kernel, grouped, len(aliased), sizes),
+        functools.partial(fwd_kernel, grouped, len(aliased), sizes, offset if blocks == 1 else None),
         out_shape=out_shapes,
         grid_spec=pltpu.PrefetchScalarGridSpec(
             num_scalar_prefetch=1,
@@ -425,7 +463,14 @@
             + [ANY] * (7 + len(aliased) + len(sends)),
             out_specs=out_specs,
             scratch_shapes=[pltpu.VMEM(weight.shape, BF16) for weight in weights]
-            + [pltpu.SemaphoreType.DMA((7,)), pltpu.VMEM((rows, width), F32)]
+            + [
+                pltpu.SemaphoreType.DMA((7,)),
+                pltpu.VMEM((rows, width), F32),
+                pltpu.VMEM((2, 2, rows, rows), BF16),
+                pltpu.VMEM((2, rows, width), BF16),
+                pltpu.VMEM((2, rows, width), BF16),
+                pltpu.SemaphoreType.DMA((6,)),
+            ]
             + sem_shapes,
         ),
         input_output_aliases={10 + index: shared[index] for index in range(len(aliased))},
@@ -1541,8 +1586,24 @@
     )(*arrays, *passage_kept, *query_kept, *weights, *sums)
 
 
-def unpack_kernel(part, sums_ref, q_ref, k_ref, v_ref, o_ref, inner_ref, outer_ref, thin_ref, vec_ref):
+def unpack_kernel(part, sums_ref, gx_p, gx_q, *refs):
+    q_ref, k_ref, v_ref, o_ref, inner_ref, outer_ref, thin_ref, vec_ref, to_p, to_q = refs[:10]
+    buf, in_sem, out_sem = refs[10:]
     width = q_ref.shape[1]
+    rows = gx_q.shape[0]
+    pieces = []
+    for source, target in ((gx_p, to_p), (gx_q, to_q)):
+        for start in range(0, source.shape[0], rows):
+            at = pl.ds(start, rows)
+            slot = len(pieces)
+            pieces.append(
+                (
+                    pltpu.make_async_copy(source.at[at], buf.at[slot], in_sem.at[slot]),
+                    pltpu.make_async_copy(buf.at[slot], target.at[at], out_sem.at[slot]),
+                )
+            )
+    for arrive, _ in pieces:
+        arrive.start()
     lanes = thin_ref.shape[1]
     for owner, ref in enumerate((q_ref, k_ref, v_ref, o_ref)):
         ref[...] = sums_ref[owner, 2 * part : 3 * part].astype(F32)
@@ -1550,29 +1611,42 @@
             owner, part : 2 * part
         ].astype(F32)
         outer_ref[owner * part : (owner + 1) * part] = sums_ref[owner, :part].astype(F32)
+        pieces[owner][0].wait()
+        pieces[owner][1].start()
+    for arrive, leave in pieces[4:]:
+        arrive.wait()
+        leave.start()
     tail = sums_ref[0, 3 * part :].astype(F32)
     for block in range(width // lanes):
         thin_ref[block * 16 : (block + 1) * 16] = tail[:, block * lanes : (block + 1) * lanes]
     vec_ref[...] = sums_ref[1, 3 * part :].astype(F32)
-
-
-def unpack(summed, part, embed_width):
+    for _, leave in pieces:
+        leave.wait()
+
+
+def unpack(summed, grad_p, grad_q, part, embed_width):
     width = summed.shape[-1]
+    rows = grad_q.shape[0]
+    count = grad_p.shape[0] // rows + 1
+    sem = pltpu.SemaphoreType.DMA
     vmem = pl.BlockSpec(memory_space=pltpu.VMEM)
     shapes = [(part, width)] * 4 + [
         (part, 4 * width),
         (4 * part, width),
         (part, embed_width),
         (16, width),
+        grad_p.shape,
+        grad_q.shape,
     ]
     return pl.pallas_call(
         functools.partial(unpack_kernel, part),
         out_shape=[jax.ShapeDtypeStruct(shape, F32) for shape in shapes],
-        in_specs=[vmem],
-        out_specs=[vmem] * len(shapes),
+        in_specs=[vmem, ANY, ANY],
+        out_specs=[vmem] * (len(shapes) - 2) + [ANY] * 2,
+        scratch_shapes=[pltpu.VMEM((count, rows, width), F32), sem((count,)), sem((count,))],
         compiler_params=pltpu.CompilerParams(vmem_limit_bytes=VMEM_LIMIT),
         name="unpack_gradients",
-    )(summed)
+    )(summed, grad_p, grad_q)
 
 
 def outer(left, right):
@@ -1720,8 +1794,8 @@
             (back_p[5], sums_q),
             n_wide,
         )
-        r_q, r_k, r_v, r_out, r_inner, r_outer, r_linear, vectors = unpack(
-            summed, part, embed_width
+        r_q, r_k, r_v, r_out, r_inner, r_outer, r_linear, vectors, grad_p, grad_q = unpack(
+            summed, grad_p, grad_q, part, embed_width
         )
         own = lax.dynamic_slice_in_dim(vectors[:8], wide_index * part, part, axis=1)
         v_q, v_v, v_o, v_g1, v_s1, v_2, v_g2, v_s2 = (

time: 286 us -> 280 us (0.979)
  local copies, waits for them, and re-layouts: 13.2 us -> 8.55 us
    pallas_call x2, Pallas kernels: 76.2 us -> 71.5 us  [encode(): pl.pallas_call(functools.partial(fwd_kernel, grouped, len(aliased), sizes...]
    unnamed x11 -> x7, local copies, waits for them, and re-layouts: 5.99 us -> 1.35 us
    pallas_call x1, Pallas kernels: 3.43 us -> 6.45 us  [unpack(): pl.pallas_call(functools.partial(unpack_kernel, part), out_shape=[jax.Sha...]
where the time goes in v5:
time: 280 us; the launch traced here: 279 us
  Pallas kernels  269 us (96%)
  local copies, waits for them, and re-layouts  8.55 us (3%)
    pallas_call x1, Pallas kernels, backward_tail(): pl.pallas_call(functools.partial(tail_kernel, n_z, part), out_shape=(jax....  131 us
    pallas_call x2, Pallas kernels, encode(): pl.pallas_call(functools.partial(fwd_kernel, grouped, len(aliased), sizes...  71.5 us
    pallas_call x2, Pallas kernels, mlp_back(): pl.pallas_call(functools.partial(mlp_back_kernel, len(aliased), sizes), o...  40 us
    pallas_call x1, Pallas kernels, match(): pl.pallas_call(functools.partial(match_kernel, n_wide, n_narrow, group, q...  19.9 us
    pallas_call x1, Pallas kernels, unpack(): pl.pallas_call(functools.partial(unpack_kernel, part), out_shape=[jax.Sha...  6.45 us

profile of v5, /device:TPU:0, one launch (start us, length us, event | category | flops | bytes accessed | tf_op | source)
XLA Modules:
  0.0 278.7 jit_solution(1105521753308593593)
XLA Ops:
  0.7 0.0 copy-start
  0.7 0.7 copy-done
  1.3 0.7 fusion.refs_0_
  2.0 0.8 convert_add_fusion
  2.9 0.6 reshape.90.refs_2_.refs_8_
  3.5 17.8 %encode_queries.1 = (bf16[256,768]{1,0:T(8,128)(2,1)}, bf16[256,768]{1,0:T(8,128)(2,1)}, bf16[256,768]{1,0:T(8,128)(2,1)}, bf16[1,12,256,256]{3,2,1,0:T(8,128)(2...) custom-call(s32[2]{0:T(128)} %fusion.refs_0_, ...), custom_call_target="tpu_custom_call" | custom-call | tf_op jit(solution)/shard_map/encode_queries/pallas_call | solution.py:453
  21.3 0.0 copy-start.2
  21.3 53.7 %encode_passages.1 = (bf16[1024,768]{1,0:T(8,128)(2,1)}, bf16[1024,768]{1,0:T(8,128)(2,1)}, bf16[1024,768]{1,0:T(8,128)(2,1)}, bf16[2,12,512,512]{3,2,1,0:T(8,12...) custom-call(s32[2]{0:T(128)} %fusion.refs_0_, ...), custom_call_target="tpu_custom_call", output_to_operand_aliasing={{4}: (10, {}), {7}: (11, {}), {8}: (12, {}), {12}: (13, {})} | custom-call | tf_op jit(solution)/shard_map/encode_passages/pallas_call | solution.py:453
  75.0 0.0 copy-done.2
  75.0 0.1 reshape.94
  75.1 0.1 copy.57
  75.2 0.6 pad.85.refs_3_
  75.8 19.9 %match.1 = (f32[32,8,64]{2,1,0:T(8,128)}, f32[8,64]{1,0:T(8,128)}, f32[2,512,128]{2,1,0:T(8,128)}, bf16[16,256,128]{2,1,0:T(8,128)(2,1)}) custom-call(s32[2]{0:T(128)} %fusion.refs_0_, bf16[32,2,128,128]{3,2,1,0:T(8,128)(2,1)} %bitcast.37, bf16[2,512,128]{2,1,0:T(8,128)(2,1)} %bitcast.41, s32[8,64]{1,0:T(8,128)} %pad.85.refs_3_), custom_call_target="tpu_custom_call" | custom-call | tf_op jit(solution)/shard_map/match/pallas_call | solution.py:696
  95.7 0.8 constant_dynamic-slice_fusion.2
  96.5 0.1 copy.58
  96.6 0.7 copy.55
  97.3 0.7 slice.37
  97.9 0.1 copy.59
  98.0 0.6 reshape.99
  98.7 29.0 %mlp_back_passages.1 = (bf16[1280,128]{1,0:T(8,128)(2,1)}, bf16[1280,768]{1,0:T(8,128)(2,1)}, bf16[1280,3072]{1,0:T(8,128)(2,1)}, f32[1024,768]{1,0:T(8,128)}, b...) custom-call(f32[1024,128]{1,0:T(8,128)} %bitcast.40, f32[1024,128]{1,0:T(8,128)} %get-tuple-element.94.refs_1_, ...), custom_call_target="tpu_custom_call" | custom-call | tf_op jit(solution)/shard_map/mlp_back_passages/pallas_call | solution.py:839
  127.7 11.0 %mlp_back_queries.1 = (bf16[1280,128]{1,0:T(8,128)(2,1)}, bf16[1280,768]{1,0:T(8,128)(2,1)}, bf16[1280,3072]{1,0:T(8,128)(2,1)}, f32[256,768]{1,0:T(8,128)}, bf1...) custom-call(f32[256,128]{1,0:T(8,128)} %get-tuple-element.102.refs_0, ...), custom_call_target="tpu_custom_call", output_to_operand_aliasing={{0}: (12, {}), {1}: (13, {}), {2}: (14, {}), {4}: (15, {})} | custom-call | tf_op jit(solution)/shard_map/mlp_back_queries/pallas_call | solution.py:839
  138.7 130.7 %backward_tail.1 = (bf16[4,304,768]{2,1,0:T(8,128)(2,1)}, f32[1024,768]{1,0:T(8,128)}, f32[256,768]{1,0:T(8,128)}) custom-call(bf16[1280,3072]{1,0:T(8,128)(2,1)} %get-tuple-element.92.refs_0_, bf16[1280,768]{1,0:T(8,128)(2,1)} %get-tuple-element.114.refs_1_, bf16[1280,768]{1,0:T(8,128)(2,1)} %get-tuple-element.115.refs_2_, ...), custom_call_target="tpu_custom_call" | custom-call | tf_op jit(solution)/shard_map/backward_tail/pallas_call | solution.py:1545
  269.5 0.0 copy-start.1
  269.5 6.5 %unpack_gradients.1 = (f32[96,768]{1,0:T(8,128)}, f32[96,768]{1,0:T(8,128)}, f32[96,768]{1,0:T(8,128)}, f32[96,768]{1,0:T(8,128)}, f32[96,3072]{1,0:T(8,128)}, /...) custom-call(bf16[4,304,768]{2,1,0:T(8,128)(2,1)} %get-tuple-element., ...), custom_call_target="tpu_custom_call" | custom-call | tf_op jit(solution)/shard_map/unpack_gradients/pallas_call | solution.py:1641
  275.9 0.7 slice.38
  276.7 0.1 constant_dynamic-slice_fusion
  276.8 0.5 slice_bitcast_fusion
  277.3 0.7 slice.44
  278.1 0.7 dynamic_slice.23
  278.7 0.0 copy-done.1
  (3 shorter events, 0.0 us)
Async XLA Ops:
  0.7 0.7 copy-start
  21.3 53.7 %copy-start.2 = (s32[2,128]{1,0:T(2,128)S(1)}, s32[2,128]{1,0:T(2,128)}, u32[]{:S(2)}) copy-start(s32[2,128]{1,0:T(2,128)} %param.23) | copy-start | bytes 3076
  269.5 9.2 %copy-start.1 = (s32[2,32]{1,0:T(2,128)S(1)}, s32[2,32]{1,0:T(2,128)}, u32[]{:S(2)}) copy-start(s32[2,32]{1,0:T(2,128)} %param.22) | copy-start | bytes 772

commit v6 on v5

--- a/solution.py
+++ b/solution.py
@@ -9,6 +9,7 @@
 
 HEADS = 12
 HEAD_DIM = 64
+LOG2E = 1.4426950408889634
 SHARP = 16.0
 LAYER_EPS = 1e-12
 NORM_EPS = 1e-06
@@ -600,8 +601,9 @@
     def forward(block, carry):
         for m in range(micro):
             sims = mm(p_ref[m], query_rows(block, m), NT)
-            slot = lax.broadcasted_iota(jnp.int32, sims.shape, 0)
-            e = jnp.where(slot < lens_ref[m], jnp.exp(SHARP * sims - SHARP), 0.0)
+            slot = lax.broadcasted_iota(jnp.int32, (sims.shape[0], 1), 0)
+            shift = jnp.where(slot < lens_ref[m], SHARP * LOG2E, -MASKED)
+            e = jnp.exp2(SHARP * LOG2E * sims - shift)
             e_buf[m, block] = e.astype(BF16)
             z = jnp.sum(e, axis=0, keepdims=True)
             for index in range(group):
@@ -658,7 +660,7 @@
             weight = jnp.concatenate(
                 [z_buf[m, pl.ds(block * group + index, 1)] for index in range(group)], axis=1
             )
-            grads = (e_buf[m, block].astype(F32) * weight).astype(BF16)
+            grads = e_buf[m, block] * weight.astype(BF16)
             gp_ref[m] += mm(grads, query_rows(block, m))
             part = mm(grads, p_ref[m], TN).astype(BF16)
             for index in range(group):
@@ -725,7 +727,7 @@
     ref[row : row + 1, :] += jnp.sum(value, axis=0, keepdims=True)
 
 
-def mlp_back_kernel(alias_count, sizes, *refs):
+def mlp_back_kernel(alias_count, sizes, offset, *refs):
     (
         ge_ref,
         unit_ref,
@@ -744,9 +746,28 @@
         swap = Push(Chips(*sizes), refs[0], refs[7], refs[-4:])
         refs = refs[1:7] + refs[8:-4]
     gp_ref, go_ref, gi_ref, gh_ref, ga_ref, sums_ref = refs[:6]
-    wl, w2, wi, sem, acc_ref = refs[6:]
+    wl, w2, wi, sem, acc_ref, slope_buf, inner_buf, chunk_sem = refs[6:]
     loader = Loader(sources, (wl, w2, wi), sem)
     loader.start()
+    rows, width = go_ref.shape
+    own = pl.ds(pl.program_id(0) * rows, rows)
+    placed = pl.ds(offset + pl.program_id(0) * rows, rows)
+
+    def slope_copy(chunk):
+        slot = lax.rem(chunk, 2)
+        cols = pl.ds(pl.multiple_of(chunk * width, width), width)
+        return pltpu.make_async_copy(
+            slope_ref.at[own, cols], slope_buf.at[slot], chunk_sem.at[slot]
+        )
+
+    def inner_copy(chunk):
+        slot = lax.rem(chunk, 2)
+        cols = pl.ds(pl.multiple_of(chunk * width, width), width)
+        return pltpu.make_async_copy(
+            inner_buf.at[slot], gi_ref.at[placed, cols], chunk_sem.at[2 + slot]
+        )
+
+    slope_copy(0).start()
     if swap:
         pl.when(loader.first)(swap.start)
 
@@ -772,20 +793,25 @@
     accumulate(sums_ref, ROW_B2, outer_low.astype(F32))
     acc_ref[...] = grad_second
     loader.need(1, 2)
-    width = go_ref.shape[1]
+    chunks = wi.shape[1] // width
 
     def chunk_body(chunk, carry):
         cols = pl.ds(pl.multiple_of(chunk * width, width), width)
+        slot = lax.rem(chunk, 2)
+        slope_copy(chunk).wait()
+        pl.when(chunk < chunks - 1)(lambda: slope_copy(chunk + 1).start())
+        pl.when(chunk >= 2)(lambda: inner_copy(chunk - 2).wait())
         grad_act = mm(go_ref[...], w2[cols, :], NT)
-        inner = (grad_act * slope_ref[:, cols].astype(F32)).astype(BF16)
-        gi_ref[:, cols] = inner
+        inner = (grad_act * slope_buf[slot].astype(F32)).astype(BF16)
+        inner_buf[slot] = inner
+        inner_copy(chunk).start()
         sums_ref[pl.ds(ROW_BI + chunk, 1), :] += jnp.sum(
             inner.astype(F32), axis=0, keepdims=True
         )
         acc_ref[...] += mm(inner, wi[:, cols], NT)
         return carry
 
-    lax.fori_loop(0, wi.shape[1] // width, chunk_body, 0)
+    lax.fori_loop(0, chunks, chunk_body, 0)
     grad_first = acc_ref[...]
     normed = n1_ref[...].astype(F32)
     accumulate(sums_ref, ROW_G1, grad_first * normed)
@@ -796,6 +822,8 @@
     low = hidden.astype(BF16)
     ga_ref[...] = low
     accumulate(sums_ref, ROW_BO, low.astype(F32))
+    for back in (2, 1):
+        inner_copy(chunks - back).wait()
     if swap:
         pl.when(pl.program_id(0) == pl.num_programs(0) - 1)(swap.finish)
 
@@ -825,7 +853,7 @@
     ]
     shared = (0, 1, 2, 4)
     out_specs = [
-        (row_spec if index in shared else own_spec)(out.shape[1])
+        ANY if index == 2 else (row_spec if index in shared else own_spec)(out.shape[1])
         for index, out in enumerate(out_shapes[:5])
     ] + [pl.BlockSpec((16, width), lambda i: (0, 0))]
     aliased = [] if earlier is None else [earlier[index] for index in shared]
@@ -837,15 +865,23 @@
         scratch = push_scratch(*sent.shape)
         params = {"collective_id": 5, "has_side_effects": True}
     return pl.pallas_call(
-        functools.partial(mlp_back_kernel, len(aliased), sizes),
+        functools.partial(mlp_back_kernel, len(aliased), sizes, offset),
         out_shape=out_shapes,
         grid=(blocks,),
-        in_specs=[own_spec(arg.shape[1]) for arg in args]
+        in_specs=[
+            ANY if index == 5 else own_spec(arg.shape[1]) for index, arg in enumerate(args)
+        ]
         + [pl.BlockSpec(vec.shape, lambda i: (0, 0))]
         + [ANY] * (3 + len(aliased) + len(sends)),
         out_specs=out_specs,
         scratch_shapes=[pltpu.VMEM(weight.shape, BF16) for weight in (wl, w2, wi)]
-        + [pltpu.SemaphoreType.DMA((3,)), pltpu.VMEM((rows, width), F32)]
+        + [
+            pltpu.SemaphoreType.DMA((3,)),
+            pltpu.VMEM((rows, width), F32),
+            pltpu.VMEM((2, rows, width), BF16),
+            pltpu.VMEM((2, rows, width), BF16),
+            pltpu.SemaphoreType.DMA((4,)),
+        ]
         + scratch,
         input_output_aliases={12 + index: shared[index] for index in range(len(aliased))},
         compiler_params=pltpu.CompilerParams(vmem_limit_bytes=VMEM_LIMIT, **params),

time: 280 us -> 276 us (0.986)
  Pallas kernels: 269 us -> 264 us
    pallas_call x2, Pallas kernels: 40 us -> 36.5 us  [mlp_back(): pl.pallas_call(functools.partial(mlp_back_kernel, len(aliased), sizes, of...]
where the time goes in v6:
time: 276 us; the launch traced here: 275 us
  Pallas kernels  264 us (96%)
  local copies, waits for them, and re-layouts  8.55 us (3%)
    pallas_call x1, Pallas kernels, backward_tail(): pl.pallas_call(functools.partial(tail_kernel, n_z, part), out_shape=(jax....  131 us
    pallas_call x2, Pallas kernels, encode(): pl.pallas_call(functools.partial(fwd_kernel, grouped, len(aliased), sizes...  71.5 us
    pallas_call x2, Pallas kernels, mlp_back(): pl.pallas_call(functools.partial(mlp_back_kernel, len(aliased), sizes, of...  36.5 us
    pallas_call x1, Pallas kernels, match(): pl.pallas_call(functools.partial(match_kernel, n_wide, n_narrow, group, q...  19.2 us
    pallas_call x1, Pallas kernels, unpack(): pl.pallas_call(functools.partial(unpack_kernel, part), out_shape=[jax.Sha...  6.45 us

profile of v6, /device:TPU:0, one launch (start us, length us, event | category | flops | bytes accessed | tf_op | source)
XLA Modules:
  0.0 274.6 jit_solution(3460891558592670210)
XLA Ops:
  0.7 0.0 copy-start
  0.7 0.7 copy-done
  1.3 0.7 fusion.refs_0_
  2.0 0.8 convert_add_fusion
  2.9 0.6 reshape.90.refs_2_.refs_8_
  3.5 17.8 %encode_queries.1 = (bf16[256,768]{1,0:T(8,128)(2,1)}, bf16[256,768]{1,0:T(8,128)(2,1)}, bf16[256,768]{1,0:T(8,128)(2,1)}, bf16[1,12,256,256]{3,2,1,0:T(8,128)(2...) custom-call(s32[2]{0:T(128)} %fusion.refs_0_, ...), custom_call_target="tpu_custom_call" | custom-call | tf_op jit(solution)/shard_map/encode_queries/pallas_call | solution.py:454
  21.3 0.0 copy-start.2
  21.3 53.7 %encode_passages.1 = (bf16[1024,768]{1,0:T(8,128)(2,1)}, bf16[1024,768]{1,0:T(8,128)(2,1)}, bf16[1024,768]{1,0:T(8,128)(2,1)}, bf16[2,12,512,512]{3,2,1,0:T(8,12...) custom-call(s32[2]{0:T(128)} %fusion.refs_0_, ...), custom_call_target="tpu_custom_call", output_to_operand_aliasing={{4}: (10, {}), {7}: (11, {}), {8}: (12, {}), {12}: (13, {})} | custom-call | tf_op jit(solution)/shard_map/encode_passages/pallas_call | solution.py:454
  75.0 0.0 copy-done.2
  75.0 0.1 reshape.94
  75.1 0.1 copy.57
  75.2 0.6 pad.85.refs_3_
  75.8 19.2 %match.1 = (f32[32,8,64]{2,1,0:T(8,128)}, f32[8,64]{1,0:T(8,128)}, f32[2,512,128]{2,1,0:T(8,128)}, bf16[16,256,128]{2,1,0:T(8,128)(2,1)}) custom-call(s32[2]{0:T(128)} %fusion.refs_0_, bf16[32,2,128,128]{3,2,1,0:T(8,128)(2,1)} %bitcast.37, bf16[2,512,128]{2,1,0:T(8,128)(2,1)} %bitcast.41, s32[8,64]{1,0:T(8,128)} %pad.85.refs_3_), custom_call_target="tpu_custom_call" | custom-call | tf_op jit(solution)/shard_map/match/pallas_call | solution.py:698
  95.0 0.8 constant_dynamic-slice_fusion.2
  95.8 0.1 copy.58
  95.9 0.7 copy.55
  96.6 0.7 slice.37
  97.3 0.1 copy.59
  97.4 0.6 reshape.99
  98.0 25.7 %mlp_back_passages.1 = (bf16[1280,128]{1,0:T(8,128)(2,1)}, bf16[1280,768]{1,0:T(8,128)(2,1)}, bf16[1280,3072]{1,0:T(8,128)(2,1)}, f32[1024,768]{1,0:T(8,128)}, b...) custom-call(f32[1024,128]{1,0:T(8,128)} %bitcast.40, f32[1024,128]{1,0:T(8,128)} %get-tuple-element.94.refs_1_, ...), custom_call_target="tpu_custom_call" | custom-call | tf_op jit(solution)/shard_map/mlp_back_passages/pallas_call | solution.py:867
  123.7 10.9 %mlp_back_queries.1 = (bf16[1280,128]{1,0:T(8,128)(2,1)}, bf16[1280,768]{1,0:T(8,128)(2,1)}, bf16[1280,3072]{1,0:T(8,128)(2,1)}, f32[256,768]{1,0:T(8,128)}, bf1...) custom-call(f32[256,128]{1,0:T(8,128)} %get-tuple-element.102.refs_0, ...), custom_call_target="tpu_custom_call", output_to_operand_aliasing={{0}: (12, {}), {1}: (13, {}), {2}: (14, {}), {4}: (15, {})} | custom-call | tf_op jit(solution)/shard_map/mlp_back_queries/pallas_call | solution.py:867
  134.6 130.7 %backward_tail.1 = (bf16[4,304,768]{2,1,0:T(8,128)(2,1)}, f32[1024,768]{1,0:T(8,128)}, f32[256,768]{1,0:T(8,128)}) custom-call(bf16[1280,3072]{1,0:T(8,128)(2,1)} %get-tuple-element.92.refs_0_, bf16[1280,768]{1,0:T(8,128)(2,1)} %get-tuple-element.114.refs_1_, bf16[1280,768]{1,0:T(8,128)(2,1)} %get-tuple-element.115.refs_2_, ...), custom_call_target="tpu_custom_call" | custom-call | tf_op jit(solution)/shard_map/backward_tail/pallas_call | solution.py:1581
  265.3 0.0 copy-start.1
  265.3 6.5 %unpack_gradients.1 = (f32[96,768]{1,0:T(8,128)}, f32[96,768]{1,0:T(8,128)}, f32[96,768]{1,0:T(8,128)}, f32[96,768]{1,0:T(8,128)}, f32[96,3072]{1,0:T(8,128)}, /...) custom-call(bf16[4,304,768]{2,1,0:T(8,128)(2,1)} %get-tuple-element., ...), custom_call_target="tpu_custom_call" | custom-call | tf_op jit(solution)/shard_map/unpack_gradients/pallas_call | solution.py:1677
  271.8 0.7 slice.38
  272.5 0.1 constant_dynamic-slice_fusion
  272.6 0.5 slice_bitcast_fusion
  273.2 0.7 slice.44
  273.9 0.7 dynamic_slice.23
  274.6 0.0 copy-done.1
  (3 shorter events, 0.0 us)
Async XLA Ops:
  0.7 0.7 copy-start
  21.3 53.7 %copy-start.2 = (s32[2,128]{1,0:T(2,128)S(1)}, s32[2,128]{1,0:T(2,128)}, u32[]{:S(2)}) copy-start(s32[2,128]{1,0:T(2,128)} %param.23) | copy-start | bytes 3076
  265.3 9.2 %copy-start.1 = (s32[2,32]{1,0:T(2,128)S(1)}, s32[2,32]{1,0:T(2,128)}, u32[]{:S(2)}) copy-start(s32[2,32]{1,0:T(2,128)} %param.22) | copy-start | bytes 772

commit v7 on v6

--- a/solution.py
+++ b/solution.py
@@ -1376,6 +1376,7 @@
             (v.at[own], buf.at[1, low]),
             (ga.at[pl.ds(base, rows)], buf.at[1, high]),
             (gh.at[own], hidden_of(block)),
+            (ctx.at[pl.ds(base, rows)], grads.at[0, pl.ds(base, rows)]),
         )
         return [
             pltpu.make_async_copy(*pair, block_sem.at[block % 2, index])
@@ -1434,16 +1435,15 @@
             pl.when(pair < HEADS // 2 - 1)(lambda: att_copy(pair + 1).start())
             q_pair, k_pair, v_pair = q_ref[:, cols], k_ref[:, cols], v_ref[:, cols]
             gc_pair = grads[2, own, cols]
+            shares = gc_pair.astype(F32) * grads[0, own, cols].astype(F32)
             parts = []
             for half in range(2):
                 mask = low_half if half == 0 else jnp.logical_not(low_half)
                 low_att = att_buf[slot, half, size, size]
                 wide_att = low_att.astype(F32)
                 grad_att = mm(jnp.where(mask, gc_pair, jnp.zeros_like(gc_pair)), v_pair, NT)
-                weighted = grad_att * wide_att
-                grad_logits = (
-                    weighted - wide_att * jnp.sum(weighted, axis=-1, keepdims=True)
-                ).astype(BF16)
+                overlap = jnp.sum(jnp.where(mask, shares, 0.0), axis=-1, keepdims=True)
+                grad_logits = (wide_att * (grad_att - overlap)).astype(BF16)
                 parts.append(
                     (
                         mm(grad_logits, k_pair) * scale,
@@ -1608,7 +1608,7 @@
             pltpu.VMEM((8, width), F32),
             sem((2, 2)),
             sem((4,)),
-            sem((2, 5)),
+            sem((2, 6)),
             sem((2,)),
             sem((3,)),
         ]

time: 276 us -> 275 us (level)
  no operation moved by 1% of the time
where the time goes in v7:
time: 275 us; the launch traced here: 274 us
  Pallas kernels  264 us (96%)
  local copies, waits for them, and re-layouts  8.55 us (3%)
    pallas_call x1, Pallas kernels, backward_tail(): pl.pallas_call(functools.partial(tail_kernel, n_z, part), out_shape=(jax....  131 us
    pallas_call x2, Pallas kernels, encode(): pl.pallas_call(functools.partial(fwd_kernel, grouped, len(aliased), sizes...  71.5 us
    pallas_call x2, Pallas kernels, mlp_back(): pl.pallas_call(functools.partial(mlp_back_kernel, len(aliased), sizes, of...  36.5 us
    pallas_call x1, Pallas kernels, match(): pl.pallas_call(functools.partial(match_kernel, n_wide, n_narrow, group, q...  19.2 us
    pallas_call x1, Pallas kernels, unpack(): pl.pallas_call(functools.partial(unpack_kernel, part), out_shape=[jax.Sha...  6.45 us

profile of v7, /device:TPU:0, one launch (start us, length us, event | category | flops | bytes accessed | tf_op | source)
XLA Modules:
  0.0 274.4 jit_solution(4978882649109301112)
XLA Ops:
  0.7 0.0 copy-start
  0.7 0.7 copy-done
  1.3 0.7 fusion.refs_0_
  2.0 0.8 convert_add_fusion
  2.9 0.6 reshape.90.refs_2_.refs_8_
  3.5 17.8 %encode_queries.1 = (bf16[256,768]{1,0:T(8,128)(2,1)}, bf16[256,768]{1,0:T(8,128)(2,1)}, bf16[256,768]{1,0:T(8,128)(2,1)}, bf16[1,12,256,256]{3,2,1,0:T(8,128)(2...) custom-call(s32[2]{0:T(128)} %fusion.refs_0_, ...), custom_call_target="tpu_custom_call" | custom-call | tf_op jit(solution)/shard_map/encode_queries/pallas_call | solution.py:454
  21.3 0.0 copy-start.2
  21.3 53.7 %encode_passages.1 = (bf16[1024,768]{1,0:T(8,128)(2,1)}, bf16[1024,768]{1,0:T(8,128)(2,1)}, bf16[1024,768]{1,0:T(8,128)(2,1)}, bf16[2,12,512,512]{3,2,1,0:T(8,12...) custom-call(s32[2]{0:T(128)} %fusion.refs_0_, ...), custom_call_target="tpu_custom_call", output_to_operand_aliasing={{4}: (10, {}), {7}: (11, {}), {8}: (12, {}), {12}: (13, {})} | custom-call | tf_op jit(solution)/shard_map/encode_passages/pallas_call | solution.py:454
  75.0 0.0 copy-done.2
  75.0 0.1 reshape.94
  75.1 0.1 copy.57
  75.2 0.6 pad.85.refs_3_
  75.8 19.2 %match.1 = (f32[32,8,64]{2,1,0:T(8,128)}, f32[8,64]{1,0:T(8,128)}, f32[2,512,128]{2,1,0:T(8,128)}, bf16[16,256,128]{2,1,0:T(8,128)(2,1)}) custom-call(s32[2]{0:T(128)} %fusion.refs_0_, bf16[32,2,128,128]{3,2,1,0:T(8,128)(2,1)} %bitcast.37, bf16[2,512,128]{2,1,0:T(8,128)(2,1)} %bitcast.41, s32[8,64]{1,0:T(8,128)} %pad.85.refs_3_), custom_call_target="tpu_custom_call" | custom-call | tf_op jit(solution)/shard_map/match/pallas_call | solution.py:698
  95.0 0.8 constant_dynamic-slice_fusion.2
  95.8 0.1 copy.58
  95.9 0.7 copy.55
  96.6 0.7 slice.37
  97.3 0.1 copy.59
  97.4 0.6 reshape.99
  98.0 25.7 %mlp_back_passages.1 = (bf16[1280,128]{1,0:T(8,128)(2,1)}, bf16[1280,768]{1,0:T(8,128)(2,1)}, bf16[1280,3072]{1,0:T(8,128)(2,1)}, f32[1024,768]{1,0:T(8,128)}, b...) custom-call(f32[1024,128]{1,0:T(8,128)} %bitcast.40, f32[1024,128]{1,0:T(8,128)} %get-tuple-element.94.refs_1_, ...), custom_call_target="tpu_custom_call" | custom-call | tf_op jit(solution)/shard_map/mlp_back_passages/pallas_call | solution.py:867
  123.7 10.9 %mlp_back_queries.1 = (bf16[1280,128]{1,0:T(8,128)(2,1)}, bf16[1280,768]{1,0:T(8,128)(2,1)}, bf16[1280,3072]{1,0:T(8,128)(2,1)}, f32[256,768]{1,0:T(8,128)}, bf1...) custom-call(f32[256,128]{1,0:T(8,128)} %get-tuple-element.102.refs_0, ...), custom_call_target="tpu_custom_call", output_to_operand_aliasing={{0}: (12, {}), {1}: (13, {}), {2}: (14, {}), {4}: (15, {})} | custom-call | tf_op jit(solution)/shard_map/mlp_back_queries/pallas_call | solution.py:867
  134.6 130.6 %backward_tail.1 = (bf16[4,304,768]{2,1,0:T(8,128)(2,1)}, f32[1024,768]{1,0:T(8,128)}, f32[256,768]{1,0:T(8,128)}) custom-call(bf16[1280,3072]{1,0:T(8,128)(2,1)} %get-tuple-element.92.refs_0_, bf16[1280,768]{1,0:T(8,128)(2,1)} %get-tuple-element.114.refs_1_, bf16[1280,768]{1,0:T(8,128)(2,1)} %get-tuple-element.115.refs_2_, ...), custom_call_target="tpu_custom_call" | custom-call | tf_op jit(solution)/shard_map/backward_tail/pallas_call | solution.py:1581
  265.2 0.0 copy-start.1
  265.2 6.5 %unpack_gradients.1 = (f32[96,768]{1,0:T(8,128)}, f32[96,768]{1,0:T(8,128)}, f32[96,768]{1,0:T(8,128)}, f32[96,768]{1,0:T(8,128)}, f32[96,3072]{1,0:T(8,128)}, /...) custom-call(bf16[4,304,768]{2,1,0:T(8,128)(2,1)} %get-tuple-element., ...), custom_call_target="tpu_custom_call" | custom-call | tf_op jit(solution)/shard_map/unpack_gradients/pallas_call | solution.py:1677
  271.6 0.7 slice.38
  272.4 0.1 constant_dynamic-slice_fusion
  272.5 0.5 slice_bitcast_fusion
  273.0 0.7 slice.44
  273.8 0.7 dynamic_slice.23
  274.4 0.0 copy-done.1
  (3 shorter events, 0.0 us)
Async XLA Ops:
  0.7 0.7 copy-start
  21.3 53.7 %copy-start.2 = (s32[2,128]{1,0:T(2,128)S(1)}, s32[2,128]{1,0:T(2,128)}, u32[]{:S(2)}) copy-start(s32[2,128]{1,0:T(2,128)} %param.23) | copy-start | bytes 3076
  265.2 9.2 %copy-start.1 = (s32[2,32]{1,0:T(2,128)S(1)}, s32[2,32]{1,0:T(2,128)}, u32[]{:S(2)}) copy-start(s32[2,32]{1,0:T(2,128)} %param.22) | copy-start | bytes 772
